TPU v7x, 32 devices: a whole 2x2x4 slice. The times are simulated.
32 devices in a mesh: dp: 8 (over z, x), tensor: 4 (over y, core).
Axes of the slice: x: 2, y: 2, z: 4, core: 2. Of those that a mesh axis runs over, the one named last changes fastest.
Arguments:
- layer_input: bfloat16 [24576, 768], P(('dp', 'tensor')), may hold values from -6 to 6
- segment_ids: int32 [24, 1024], P('dp'), may hold values from 0 to 3, never falling along the last dimension, each value on 1 to 800 neighbouring positions
- w_query: bfloat16 [768, 768], P(None, 'tensor'), may hold values from -0.21875 to 0.21875
- b_query: bfloat16 [768], P('tensor'), may hold values from -1.5 to 1.5
- w_key: bfloat16 [768, 768], P(None, 'tensor'), may hold values from -0.21875 to 0.21875
- w_value: bfloat16 [768, 768], P(None, 'tensor'), may hold values from -0.21875 to 0.21875
- b_value: bfloat16 [768], P('tensor'), may hold values from -1.5 to 1.5
- w_out: bfloat16 [768, 768], P('tensor'), may hold values from -1.75 to 1.75
- b_out: float32 [768], replicated, may hold values from -1.5 to 1.5
- first_gain: float32 [768], replicated, may hold values from 0.5 to 1.5
- first_shift: float32 [768], replicated, may hold values from -1.5 to 1.5
- w_in: bfloat16 [768, 3072], P(None, 'tensor'), may hold values from -0.21875 to 0.21875
- b_in: bfloat16 [3072], P('tensor'), may hold values from -1.5 to 1.5
- w_back: bfloat16 [3072, 768], P('tensor'), may hold values from -0.21875 to 0.21875
- b_back: float32 [768], replicated, may hold values from -1.5 to 1.5
- second_gain: float32 [768], replicated, may hold values from 0.5 to 1.5
- second_shift: float32 [768], replicated, may hold values from -1.5 to 1.5
- cotangent: bfloat16 [24576, 768], P(('dp', 'tensor')), may hold values from -6 to 6
Outputs:
- layer_output: bfloat16 [24576, 768], P(('dp', 'tensor'))
- input_grad: bfloat16 [24576, 768], P(('dp', 'tensor'))
- grad_w_query: float32 [768, 768], P(None, 'tensor')
- grad_b_query: float32 [768], P('tensor')
- grad_w_key: float32 [768, 768], P(None, 'tensor')
- grad_w_value: float32 [768, 768], P(None, 'tensor')
- grad_b_value: float32 [768], P('tensor')
- grad_w_out: float32 [768, 768], P('tensor')
- grad_b_out: float32 [768], replicated
- grad_first_gain: float32 [768], replicated
- grad_first_shift: float32 [768], replicated
- grad_w_in: float32 [768, 3072], P(None, 'tensor')
- grad_b_in: float32 [3072], P('tensor')
- grad_w_back: float32 [3072, 768], P('tensor')
- grad_b_back: float32 [768], replicated
- grad_second_gain: float32 [768], replicated
- grad_second_shift: float32 [768], replicated
Inputs may be any that keep to these rules, and one draw needn't show every extreme that they name: `segment_ids`: along each packed sequence the document numbers never fall; a document spans 1 to 800 tokens, and one document spans exactly that many.
All inputs are finite; a program needn't handle non-finite values.
Results may differ from a plain program's by a relative error of at most 0.023.
Values may be sent and summed in bfloat16 or wider, within the bound.
A program may use at most 128 MiB of HBM per device.

v0:
```python
from functools import partial

import jax
import jax.numpy as jnp
from jax import lax
from jax.sharding import PartitionSpec as P

HEAD_DIM = 64


EPSILON = 1e-05
SCORE_MASK = -1e30


def norm_rows(values, scale_vec, shift_vec):
    center = values - jnp.mean(values, axis=-1, keepdims=True)
    spread = jnp.mean(center * center, axis=-1, keepdims=True)
    return center * lax.rsqrt(spread + EPSILON) * scale_vec + shift_vec


def split_heads(rows):
    return rows.reshape(rows.shape[0], rows.shape[1] // HEAD_DIM, HEAD_DIM)


def masked_scores(query_heads, key_heads, segment_seq):
    scores = jnp.einsum(
        "qhd,khd->hqk", query_heads, key_heads, preferred_element_type=jnp.float32
    ) * HEAD_DIM ** (-0.5)
    same_doc = segment_seq[:, None] == segment_seq[None, :]
    return jnp.where(same_doc[None], scores, SCORE_MASK)


def attend_forward(pieces):
    query_seq, key_seq, value_seq, segment_seq = pieces
    scores = masked_scores(split_heads(query_seq), split_heads(key_seq), segment_seq)
    row_peak = jnp.max(scores, axis=-1, keepdims=True)
    exponent = jnp.exp(scores - row_peak)
    row_total = jnp.sum(exponent, axis=-1, keepdims=True)
    prob_low = (exponent / row_total).astype(jnp.bfloat16)
    mixed_heads = jnp.einsum(
        "hqk,khd->qhd", prob_low, split_heads(value_seq), preferred_element_type=jnp.float32
    )
    mixed_rows = mixed_heads.reshape(query_seq.shape).astype(jnp.bfloat16)
    return (mixed_rows, (row_peak + jnp.log(row_total))[..., 0])


def attend_backward(pieces):
    query_seq, key_seq, value_seq, segment_seq, logsum, grad_seq = pieces
    query_heads = split_heads(query_seq)
    key_heads = split_heads(key_seq)
    grad_heads = split_heads(grad_seq)
    scores = masked_scores(query_heads, key_heads, segment_seq)
    prob_full = jnp.exp(scores - logsum[..., None])
    prob_low = prob_full.astype(jnp.bfloat16)
    d_value = jnp.einsum("hqk,qhd->khd", prob_low, grad_heads, preferred_element_type=jnp.float32)
    d_prob = jnp.einsum(
        "qhd,khd->hqk", grad_heads, split_heads(value_seq), preferred_element_type=jnp.float32
    )
    d_scores = prob_full * (d_prob - jnp.sum(prob_full * d_prob, axis=-1, keepdims=True))
    d_scores = d_scores.astype(jnp.bfloat16)
    d_query = jnp.einsum(
        "hqk,khd->qhd", d_scores, key_heads, preferred_element_type=jnp.float32
    ) * HEAD_DIM ** (-0.5)
    d_key = jnp.einsum(
        "hqk,qhd->khd", d_scores, query_heads, preferred_element_type=jnp.float32
    ) * HEAD_DIM ** (-0.5)
    shape_rows = query_seq.shape
    return (
        d_query.reshape(shape_rows).astype(jnp.bfloat16),
        d_key.reshape(shape_rows).astype(jnp.bfloat16),
        d_value.reshape(shape_rows).astype(jnp.bfloat16),
    )


def local(
    layer_input,
    segment_ids,
    w_query,
    b_query,
    w_key,
    w_value,
    b_value,
    w_out,
    b_out,
    first_gain,
    first_shift,
    w_in,
    b_in,
    w_back,
    b_back,
    second_gain,
    second_shift,
    cotangent,
):
    seq_count, length = segment_ids.shape
    width_local = w_query.shape[1]

    def by_sequence(rows):
        return rows.reshape(seq_count, length, width_local)

    full_rows = lax.all_gather(layer_input, "tensor", axis=0, tiled=True)
    query_rows = (
        jnp.dot(full_rows, w_query, preferred_element_type=jnp.float32)
        + b_query.astype(jnp.float32)
    ).astype(jnp.bfloat16)
    key_rows = jnp.dot(full_rows, w_key, preferred_element_type=jnp.float32).astype(jnp.bfloat16)
    value_rows = (
        jnp.dot(full_rows, w_value, preferred_element_type=jnp.float32)
        + b_value.astype(jnp.float32)
    ).astype(jnp.bfloat16)
    mixed_rows, logsum = lax.map(
        attend_forward,
        (by_sequence(query_rows), by_sequence(key_rows), by_sequence(value_rows), segment_ids),
    )
    heads_out = mixed_rows.reshape(seq_count * length, width_local)
    attn_rows = lax.psum_scatter(
        jnp.dot(heads_out, w_out, preferred_element_type=jnp.float32).astype(jnp.bfloat16),
        "tensor",
        scatter_dimension=0,
        tiled=True,
    ).astype(jnp.float32)
    first_in = layer_input.astype(jnp.float32) + attn_rows + b_out
    first_norm, first_pull = jax.vjp(norm_rows, first_in, first_gain, first_shift)
    first_low = first_norm.astype(jnp.bfloat16)
    wide_in, wide_bias, wide_back = (w_in, b_in, w_back)
    rows_in = lax.all_gather(first_low, "tensor", axis=0, tiled=True)
    hidden_pre = jnp.dot(rows_in, wide_in, preferred_element_type=jnp.float32) + wide_bias.astype(
        jnp.float32
    )
    gelu_value, gelu_pull = jax.vjp(partial(jax.nn.gelu, approximate=False), hidden_pre)
    hidden = gelu_value.astype(jnp.bfloat16)
    ffn_term = jnp.dot(hidden, wide_back, preferred_element_type=jnp.float32)
    ffn_sum = lax.psum_scatter(
        ffn_term.astype(jnp.bfloat16), "tensor", scatter_dimension=0, tiled=True
    ).astype(jnp.float32)
    second_in = first_norm + ffn_sum + b_back
    output, second_pull = jax.vjp(norm_rows, second_in, second_gain, second_shift)
    d_second, d_second_gain, d_second_shift = second_pull(cotangent.astype(jnp.float32))
    d_back_bias = jnp.sum(d_second, axis=0)
    d_second_low = d_second.astype(jnp.bfloat16)
    grad_rows = lax.all_gather(d_second_low, "tensor", axis=0, tiled=True)
    d_w_back = jnp.einsum("tf,td->fd", hidden, grad_rows, preferred_element_type=jnp.float32)
    d_hidden = jnp.einsum("td,fd->tf", grad_rows, wide_back, preferred_element_type=jnp.float32)
    d_pre = gelu_pull(d_hidden)[0].astype(jnp.bfloat16)
    d_b_in = jnp.sum(d_pre.astype(jnp.float32), axis=0)
    d_w_in = jnp.einsum("td,tf->df", rows_in, d_pre, preferred_element_type=jnp.float32)
    first_term = jnp.einsum("tf,df->td", d_pre, wide_in, preferred_element_type=jnp.float32)
    d_first = d_second + lax.psum_scatter(
        first_term.astype(jnp.bfloat16), "tensor", scatter_dimension=0, tiled=True
    ).astype(jnp.float32)
    d_first_in, d_first_gain, d_first_shift = first_pull(d_first)
    d_out_bias = jnp.sum(d_first_in, axis=0)
    attn_grad = lax.all_gather(d_first_in.astype(jnp.bfloat16), "tensor", axis=0, tiled=True)
    d_w_out = jnp.einsum("te,td->ed", heads_out, attn_grad, preferred_element_type=jnp.float32)
    d_heads = jnp.einsum("td,ed->te", attn_grad, w_out, preferred_element_type=jnp.float32).astype(
        jnp.bfloat16
    )
    d_query, d_key, d_value = lax.map(
        attend_backward,
        (
            by_sequence(query_rows),
            by_sequence(key_rows),
            by_sequence(value_rows),
            segment_ids,
            logsum,
            by_sequence(d_heads),
        ),
    )
    row_count = seq_count * length
    d_query = d_query.reshape(row_count, width_local)
    d_key = d_key.reshape(row_count, width_local)
    d_value = d_value.reshape(row_count, width_local)
    d_w_query = jnp.einsum("td,te->de", full_rows, d_query, preferred_element_type=jnp.float32)
    d_w_key = jnp.einsum("td,te->de", full_rows, d_key, preferred_element_type=jnp.float32)
    d_w_value = jnp.einsum("td,te->de", full_rows, d_value, preferred_element_type=jnp.float32)
    d_b_query = jnp.sum(d_query.astype(jnp.float32), axis=0)
    d_b_value = jnp.sum(d_value.astype(jnp.float32), axis=0)
    input_term = jnp.einsum("te,de->td", d_query, w_query, preferred_element_type=jnp.float32)
    input_term = input_term + jnp.einsum(
        "te,de->td", d_key, w_key, preferred_element_type=jnp.float32
    )
    input_term = input_term + jnp.einsum(
        "te,de->td", d_value, w_value, preferred_element_type=jnp.float32
    )
    input_grad = (
        d_first_in
        + lax.psum_scatter(
            input_term.astype(jnp.bfloat16), "tensor", scatter_dimension=0, tiled=True
        ).astype(jnp.float32)
    ).astype(jnp.bfloat16)
    split_sums = (
        lax.psum(d_w_query.astype(jnp.bfloat16), "dp").astype(jnp.float32),
        lax.psum(d_b_query.astype(jnp.bfloat16), "dp").astype(jnp.float32),
        lax.psum(d_w_key.astype(jnp.bfloat16), "dp").astype(jnp.float32),
        lax.psum(d_w_value.astype(jnp.bfloat16), "dp").astype(jnp.float32),
        lax.psum(d_b_value.astype(jnp.bfloat16), "dp").astype(jnp.float32),
        lax.psum(d_w_out.astype(jnp.bfloat16), "dp").astype(jnp.float32),
        lax.psum(d_w_in.astype(jnp.bfloat16), "dp").astype(jnp.float32),
        lax.psum(d_b_in.astype(jnp.bfloat16), "dp").astype(jnp.float32),
        lax.psum(d_w_back.astype(jnp.bfloat16), "dp").astype(jnp.float32),
    )
    shared_sums = lax.psum(
        (d_out_bias, d_first_gain, d_first_shift, d_back_bias, d_second_gain, d_second_shift),
        ("dp", "tensor"),
    )
    return (
        output.astype(jnp.bfloat16),
        input_grad,
        split_sums[0],
        split_sums[1],
        split_sums[2],
        split_sums[3],
        split_sums[4],
        split_sums[5],
        shared_sums[0],
        shared_sums[1],
        shared_sums[2],
        split_sums[6],
        split_sums[7],
        split_sums[8],
        shared_sums[3],
        shared_sums[4],
        shared_sums[5],
    )


def solution(mesh):
    in_specs = (
        P(("dp", "tensor"), None),
        P("dp", None),
        P(None, "tensor"),
        P("tensor"),
        P(None, "tensor"),
        P(None, "tensor"),
        P("tensor"),
        P("tensor", None),
        P(),
        P(),
        P(),
        P(None, "tensor"),
        P("tensor"),
        P("tensor", None),
        P(),
        P(),
        P(),
        P(("dp", "tensor"), None),
    )
    out_specs = (
        P(("dp", "tensor"), None),
        P(("dp", "tensor"), None),
        P(None, "tensor"),
        P("tensor"),
        P(None, "tensor"),
        P(None, "tensor"),
        P("tensor"),
        P("tensor", None),
        P(),
        P(),
        P(),
        P(None, "tensor"),
        P("tensor"),
        P("tensor", None),
        P(),
        P(),
        P(),
    )
    return jax.shard_map(local, mesh=mesh, in_specs=in_specs, out_specs=out_specs, check_vma=False)
```

profile of v0, /device:TPU:4, one launch (start us, length us, event | category | flops | bytes accessed | tf_op | source)
XLA Modules:
  0.0 787.1 jit_solution(8936208881471157958)
XLA Ops:
  9.3 37.8 %all-gather.5.cloned.1.call-done = bf16[3072,768]{1,0:T(8,128)(2,1)} async-done(((bf16[768,768]{1,0:T(8,128)(2,1)}), bf16[3072,768]{1,0:T(8,128)(2,1)}) %all-gather.5.cloned.1.call-update) | async-done | bytes 4718608 | tf_op jit(solution)/shard_map/all_gather | solution.py:101
  57.7 72.2 %while.26 = (s32[]{:T(128)}, bf16[3,1024,192]{1,2,0:T(8,128)(2,1)}, f32[3,3,1024]{2,1,0:T(4,128)}, bf16[3,1024,192]{1,2,0:T(8,128)(2,1)S(1)}, s32[3,1024]{1,0:T(...) while((s32[]{:T(128)}, bf16[3,1024,192]{1,2,0:T(8,128)(2,1)}, ...), condition=%wide.region_3.4_spmd, body=%wide.region_0.3_spmd.sunk | while | flops 844297216 | bytes 46777440 | solution.py:111
  66.1 7.3 fusion.118
  90.2 7.3 fusion.118
  114.2 7.3 fusion.118
  137.5 47.9 %reduce-scatter.5.cloned.1.call-done = bf16[768,768]{1,0:T(8,128)(2,1)} async-done(((bf16[3072,768]{1,0:T(8,128)(2,1)}), bf16[768,768]{1,0:T(8,128)(2,1)}) %reduce-scatter.5.cloned.1.call-update) | async-done | bytes 1179664 | tf_op jit(solution)/shard_map/reduce_scatter | solution.py:116
  192.2 36.3 %all-gather.7.cloned.1.call-done = bf16[3072,768]{1,0:T(8,128)(2,1)} async-done(((bf16[768,768]{1,0:T(8,128)(2,1)}), bf16[3072,768]{1,0:T(8,128)(2,1)}) %all-gather.7.cloned.1.call-update) | async-done | bytes 4718608 | tf_op jit(solution)/shard_map/all_gather | solution.py:126
  228.4 26.2 %multiply_convert_fusion.1 = (bf16[3072,768]{1,0:T(8,128)(2,1)S(1)}, f32[3072,768]{1,0:T(8,128)}, f32[3072,768]{1,0:T(8,128)}) fusion(f32[768]{0:T(1024)} %convert_element_type.214, bf16[3072,768]{1,0:T(8,128)(2,1)} %all-gather.7.cloned.1.call-done, bf16[768,768]{1,0:T(8,128)(2,1)S(1)} %copy-done), kind=kOutput, calls=%fused_computation.43 | convolution fusion | flops 3779592192 | bytes 29494272 | tf_op jit(solution)/shard_map/dot_general | solution.py:127
  262.3 48.1 %reduce-scatter.7.cloned.1.call-done = bf16[768,768]{1,0:T(8,128)(2,1)} async-done(((bf16[3072,768]{1,0:T(8,128)(2,1)}), bf16[768,768]{1,0:T(8,128)(2,1)}) %reduce-scatter.7.cloned.1.call-update) | async-done | bytes 1179664 | tf_op jit(solution)/shard_map/reduce_scatter | solution.py:133
  320.1 37.1 %all-gather.9.cloned.1.call-done = bf16[3072,768]{1,0:T(8,128)(2,1)} async-done(((bf16[768,768]{1,0:T(8,128)(2,1)}), bf16[3072,768]{1,0:T(8,128)(2,1)}) %all-gather.9.cloned.1.call-update) | async-done | bytes 4718608 | tf_op jit(solution)/shard_map/all_gather | solution.py:141
  357.3 13.5 %fusion.38 = (bf16[768]{0:T(1024)(128)(2,1)}, bf16[3072,768]{1,0:T(8,128)(2,1)S(1)}) fusion(f32[3072,768]{1,0:T(8,128)} %get-tuple-element.213, f32[3072,768]{1,0:T(8,128)} %get-tuple-element.225, f32[768]{0:T(1024)} %convert_element_type.214, bf16[3072,768]{1,0:T(8,128)(2,1)} %all-gather.9.cloned.1.call-done, bf16[768,768]{1,0:T(8,128)(2,1)} %param.35), kind=kOutput, calls=%fused_computation.116 | convolution fusion | flops 3661626624 | bytes 29495808 | tf_op jit(solution)/shard_map/td,fd->tf/dot_general | solution.py:143
  378.6 48.1 %reduce-scatter.9.cloned.1.call-done = bf16[768,768]{1,0:T(8,128)(2,1)} async-done(((bf16[3072,768]{1,0:T(8,128)(2,1)}), bf16[768,768]{1,0:T(8,128)(2,1)}) %reduce-scatter.9.cloned.1.call-update) | async-done | bytes 1179664 | tf_op jit(solution)/shard_map/reduce_scatter | solution.py:148
  437.5 8.7 %convolution_convert_fusion.5 = bf16[768,768]{1,0:T(8,128)(2,1)} fusion(bf16[3072,768]{1,0:T(8,128)(2,1)} %copy-done.44, bf16[3072,768]{1,0:T(8,128)(2,1)} %all-gather.9.cloned.1.call-done), kind=kOutput, calls=%fused_computation.92 | convolution fusion | flops 3624468480 | bytes 10616832 | tf_op jit(solution)/shard_map/tf,td->fd/dot_general | solution.py:142
  446.2 9.7 %convolution_convert_fusion.6 = bf16[768,768]{1,0:T(8,128)(2,1)} fusion(bf16[3072,768]{1,0:T(8,128)(2,1)} %all-gather.7.cloned.1.call-done, bf16[3072,768]{1,0:T(8,128)(2,1)} %copy-done.45), kind=kOutput, calls=%fused_computation.93 | convolution fusion | flops 3624468480 | bytes 10616832 | tf_op jit(solution)/shard_map/td,tf->df/dot_general | solution.py:146
  455.8 19.0 %all-gather.11.cloned.1.call-done = bf16[3072,768]{1,0:T(8,128)(2,1)} async-done(((bf16[768,768]{1,0:T(8,128)(2,1)}), bf16[3072,768]{1,0:T(8,128)(2,1)}) %all-gather.11.cloned.1.call-update) | async-done | bytes 4718608 | tf_op jit(solution)/shard_map/all_gather | solution.py:153
  482.4 91.1 %while.27 = (s32[]{:T(128)}, bf16[3,1024,192]{1,2,0:T(8,128)(2,1)S(1)}, bf16[3,1024,192]{1,2,0:T(8,128)(2,1)}, bf16[3,1024,192]{1,2,0:T(8,128)(2,1)}, bf16[3,102...) while((s32[]{:T(128)}, ...), condition=%wide.region_17.18_spmd, body=%wide.region_15.17_spmd.sunk | while | flops 2062480384 | bytes 108102272 | solution.py:158
  490.7 7.2 multiply_reduce_fusion.6
  497.8 6.9 multiply_convert_fusion.3
  520.9 7.2 multiply_reduce_fusion.6
  551.1 7.2 multiply_reduce_fusion.6
  597.0 46.6 %all-reduce = (f32[768]{0:T(1024)}, f32[768]{0:T(1024)}, f32[768]{0:T(1024)}, f32[768]{0:T(1024)}, f32[768]{0:T(1024)}, /*index=5*/f32[768]{0:T(1024)}) all-reduce(f32[768]{0:T(1024)S(1)} %copy-done.39, f32[768]{0:T(1024)S(1)} %copy-done.36, f32[768]{0:T(1024)S(1)} %copy-done.37, ...), channel_id=1, replica_groups=mesh['dp'=8,'tensor'=4] {'dp','tensor'}, use_global_device_ids=true, to_apply=%region_28.29 | all-reduce | flops 4608 | bytes 36864 | tf_op jit(solution)/shard_map/psum | solution.py:202
  644.1 19.2 %all-reduce.1 = (bf16[192]{0:T(256)(128)(2,1)S(1)}, bf16[192]{0:T(256)(128)(2,1)S(1)}, bf16[768]{0:T(1024)(128)(2,1)S(1)}) all-reduce(bf16[192]{0:T(256)(128)(2,1)S(1)} %reduce_sum.220, bf16[192]{0:T(256)(128)(2,1)S(1)} %reduce_sum.221, bf16[768]{0:T(1024)(128)(2,1)S(1)} %copy-done.41), channel_id=1, replica_groups=mesh['dp'=8,'tensor'=4] {'dp'}, use_global_device_ids=true, to_apply=%region_21.22 | all-reduce | flops 1152 | bytes 4608 | tf_op jit(solution)/shard_map/psum | solution.py:193
  665.0 63.4 %all-reduce.5.cloned.1.call-done = (bf16[768,192]{0,1:T(8,128)(2,1)}, bf16[768,192]{0,1:T(8,128)(2,1)}, bf16[768,192]{0,1:T(8,128)(2,1)}, bf16[192,768]{1,0:T(8,...) async-done(((bf16[768,192]{0,1:T(8,128)(2,1)}, bf16[768,192]{0,1:T(8,128)(2,1)}, bf16[768,192]{0,1:T(8,128)(2,1)}, bf16[192,768]{1,0:T(8,128)(2,1)}, ...) | async-done | bytes 3538960 | tf_op jit(solution)/shard_map/psum | solution.py:192
  736.4 40.3 %reduce-scatter.11.cloned.1.call-done = bf16[768,768]{1,0:T(8,128)(2,1)} async-done(((bf16[3072,768]{1,0:T(8,128)(2,1)}), bf16[768,768]{1,0:T(8,128)(2,1)}) %reduce-scatter.11.cloned.1.call-update) | async-done | bytes 1179664 | tf_op jit(solution)/shard_map/reduce_scatter | solution.py:187
  (240 shorter events, 219.5 us)
Async XLA Ops:
  7.2 221.2 %copy-start = (bf16[768,768]{1,0:T(8,128)(2,1)S(1)}, bf16[768,768]{1,0:T(8,128)(2,1)}, u32[]{:S(2)}) copy-start(bf16[768,768]{1,0:T(8,128)(2,1)} %param.33) | copy-start | bytes 3538948
  7.2 39.9 %all-gather.5.cloned.1.call-start = ((), (), s32[]{:S(2)}) async-start(), calls=%async_computation.4 | async-start | bytes 5898240 | tf_op jit(solution)/shard_map/all_gather | solution.py:101
  7.9 177.4 %reduce-scatter.5.cloned.1.call-start = ((), (), s32[]{:S(2)}) async-start(), calls=%async_computation.5 | async-start | bytes 5898240 | tf_op jit(solution)/shard_map/reduce_scatter | solution.py:116
  129.8 7.4 copy-start.6
  137.2 48.2 %copy-start.2 = (bf16[768,768]{1,0:T(8,128)(2,1)S(1)}, bf16[768,768]{1,0:T(8,128)(2,1)}, u32[]{:S(2)}) copy-start(bf16[768,768]{1,0:T(8,128)(2,1)} %param.22) | copy-start | bytes 3538948
  137.2 48.2 %copy-start.27 = (f32[768]{0:T(1024)S(1)}, f32[768]{0:T(1024)}, u32[]{:S(2)}) copy-start(f32[768]{0:T(1024)} %param.30) | copy-start | bytes 9220
  137.2 51.2 %copy-start.28 = (f32[768]{0:T(1024)S(1)}, f32[768]{0:T(1024)}, u32[]{:S(2)}) copy-start(f32[768]{0:T(1024)} %param.31) | copy-start | bytes 9220
  137.2 91.2 %all-gather.7.cloned.1.call-start = ((), (), s32[]{:S(2)}) async-start(), calls=%async_computation.6 | async-start | bytes 5898240 | tf_op jit(solution)/shard_map/all_gather | solution.py:126
  190.8 119.6 %reduce-scatter.7.cloned.1.call-start = ((), (), s32[]{:S(2)}) async-start(), calls=%async_computation.7 | async-start | bytes 5898240 | tf_op jit(solution)/shard_map/reduce_scatter | solution.py:133
  228.4 28.3 %copy-start.43 = (bf16[768,768]{1,0:T(8,128)(2,1)S(1)}, bf16[768,768]{1,0:T(8,128)(2,1)}, u32[]{:S(2)}) copy-start(bf16[768,768]{1,0:T(8,128)(2,1)} %param.35) | copy-start | bytes 3538948
  262.3 95.0 %all-gather.9.cloned.1.call-start = ((), (), s32[]{:S(2)}) async-start(), calls=%async_computation.8 | async-start | bytes 5898240 | tf_op jit(solution)/shard_map/all_gather | solution.py:141
  319.7 107.0 %reduce-scatter.9.cloned.1.call-start = ((), (), s32[]{:S(2)}) async-start(), calls=%async_computation.9 | async-start | bytes 5898240 | tf_op jit(solution)/shard_map/reduce_scatter | solution.py:148
  378.5 96.3 %all-gather.11.cloned.1.call-start = ((), (), s32[]{:S(2)}) async-start(), calls=%async_computation.10 | async-start | bytes 5898240 | tf_op jit(solution)/shard_map/all_gather | solution.py:153
  437.2 291.2 %all-reduce.5.cloned.1.call-start = ((), (), s32[]{:S(2)}) async-start(), calls=%async_computation.12 | async-start | bytes 7077888 | tf_op jit(solution)/shard_map/psum | solution.py:192
  446.2 28.6 %copy-start.19 = (bf16[192,768]{1,0:T(8,128)(2,1)S(1)}, bf16[192,768]{1,0:T(8,128)(2,1)}, u32[]{:S(2)}) copy-start(bf16[192,768]{1,0:T(8,128)(2,1)} %param.29) | copy-start | bytes 884740
  573.5 7.7 slice-start
  573.6 7.6 copy-start.13
  575.3 7.8 copy-start.11
  575.5 5.7 slice-start.1
  575.9 9.0 %copy-start.15 = (bf16[3,24,8,1024]{3,2,0,1:T(8,128)(2,1)}, bf16[3,24,8,1024]{3,2,0,1:T(8,128)(2,1)S(1)}, u32[]{:S(2)}) copy-start(bf16[3,24,8,1024]{3,2,0,1:T(8,128)(2,1)S(1)} %copy.72) | copy-start | bytes 3538948
  586.8 190.0 %reduce-scatter.11.cloned.1.call-start = ((), (), s32[]{:S(2)}) async-start(), calls=%async_computation.11 | async-start | bytes 5898240 | tf_op jit(solution)/shard_map/reduce_scatter | solution.py:187
  596.3 47.8 %copy-start.41 = (bf16[768]{0:T(1024)(128)(2,1)S(1)}, bf16[768]{0:T(1024)(128)(2,1)}, u32[]{:S(2)}) copy-start(bf16[768]{0:T(1024)(128)(2,1)} %get-tuple-element.204) | copy-start | bytes 4612
  731.4 45.3 %copy-start.32 = (f32[768]{0:T(1024)S(1)}, f32[768]{0:T(1024)}, u32[]{:S(2)}) copy-start(f32[768]{0:T(1024)} %copy-done.31) | copy-start | bytes 9220
  734.7 45.4 %copy-start.1 = (bf16[768,768]{1,0:T(8,128)(2,1)S(1)}, bf16[768,768]{1,0:T(8,128)(2,1)}, u32[]{:S(2)}) copy-start(bf16[768,768]{1,0:T(8,128)(2,1)} %param.33) | copy-start | bytes 3538948
  (33 other events, 80.0 us)
Sparse Core Ops, SparseCore 0:
  9.6 37.4 all-gather.4
  137.4 47.9 reduce-scatter.4
  191.0 37.4 all-gather.6
  262.4 47.9 reduce-scatter.6
  319.8 37.4 all-gather.8
  378.7 47.9 reduce-scatter.8
  437.4 37.4 all-gather.10
  586.9 141.5 all-reduce.4
  731.0 45.7 reduce-scatter.10
where the time goes:
time: 800 us; the launch traced here: 787 us
  waiting for transfers between devices  379 us (47%)
  matrix products  192 us (24%)
  other arithmetic  86.4 us (11%)
  blocking collectives  65.8 us (8%)
  local copies, waits for them, and re-layouts  47.8 us (6%)
  between operations  14.7 us (2%)
    psum x1, waiting for transfers between devices, local(): lax.psum(d_w_query.astype(jnp.bfloat16), 'dp').astype(jnp.float32)  63.4 us
    reduce_scatter x1, waiting for transfers between devices, local(): lax.psum_scatter(ffn_term.astype(jnp.bfloat16), 'tensor', scatter_dimensi...  48.1 us
    reduce_scatter x1, waiting for transfers between devices, local(): lax.psum_scatter(first_term.astype(jnp.bfloat16), 'tensor', scatter_dimen...  48.1 us
    reduce_scatter x1, waiting for transfers between devices, local(): lax.psum_scatter(jnp.dot(heads_out, w_out, preferred_element_type=jnp.flo...  47.9 us
    psum x1, blocking collectives, local(): lax.psum((d_out_bias, d_first_gain, d_first_shift, d_back_bias, d_second_...  46.6 us
    reduce_scatter x1, waiting for transfers between devices, local(): lax.psum_scatter(input_term.astype(jnp.bfloat16), 'tensor', scatter_dimen...  40.3 us
    all_gather x1, waiting for transfers between devices, local(): full_rows = lax.all_gather(layer_input, 'tensor', axis=0, tiled=True)  37.8 us
    all_gather x1, waiting for transfers between devices, local(): grad_rows = lax.all_gather(d_second_low, 'tensor', axis=0, tiled=True)  37.1 us
  transfers between devices with their start and end apart: 9, of which 9 were waited for; matrix products, arithmetic and copies ran while one was open for 5% of the time, Pallas kernels for 0%

commit v1 on v0

v1 whole, which is shorter than its diff:
```python
import math

import jax
import jax.numpy as jnp
from jax import lax
from jax.experimental import pallas as pl
from jax.experimental.pallas import tpu as pltpu
from jax.sharding import PartitionSpec as P

F32 = jnp.float32
BF = jnp.bfloat16
MESH = pl.DeviceIdType.MESH
HEAD_DIM = 64
EPSILON = 1e-05
BIG = 1e30
LOG2E = 1.0 / math.log(2.0)
QSCALE = HEAD_DIM ** (-0.5) * LOG2E
BLK = 256


def dg(a, b, ca, cb):
    return lax.dot_general(a, b, (((ca,), (cb,)), ((), ())), preferred_element_type=F32)


def where_am_i():
    t = lax.axis_index("tensor")
    d = lax.axis_index("dp")
    core = t + 1 - 2 * (t % 2)
    across = (t + 2) % 4
    diag = 3 - t
    side = d + 1 - 2 * (d % 2)
    return t, d, core, across, diag, side


def block_of(t, i):
    b = 3 * t + i
    middle = (b // 4) % 2
    return middle, b % 4


class Copies:
    def __init__(self, send, recv):
        self.send, self.recv, self.used = send, recv, 0

    def new(self, src, dst, **device):
        k = self.used
        self.used += 1
        return pltpu.make_async_remote_copy(
            src_ref=src,
            dst_ref=dst,
            send_sem=self.send.at[k],
            recv_sem=self.recv.at[k],
            device_id=device,
            device_id_type=MESH,
        )


def greet(devices):
    barrier = pltpu.get_barrier_semaphore()
    for dev in devices:
        pl.semaphore_signal(barrier, inc=1, device_id=dev, device_id_type=MESH)
    pl.semaphore_wait(barrier, len(devices))


def gather_shard(cp, own, gathered, core, across, side, half):
    rows = own.shape[0] // 2
    part = pl.ds(pl.multiple_of(half * rows, rows), rows)
    first = [
        cp.new(own.at[part], gathered.at[1, part], tensor=across),
        cp.new(own, gathered.at[0], tensor=core),
    ]
    second = cp.new(gathered.at[1, part], gathered.at[1, part], dp=side)
    third = cp.new(gathered.at[1], gathered.at[2], tensor=core)
    return first, second, third


def k1(
    x_ref, wt_ref, bias_ref, seg_ref, wout_ref, win_ref,
    qkv_ref, o_ref, lse_ref, xab_ref, wpar_ref, woutg_ref, wing_ref, biasg_ref,
    wt_v, qa, ka, va, send, recv, local,
):
    length = 1024
    t, d, core, across, diag, side = where_am_i()
    y, c = t // 2, t % 2
    half = d % 2
    greet([{"tensor": core}, {"tensor": across}, {"tensor": diag}, {"dp": side}])
    cp = Copies(send, recv)
    rows_out, rows_local = [], []
    for i in range(3):
        middle, blk = block_of(t, i)
        src = x_ref.at[pl.ds(i * BLK, BLK)]
        dst = xab_ref.at[middle, pl.ds(pl.multiple_of(blk * BLK, BLK), BLK)]
        rows_local.append(pltpu.make_async_copy(src, dst, local.at[i]))
        rows_out.append(cp.new(src, dst, tensor=core))
    w_local = pltpu.make_async_copy(wt_ref, wt_v, local.at[3])
    for copy in rows_local + [w_local] + rows_out:
        copy.start()
    rows = wt_ref.shape[0] // 2
    part = pl.ds(pl.multiple_of(half * rows, rows), rows)
    wp_first = cp.new(wt_ref.at[part], wpar_ref.at[part], tensor=across)
    wp_second = cp.new(wpar_ref.at[part], wpar_ref.at[part], dp=side)
    bias_out = [
        cp.new(bias_ref, biasg_ref.at[0], tensor=core),
        cp.new(bias_ref, biasg_ref.at[1], tensor=across),
        cp.new(bias_ref, biasg_ref.at[2], tensor=diag),
    ]
    cross_in = 2 * (1 - y) + c
    cross_slot = pl.ds(pl.multiple_of(cross_in * BLK, BLK), BLK)
    mixed = (t == 1) | (t == 2)
    first_middle = jnp.where(t == 1, 1, 0)
    cross_out = []
    base = cp.used
    for k in range(2):
        src = x_ref.at[pl.ds(pl.multiple_of((first_middle + k) * BLK, BLK), BLK)]
        dst_blk = 2 * y + k
        dst = xab_ref.at[1, pl.ds(pl.multiple_of(dst_blk * BLK, BLK), BLK)]
        cross_out.append(
            pltpu.make_async_remote_copy(
                src_ref=src, dst_ref=dst, send_sem=send.at[base + k], recv_sem=recv.at[base],
                device_id={"tensor": 2 * (1 - y) + k}, device_id_type=MESH,
            )
        )
    cp.used += 2
    cross_arrived = pltpu.make_async_remote_copy(
        src_ref=x_ref.at[pl.ds(0, BLK)], dst_ref=xab_ref.at[1, cross_slot], send_sem=send.at[base],
        recv_sem=recv.at[base], device_id={"tensor": core}, device_id_type=MESH,
    )
    cross_forward = cp.new(xab_ref.at[1, cross_slot], xab_ref.at[1, cross_slot], tensor=core)

    wp_first.start()
    for copy in bias_out:
        copy.start()

    @pl.when(mixed)
    def _():
        for copy in cross_out:
            copy.start()

    out1, out2, out3 = gather_shard(cp, wout_ref, woutg_ref, core, across, side, half)
    in1, in2, in3 = gather_shard(cp, win_ref, wing_ref, core, across, side, half)
    for copy in out1 + in1:
        copy.start()

    def project(g, middle, w, bias):
        col = jnp.transpose(bias)[0:576, 1:2]

        def body(n, _):
            cs = pl.ds(pl.multiple_of(n * BLK, BLK), BLK)
            r = dg(w[...], xab_ref[middle, cs, :], 1, 1) + col
            qkv_ref[g, 0:192, cs] = (r[0:192] * QSCALE).astype(BF)
            qkv_ref[g, 192:576, cs] = r[192:576].astype(BF)
            return 0

        lax.fori_loop(0, length // BLK, body, 0)

    def attend(g, which):
        seg = seg_ref[which]
        row = lax.broadcasted_iota(jnp.int32, (64, length), 0)
        same = (row == seg).astype(F32)
        qa[64:128, :] = same.astype(BF)
        key_mark = ((same - 1.0) * BIG).astype(BF)
        va[64:80, :] = jnp.ones((16, length), BF)

        def unit(h, _):
            r = pl.multiple_of(h * 64, 64)
            qa[0:64, :] = qkv_ref[g, pl.ds(r, 64), :]
            ka[...] = jnp.concatenate([qkv_ref[g, pl.ds(r + 192, 64), :], key_mark], axis=0).T
            va[0:64, :] = qkv_ref[g, pl.ds(r + 384, 64), :]
            s = jnp.dot(ka[...], qa[...], preferred_element_type=F32)
            m = jnp.max(s, axis=0, keepdims=True)
            p = jnp.exp2(s - m).astype(BF)
            o = jnp.dot(va[...], p, preferred_element_type=F32)
            total = o[64:65, :]
            res = (o[0:64] * (1.0 / total)).astype(BF)
            for b in range(4):
                o_ref[g, b, pl.ds(r, 64), :] = res[:, b * BLK : (b + 1) * BLK]
            lse_ref[g * 3 + h] = m + jnp.log2(total)
            return 0

        lax.fori_loop(0, 3, unit, 0)

    for copy in rows_local + [w_local]:
        copy.wait()
    for copy in rows_out:
        copy.wait_recv()
    own_seq = 2 * y
    project(0, 0, wt_v, bias_ref[...])
    attend(0, own_seq)
    wp_first.wait_recv()
    wp_second.start()
    cross_arrived.wait_recv()
    cross_forward.start()
    bias_out[1].wait_recv()
    cross_forward.wait_recv()
    project(2, 1, wt_v, bias_ref[...])
    attend(2, 1)
    out1[0].wait_recv()
    out2.start()
    wp_second.wait_recv()
    project(1, 0, wpar_ref, biasg_ref[1])
    attend(1, own_seq)
    out2.wait_recv()
    out3.start()
    in1[0].wait_recv()
    in2.start()
    in2.wait_recv()
    in3.start()
    for copy in (bias_out[0], bias_out[2], out1[1], in1[1], out3, in3):
        copy.wait_recv()
    for copy in rows_out + [wp_first, wp_second, cross_forward] + bias_out + out1 + in1 + [out2, in2, out3, in3]:
        copy.wait_send()

    @pl.when(mixed)
    def _():
        for copy in cross_out:
            copy.wait_send()


def layer_stats(z):
    mean = jnp.mean(z, axis=-1, keepdims=True)
    cen = z - mean
    var = jnp.mean(cen * cen, axis=-1, keepdims=True)
    inv = lax.rsqrt(var + EPSILON)
    return cen * inv, inv


def k2(
    x_ref, cot_ref, vec_ref, bias_ref, biasg_ref, o_ref, wout_ref, woutg_ref, win_ref, wing_ref, wback_ref,
    out_ref, dz1_ref, do_ref, g_ref, small_ref,
    ot, wo, wi, wb, wbg, h1b, h1t, xh1, inv1, gg, gp, z2, dz2b, dz2t, dz2, send, recv, local,
):
    t, d, core, across, diag, side = where_am_i()
    half = d % 2
    tok = x_ref.shape[0]
    greet([{"tensor": core}, {"tensor": across}, {"tensor": diag}, {"dp": side}])
    cp = Copies(send, recv)

    peers = (t, core, across, diag)
    pending = []
    for j, dev in enumerate(peers):
        for i in range(3):
            middle, blk = block_of(dev, i)
            for second in (False, True) if j < 2 else (False,):
                slot = j + 2 if second else j
                src_group = 1 if second else None
                src = o_ref.at[1 if second else 2 * middle, blk]
                dst = ot.at[i, pl.ds(slot * 192, 192)]
                sem = recv.at[i * 4 + slot]
                if j == 0:
                    copy = pltpu.make_async_copy(src, dst, sem)
                else:
                    k = 3 * (4 + j) + i if not second else 24 + i
                    copy = pltpu.make_async_remote_copy(
                        src_ref=src, dst_ref=dst, send_sem=send.at[k], recv_sem=sem,
                        device_id={"tensor": dev}, device_id_type=MESH,
                    )
                if j == 0 and not second or j == 1 and not second:
                    cond = None
                elif second:
                    cond = middle == 0
                else:
                    cond = middle == 1
                if cond is None:
                    copy.start()
                else:
                    pl.when(cond)(copy.start)
                if j:
                    pending.append((cond, copy))
    cp.used = 27
    b1, b2, b3 = gather_shard(cp, wback_ref, wbg, core, across, side, half)
    for copy in b1:
        copy.start()
    loads = [pltpu.make_async_copy(wout_ref, wo.at[pl.ds(0, 192)], local.at[0])]
    loads += [pltpu.make_async_copy(woutg_ref.at[j], wo.at[pl.ds(192 * (j + 1), 192)], local.at[j + 1]) for j in range(3)]
    loads_in = [pltpu.make_async_copy(win_ref, wi.at[:, pl.ds(0, 768)], local.at[4])]
    loads_in += [pltpu.make_async_copy(wing_ref.at[j], wi.at[:, pl.ds(768 * (j + 1), 768)], local.at[5 + j]) for j in range(3)]
    load_b0 = pltpu.make_async_copy(wback_ref, wb.at[pl.ds(0, 768)], local.at[8])
    for copy in loads + loads_in + [load_b0]:
        copy.start()

    b_out, gain1, shift1, b_back, gain2, shift2 = [vec_ref[k : k + 1, :] for k in range(6)]
    for copy in loads:
        copy.wait()
    for i in range(3):
        for slot in range(4):
            pltpu.make_async_copy(o_ref.at[0, 0], ot.at[i, pl.ds(slot * 192, 192)], recv.at[i * 4 + slot]).wait()

    def first(i, _):
        rs = pl.ds(pl.multiple_of(i * BLK, BLK), BLK)
        z = x_ref[rs, :].astype(F32) + dg(ot[i], wo[...], 0, 0) + b_out
        xh, inv = layer_stats(z)
        xh1[rs, :] = xh
        inv1[rs, :] = inv
        h1b[rs, :] = (xh * gain1 + shift1).astype(BF)
        return 0

    lax.fori_loop(0, 3, first, 0)
    h1t[...] = h1b[...].T
    for copy in loads_in:
        copy.wait()

    def up(n, _):
        cs = pl.ds(pl.multiple_of(n * BLK, BLK), BLK)
        j = n // 3
        low = pl.ds(pl.multiple_of((n % 3) * BLK, BLK), BLK)
        bias = jnp.where(j == 0, bias_ref[0:1, low], biasg_ref[jnp.maximum(j - 1, 0), 0:1, low])
        u = jnp.dot(h1b[...], wi[:, cs], preferred_element_type=F32) + bias
        cdf = 0.5 * (1.0 + lax.erf(u * (2.0 ** -0.5)))
        pdf = jnp.exp(-0.5 * u * u) * (1.0 / math.sqrt(2.0 * math.pi))
        gg[:, cs] = (u * cdf).astype(BF)
        gp[:, cs] = (cdf + u * pdf).astype(BF)
        return 0

    lax.fori_loop(0, 6, up, 0)
    b1[0].wait_recv()
    b2.start()
    lax.fori_loop(6, 12, up, 0)
    b2.wait_recv()
    b3.start()
    b1[1].wait_recv()
    loads_b = [pltpu.make_async_copy(wbg.at[j], wb.at[pl.ds(768 * (j + 1), 768)], local.at[9 + j]) for j in range(3)]
    loads_b[0].start()
    loads_b[1].start()
    b3.wait_recv()
    loads_b[2].start()
    load_b0.wait()
    for copy in loads_b:
        copy.wait()

    def down(n, _):
        cs = pl.ds(pl.multiple_of(n * BLK, BLK), BLK)
        z2[:, cs] = jnp.dot(gg[...], wb[:, cs], preferred_element_type=F32)
        return 0

    lax.fori_loop(0, 3, down, 0)

    def second_norm(i, sums):
        rs = pl.ds(pl.multiple_of(i * BLK, BLK), BLK)
        h1 = xh1[rs, :] * gain1 + shift1
        xh, inv = layer_stats(h1 + z2[rs, :] + b_back)
        out_ref[rs, :] = (xh * gain2 + shift2).astype(BF)
        cot = cot_ref[rs, :].astype(F32)
        dxh = cot * gain2
        dz = inv * (dxh - jnp.mean(dxh, axis=-1, keepdims=True) - xh * jnp.mean(dxh * xh, axis=-1, keepdims=True))
        dz2[rs, :] = dz
        dz2b[rs, :] = dz.astype(BF)
        return (
            sums[0] + jnp.sum(dz, axis=0, keepdims=True),
            sums[1] + jnp.sum(cot * xh, axis=0, keepdims=True),
            sums[2] + jnp.sum(cot, axis=0, keepdims=True),
        )

    zero = jnp.zeros((1, 768), F32)
    s3, s4, s5 = lax.fori_loop(0, 3, second_norm, (zero, zero, zero))
    small_ref[3:4, :] = s3
    small_ref[4:5, :] = s4
    small_ref[5:6, :] = s5
    dz2t[...] = dz2b[...].T

    def back(n, _):
        cs = pl.ds(pl.multiple_of(n * BLK, BLK), BLK)
        j = n // 3
        low = pl.ds(pl.multiple_of((n % 3) * BLK, BLK), BLK)
        g = gg[:, cs]
        g_ref[j, 768:1536, low] = jnp.dot(dz2t[...], g, preferred_element_type=F32).astype(BF)
        du = (dg(dz2b[...], wb[cs, :], 1, 1) * gp[:, cs].astype(F32)).astype(BF)
        gg[:, cs] = du
        small_ref[pl.ds(8 + j, 1), low] = jnp.sum(du.astype(F32), axis=0, keepdims=True)
        g_ref[j, 0:768, low] = jnp.dot(h1t[...], du, preferred_element_type=F32).astype(BF)
        return 0

    lax.fori_loop(0, 12, back, 0)

    def into_h(n, _):
        cs = pl.ds(pl.multiple_of(n * BLK, BLK), BLK)
        z2[:, cs] = dg(gg[...], wi[cs, :], 1, 1) + dz2[:, cs]
        return 0

    lax.fori_loop(0, 3, into_h, 0)

    def first_norm(i, sums):
        rs = pl.ds(pl.multiple_of(i * BLK, BLK), BLK)
        dh = z2[rs, :]
        xh = xh1[rs, :]
        dxh = dh * gain1
        dz = inv1[rs, :] * (dxh - jnp.mean(dxh, axis=-1, keepdims=True) - xh * jnp.mean(dxh * xh, axis=-1, keepdims=True))
        dz1_ref[rs, :] = dz
        dzb = dz.astype(BF)
        dz2b[rs, :] = dzb
        do_ref[i] = dg(wo[...], dzb, 1, 1).astype(BF)
        return (
            sums[0] + jnp.sum(dz, axis=0, keepdims=True),
            sums[1] + jnp.sum(dh * xh, axis=0, keepdims=True),
            sums[2] + jnp.sum(dh, axis=0, keepdims=True),
        )

    s0, s1, s2 = lax.fori_loop(0, 3, first_norm, (zero, zero, zero))
    small_ref[0:1, :] = s0
    small_ref[1:2, :] = s1
    small_ref[2:3, :] = s2
    for j in range(4):
        rows = pl.ds(192 * j, 192)
        acc = jnp.dot(ot[0, rows, :], dz2b[0:BLK, :], preferred_element_type=F32)
        acc += jnp.dot(ot[1, rows, :], dz2b[BLK : 2 * BLK, :], preferred_element_type=F32)
        acc += jnp.dot(ot[2, rows, :], dz2b[2 * BLK : 3 * BLK, :], preferred_element_type=F32)
        g_ref[j, 1536:1728, :] = acc.astype(BF)
    small_ref[6:8, :] = jnp.zeros((2, 768), F32)
    small_ref[12:16, :] = jnp.zeros((4, 768), F32)

    for cond, copy in pending:
        if cond is None:
            copy.wait_send()
        else:
            pl.when(cond)(copy.wait_send)
    for copy in b1 + [b2, b3]:
        copy.wait_send()


def split3(v):
    a = v.astype(BF).astype(F32)
    b = (v - a).astype(BF).astype(F32)
    return a, b, v - a - b


def k3(
    qkv_ref, seg_ref, o_ref, lse_ref, xab_ref, wt_ref, wpar_ref, do_in, dz1_ref,
    din_ref, dw_ref, db_ref,
    do_ref, dq_s, qa, ka, va, da, dk, dv, pab, sbuf, rcore, rmid, rhalf, hsum, send, recv, landed,
):
    length = 1024
    t, d, core, across, diag, side = where_am_i()
    y, c = t // 2, t % 2
    greet([{"tensor": core}, {"tensor": across}, {"tensor": diag}])
    pending = []
    peers = (t, core, across, diag)
    for i in range(3):
        middle, blk = block_of(t, i)
        for j, dev in enumerate(peers):
            src = do_in.at[i, pl.ds(192 * j, 192)]
            group = jnp.where(middle == 1, 2, j // 2)
            dst = do_ref.at[group, blk]
            sem = landed.at[group * 4 + blk]
            if j == 0:
                pltpu.make_async_copy(src, dst, sem).start()
                continue
            if j == 2:
                pl.when(middle == 0)(pltpu.make_async_copy(src, dst, sem).start)
                to, cond = across, middle == 1
            elif j == 1:
                to, cond = core, None
            else:
                to, cond = jnp.where(middle == 1, diag, core), None
            copy = pltpu.make_async_remote_copy(
                src_ref=src, dst_ref=dst, send_sem=send.at[i * 3 + j - 1], recv_sem=sem,
                device_id={"tensor": to}, device_id_type=MESH,
            )
            if cond is None:
                copy.start()
            else:
                pl.when(cond)(copy.start)
            pending.append((cond, copy))

    def attend_back(g, which):
        for blk in range(4):
            pltpu.make_async_copy(do_in.at[0, pl.ds(0, 192)], do_ref.at[g, blk], landed.at[g * 4 + blk]).wait()
        seg = seg_ref[which]
        row = lax.broadcasted_iota(jnp.int32, (64, length), 0)
        same = (row == seg).astype(F32)
        key_mark = jnp.where(row >= 8, 1.0, (same - 1.0) * BIG).astype(BF)

        def unit(h, _):
            r = pl.multiple_of(h * 64, 64)
            hs = pl.ds(r, 64)
            l1, l2, l3 = split3(-lse_ref[g * 3 + h])
            qa[0:64, :] = qkv_ref[g, hs, :]
            qa[64:128, :] = jnp.where(row == 8, l1, jnp.where(row == 9, l2, jnp.where(row == 10, l3, same))).astype(BF)
            ka[...] = jnp.concatenate([qkv_ref[g, pl.ds(r + 192, 64), :], key_mark], axis=0).T
            va[...] = jnp.concatenate([qkv_ref[g, pl.ds(r + 384, 64), :], jnp.ones((64, length), BF)], axis=0).T
            for b in range(4):
                bs = slice(b * BLK, (b + 1) * BLK)
                do = do_ref[g, b, hs, :]
                e1, e2, e3 = split3(-jnp.sum(do.astype(F32) * o_ref[g, b, hs, :].astype(F32), axis=0, keepdims=True))
                da[0:64, bs] = do
                rb = row[:, bs]
                da[64:128, bs] = jnp.where(rb == 8, e1, jnp.where(rb == 9, e2, jnp.where(rb == 10, e3, 0.0))).astype(BF)
            dk[...] = jnp.zeros_like(dk)
            dv[...] = jnp.zeros_like(dv)

            def chunk(n, _):
                cs = pl.ds(pl.multiple_of(n * 512, 512), 512)
                s = jnp.dot(ka[...], qa[:, cs], preferred_element_type=F32)
                p = jnp.exp2(s)
                dp = jnp.dot(va[...], da[:, cs], preferred_element_type=F32)
                pb = p.astype(BF)
                ds = (p * dp).astype(BF)
                dv[...] += dg(da[0:64, cs], pb, 1, 1)
                dk[...] += dg(qa[0:64, cs], ds, 1, 1)
                dq = jnp.dot(qkv_ref[g, pl.ds(r + 192, 64), :], ds, preferred_element_type=F32)
                dq_s[g, hs, cs] = (dq * (HEAD_DIM ** (-0.5))).astype(BF)
                return 0

            lax.fori_loop(0, length // 512, chunk, 0)
            dq_s[g, pl.ds(r + 192, 64), :] = (dk[...] * math.log(2.0)).astype(BF)
            dq_s[g, pl.ds(r + 384, 64), :] = dv[...].astype(BF)
            return 0

        lax.fori_loop(0, 3, unit, 0)

    own_seq = 2 * y
    attend_back(1, own_seq)
    dw_ref[1] = jnp.dot(dq_s[1], xab_ref[0], preferred_element_type=F32).astype(BF)
    attend_back(2, 1)
    attend_back(0, own_seq)
    dw_ref[0] = (
        jnp.dot(dq_s[0], xab_ref[0], preferred_element_type=F32) + jnp.dot(dq_s[2], xab_ref[1], preferred_element_type=F32)
    ).astype(BF)
    db_ref[0] = jnp.broadcast_to(
        jnp.sum(dq_s[0].astype(F32), axis=1, keepdims=True) + jnp.sum(dq_s[2].astype(F32), axis=1, keepdims=True), (576, 128)
    )
    db_ref[1] = jnp.broadcast_to(jnp.sum(dq_s[1].astype(F32), axis=1, keepdims=True), (576, 128))

    def into_x(n, _):
        cs = pl.ds(pl.multiple_of(n * BLK, BLK), BLK)
        ra = dg(dq_s[0, :, cs], wt_ref[...], 0, 0) + dg(dq_s[1, :, cs], wpar_ref[...], 0, 0)
        rb = dg(dq_s[2, :, cs], wt_ref[...], 0, 0)
        pab[0, cs, :] = ra
        pab[1, cs, :] = rb
        sbuf[0, cs, :] = ra.astype(BF)
        sbuf[1, cs, :] = rb.astype(BF)
        return 0

    lax.fori_loop(0, 4, into_x, 0)

    def rows_of(blk):
        return pl.ds(pl.multiple_of(blk * BLK, BLK), BLK)

    base = 9
    outs = []
    for i in range(3):
        middle, blk = block_of(core, i)
        outs.append(
            pltpu.make_async_remote_copy(
                src_ref=sbuf.at[middle, rows_of(blk)], dst_ref=rcore.at[i], send_sem=send.at[base + i],
                recv_sem=recv.at[i], device_id={"tensor": core}, device_id_type=MESH,
            )
        )
    far = 2 * (1 - y)
    outs.append(
        pltpu.make_async_remote_copy(
            src_ref=sbuf.at[1, rows_of(far + 1 - c)], dst_ref=rhalf, send_sem=send.at[base + 3],
            recv_sem=recv.at[3], device_id={"tensor": core}, device_id_type=MESH,
        )
    )
    for copy in reversed(outs):
        copy.start()
    outs[3].wait_recv()
    hsum[...] = (pab[1, rows_of(far + c), :] + rhalf[...].astype(F32)).astype(BF)
    hcopy = pltpu.make_async_remote_copy(
        src_ref=hsum, dst_ref=rmid.at[c], send_sem=send.at[base + 4], recv_sem=recv.at[4 + c],
        device_id={"tensor": 2 * (1 - y) + y}, device_id_type=MESH,
    )
    hcopy.start()
    for i in range(3):
        outs[i].wait_recv()
        middle, blk = block_of(t, i)
        rs = pl.ds(i * BLK, BLK)

        @pl.when(middle == 0)
        def _():
            din_ref[rs, :] = (dz1_ref[rs, :] + pab[0, rows_of(blk), :] + rcore[i].astype(F32)).astype(BF)

        @pl.when(middle == 1)
        def _():
            k = blk % 2
            pltpu.make_async_copy(hsum, rmid.at[k], recv.at[4 + k]).wait()
            din_ref[rs, :] = (
                dz1_ref[rs, :] + pab[1, rows_of(blk), :] + rcore[i].astype(F32) + rmid[k].astype(F32)
            ).astype(BF)

    for copy in outs + [hcopy]:
        copy.wait_send()
    for cond, copy in pending:
        if cond is None:
            copy.wait_send()
        else:
            pl.when(cond)(copy.wait_send)


def vm(*shape, dtype=BF):
    return pltpu.VMEM(shape, dtype)


def sds(*shape, dtype=BF):
    return jax.ShapeDtypeStruct(shape, dtype)


VM = pl.BlockSpec(memory_space=pltpu.VMEM)
ANY = pl.BlockSpec(memory_space=pl.ANY)


def params(cid):
    return pltpu.CompilerParams(collective_id=cid, has_side_effects=True, vmem_limit_bytes=62 * 2**20)


def local_step(
    layer_input, segment_ids, w_query, b_query, w_key, w_value, b_value, w_out, b_out, first_gain, first_shift,
    w_in, b_in, w_back, b_back, second_gain, second_shift, cotangent,
):
    seg = segment_ids.reshape(3, 1, 1024)
    wt = jnp.concatenate([w_query, w_key, w_value], axis=1).T
    zeros = jnp.zeros((192,), F32)
    bias = jnp.stack([b_in.astype(F32), jnp.concatenate([b_query.astype(F32), zeros, b_value.astype(F32), zeros])])
    bias = jnp.concatenate([bias, jnp.zeros((6, 768), F32)])
    vec = jnp.stack([b_out, first_gain, first_shift, b_back, second_gain, second_shift])
    vec = jnp.concatenate([vec, jnp.zeros((2, 768), F32)])
    dma = pltpu.SemaphoreType.DMA

    qkv, o, lse, xab, wpar, woutg, wing, biasg = pl.pallas_call(
        k1,
        out_shape=(
            sds(3, 576, 1024), sds(3, 4, 192, BLK), sds(9, 1, 1024, dtype=F32), sds(2, 1024, 768), sds(576, 768),
            sds(3, 192, 768), sds(3, 768, 768), sds(3, 8, 768, dtype=F32),
        ),
        in_specs=[ANY, ANY, VM, VM, ANY, ANY],
        out_specs=(VM, VM, VM, VM, VM, ANY, ANY, VM),
        scratch_shapes=[vm(576, 768), vm(128, 1024), vm(1024, 128), vm(80, 1024), dma((24,)), dma((24,)), dma((4,))],
        compiler_params=params(0),
        name="attention_forward",
    )(layer_input, wt, bias, seg, w_out, w_in)

    out, dz1, do, g, small, _ = pl.pallas_call(
        lambda *r: k2(*r[:16], *r[17:20], r[20], r[16], *r[21:]),
        out_shape=(
            sds(768, 768), sds(768, 768, dtype=F32), sds(3, 768, BLK), sds(4, 1728, 768), sds(16, 768, dtype=F32),
            sds(3, 768, 768),
        ),
        in_specs=[VM, VM, VM, VM, VM, ANY, ANY, ANY, ANY, ANY, ANY],
        out_specs=(VM, VM, VM, VM, VM, ANY),
        scratch_shapes=[
            vm(3, 768, BLK), vm(768, 768), vm(768, 3072), vm(3072, 768),
            vm(768, 768), vm(768, 768), vm(768, 768, dtype=F32), vm(768, 1, dtype=F32), vm(768, 3072), vm(768, 3072),
            vm(768, 768, dtype=F32), vm(768, 768), vm(768, 768), vm(768, 768, dtype=F32),
            dma((34,)), dma((34,)), dma((12,)),
        ],
        compiler_params=params(1),
        name="feed_forward",
    )(layer_input, cotangent, vec, bias, biasg, o, w_out, woutg, w_in, wing, w_back)

    din, dw, db = pl.pallas_call(
        k3,
        out_shape=(sds(768, 768), sds(2, 576, 768), sds(2, 576, 128, dtype=F32)),
        in_specs=[VM, VM, VM, VM, VM, VM, VM, ANY, VM],
        out_specs=(VM, VM, VM),
        scratch_shapes=[
            vm(3, 4, 192, BLK), vm(3, 576, 1024), vm(128, 1024), vm(1024, 128), vm(1024, 128), vm(128, 1024),
            vm(64, 1024, dtype=F32), vm(64, 1024, dtype=F32), vm(2, 1024, 768, dtype=F32), vm(2, 1024, 768),
            vm(3, BLK, 768), vm(2, BLK, 768), vm(BLK, 768), vm(BLK, 768), dma((14,)), dma((6,)), dma((12,)),
        ],
        compiler_params=params(2),
        name="attention_backward",
    )(qkv, seg, o, lse, xab, wt, wpar, do, dz1)

    def core_swap(v):
        return lax.ppermute(v, "tensor", [(0, 1), (1, 0), (2, 3), (3, 2)])

    def across_swap(v):
        return lax.ppermute(v, "tensor", [(0, 2), (2, 0), (1, 3), (3, 1)])

    bi = small[8:12]
    r1, r3 = core_swap(g[1]), core_swap(g[3])
    p2 = (g[2].astype(F32) + r3.astype(F32)).astype(BF)
    p0 = g[0].astype(F32) + r1.astype(F32) + across_swap(p2).astype(F32)
    pq = dw[0].astype(F32) + across_swap(dw[1]).astype(F32)
    bi0 = bi[0] + core_swap(bi[1])
    bi2 = bi[2] + core_swap(bi[3])
    bi = bi0 + across_swap(bi2)
    bq = db[0, :, 0] + across_swap(db[1, :, 0])
    big = lax.psum((p0.astype(BF), pq.astype(BF)), "dp")
    bi, bq = lax.psum((bi, bq), "dp")
    shared = lax.psum(small[0:6], ("dp", "tensor"))
    gw, gq = big
    gw = gw.astype(F32)
    gq = gq.astype(F32)
    return (
        out, din, gq[0:192].T, bq[0:192], gq[192:384].T, gq[384:576].T, bq[384:576], gw[1536:1728],
        shared[0], shared[1], shared[2], gw[0:768], bi, gw[768:1536].T, shared[3], shared[4], shared[5],
    )


def solution(mesh):
    rows = P(("dp", "tensor"), None)
    in_specs = (
        rows, P("dp", None), P(None, "tensor"), P("tensor"), P(None, "tensor"), P(None, "tensor"), P("tensor"),
        P("tensor", None), P(), P(), P(), P(None, "tensor"), P("tensor"), P("tensor", None), P(), P(), P(), rows,
    )
    out_specs = (
        rows, rows, P(None, "tensor"), P("tensor"), P(None, "tensor"), P(None, "tensor"), P("tensor"),
        P("tensor", None), P(), P(), P(), P(None, "tensor"), P("tensor"), P("tensor", None), P(), P(), P(),
    )
    return jax.shard_map(local_step, mesh=mesh, in_specs=in_specs, out_specs=out_specs, check_vma=False)
```

time: 800 us -> 476 us (0.59); the launches traced: 787 us -> 474 us
  waiting for transfers between devices: 379 us -> 96.2 us
  Pallas kernels: 0 us -> 249 us
  matrix products: 192 us -> 0 us
  other arithmetic: 86.4 us -> 16.9 us
  local copies, waits for them, and re-layouts: 47.8 us -> 26.7 us
    pallas_call x0 -> x3, Pallas kernels: none -> 249 us  [the longest x1 103 us: local_step(): pl.pallas_call(k3, out_shape=(sds(768, 768), sds(2, 576, 768), sds(2, 576...]
    dot_general x39 -> x0, matrix products: 192 us -> none  [the longest x1 26.2 us: local(): jnp.dot(rows_in, wide_in, preferred_element_type=jnp.float32)]
    reduce_scatter x4 -> x0, waiting for transfers between devices: 184 us -> none  [the longest x1 48.1 us: local(): lax.psum_scatter(ffn_term.astype(jnp.bfloat16), 'tensor', scatter_dimensi...]
    all_gather x4 -> x0, waiting for transfers between devices: 130 us -> none  [the longest x1 37.8 us: local(): full_rows = lax.all_gather(layer_input, 'tensor', axis=0, tiled=True)]
    reduce_sum x14 -> x0, other arithmetic: 39.8 us -> none  [the longest x3 21.9 us: attend_forward(): row_total = jnp.sum(exponent, axis=-1, keepdims=True)]
    ppermute x0 -> x8, waiting for transfers between devices: none -> 27.5 us  [the longest x4 22.9 us: across_swap(): return lax.ppermute(v, 'tensor', [(0, 2), (2, 0), (1, 3), (3, 1)])]
    convert_element_type x18 -> x7, other arithmetic: 40 us -> 14 us  [the longest x2 8.15 us: local_step(): big = lax.psum((p0.astype(BF), pq.astype(BF)), 'dp')]
    dynamic_slice x24 -> x0, local copies, waits for them, and re-layouts: 20.3 us -> none  [local(): lax.map(attend_forward, (by_sequence(query_rows), by_sequence(key_rows),...]
  transfers between devices with their start and end apart: 9 -> 9, of which waited for: 9 -> 4; matrix products, arithmetic and copies ran while one was open for 5% -> 2% of each run, Pallas kernels for 0% -> 22%
where the time goes in v1:
time: 476 us; the launch traced here: 474 us
  Pallas kernels  249 us (52%)
  waiting for transfers between devices  96.2 us (20%)
  blocking collectives  65.2 us (14%)
  local copies, waits for them, and re-layouts  26.7 us (6%)
  other arithmetic  16.9 us (4%)
  between operations  14.2 us (3%)
  starting transfers between devices  5.59 us (1%)
    pallas_call x1, Pallas kernels, local_step(): pl.pallas_call(k3, out_shape=(sds(768, 768), sds(2, 576, 768), sds(2, 576...  103 us
    pallas_call x1, Pallas kernels, local_step(): pl.pallas_call(lambda *r: k2(*r[:16], *r[17:20], r[20], r[16], *r[21:]),...  80.1 us
    psum x1, waiting for transfers between devices, local_step(): big = lax.psum((p0.astype(BF), pq.astype(BF)), 'dp')  68.7 us
    pallas_call x1, Pallas kernels, local_step(): pl.pallas_call(k1, out_shape=(sds(3, 576, 1024), sds(3, 4, 192, BLK), sds...  66.3 us
    psum x1, blocking collectives, local_step(): shared = lax.psum(small[0:6], ('dp', 'tensor'))  44.7 us
    ppermute x4, waiting for transfers between devices, across_swap(): return lax.ppermute(v, 'tensor', [(0, 2), (2, 0), (1, 3), (3, 1)])  22.9 us
    psum x1, blocking collectives, local_step(): bi, bq = lax.psum((bi, bq), 'dp')  20.5 us
  transfers between devices with their start and end apart: 9, of which 4 were waited for; matrix products, arithmetic and copies ran while one was open for 2% of the time, Pallas kernels for 22%

profile of v1, /device:TPU:4, one launch (start us, length us, event | category | flops | bytes accessed | tf_op | source)
XLA Modules:
  0.0 473.8 jit_solution(2420598610104774990)
XLA Ops:
  13.5 1.3 reshape.43.seg_ref
  15.5 2.1 maximum_bitcast_fusion.wt_ref
  17.7 66.3 %attention_forward.1 = (bf16[3,576,1024]{2,1,0:T(8,128)(2,1)}, bf16[3,4,192,256]{3,2,1,0:T(8,128)(2,1)}, f32[9,1,1024]{2,1,0:T(1,128)}, bf16[2,1024,768]{2,1,0:T...) custom-call(bf16[768,768]{1,0:T(8,128)(2,1)} %r_0_.1, ...), custom_call_target="tpu_custom_call" | custom-call | tf_op jit(solution)/shard_map/attention_forward/pallas_call | solution.py:618
  84.7 80.1 %feed_forward.1 = (bf16[768,768]{1,0:T(8,128)(2,1)}, f32[768,768]{1,0:T(8,128)}, bf16[3,768,256]{2,1,0:T(8,128)(2,1)}, bf16[4,1728,768]{2,1,0:T(8,128)(2,1)}, f3...) custom-call(bf16[768,768]{1,0:T(8,128)(2,1)} %r_0_.1, bf16[768,768]{1,0:T(8,128)(2,1)} %r_1_.1, f32[8,768]{1,0:T(8,128)} %concatenate.12.r_2_, ...), custom_call_target="tpu_custom_call" | custom-call | tf_op jit(solution)/shard_map/feed_forward/pallas_call | solution.py:631
  164.7 4.5 slice_bitcast_fusion.1
  169.2 1.5 collective-permute-start.3
  170.7 4.6 collective-permute-done.3
  175.3 4.0 fusion
  179.4 1.5 collective-permute-start.4
  180.9 102.7 %attention_backward.1 = (bf16[768,768]{1,0:T(8,128)(2,1)}, bf16[2,576,768]{2,1,0:T(8,128)(2,1)}, f32[2,576,128]{2,1,0:T(8,128)}) custom-call(bf16[3,576,1024]{2,1,0:T(8,128)(2,1)} %get-tuple-element.38.qkv_ref, s32[3,1,1024]{2,1,0:T(1,128)} %reshape.43.seg_ref, bf16[3,4,192,256]{3,2,1,0:T(8,128)(2,1)} %get-tuple-element.34.r_5_.o_ref, ...), custom_call_target="tpu_custom_call" | custom-call | tf_op jit(solution)/shard_map/attention_backward/pallas_call | solution.py:649
  283.6 1.2 slice_bitcast_fusion.3
  284.9 20.0 %collective-permute-done = bf16[576,768]{1,0:T(8,128)(2,1)S(1)} collective-permute-done((bf16[576,768]{1,0:T(8,128)(2,1)S(1)}, bf16[576,768]{1,0:T(8,128)(2,1)S(1)}, u32[]{:S(2)}, u32[]{:S(2)}) %collective-permute-start) | collective-permute-done | bytes 884768 | tf_op jit(solution)/shard_map/ppermute | solution.py:667
  304.8 2.3 fusion.3
  307.2 5.8 %fusion.2 = bf16[1728,768]{1,0:T(8,128)(2,1)} fusion(bf16[1728,768]{1,0:T(8,128)(2,1)} %collective-permute-done.4, bf16[1728,768]{1,0:T(8,128)(2,1)} %collective-permute-done.2, bf16[4,1728,768]{2,1,0:T(8,128)(2,1)} %get-tuple-element.47), kind=kLoop, calls=%fused_computation.4 | loop fusion | flops 7962624 | bytes 10616832 | tf_op jit(solution)/shard_map/convert_element_type | solution.py:678
  313.0 1.0 copy-done.4
  314.3 1.8 collective-permute-start.1
  316.7 44.7 %psum.38 = f32[6,768]{1,0:T(8,128)S(1)} all-reduce(f32[6,768]{1,0:T(8,128)S(1)} %slice.100), channel_id=1, replica_groups=mesh['dp'=8,'tensor'=4] {'dp','tensor'}, use_global_device_ids=true, to_apply=%region_3.0 | all-reduce | flops 4608 | bytes 36864 | tf_op jit(solution)/shard_map/psum | solution.py:680
  362.1 2.9 collective-permute-done.7
  365.1 20.5 %all-reduce = (f32[576]{0:T(1024)S(1)}, f32[768]{0:T(1024)}) all-reduce(f32[576]{0:T(1024)S(1)} %add.35, f32[768]{0:T(1024)S(1)} %add_add_fusion), channel_id=1, replica_groups=mesh['dp'=8,'tensor'=4] {'dp'}, use_global_device_ids=true, to_apply=%region_1.0 | all-reduce | flops 1344 | bytes 10752 | tf_op jit(solution)/shard_map/psum | solution.py:679
  386.2 68.7 %all-reduce.4.cloned.1.call-done = (bf16[576,768]{1,0:T(8,128)(2,1)}, bf16[1728,768]{1,0:T(8,128)(2,1)}) async-done(((bf16[576,768]{1,0:T(8,128)(2,1)}, bf16[1728,768]{1,0:T(8,128)(2,1)}), (bf16[576,768]{1,0:T(8,128)(2,1)}, bf16[1728,768]{1,0:T(8,128)(2,1)})) %all-reduce.4.cloned.1.call-update) | async-done | bytes 3538960 | tf_op jit(solution)/shard_map/psum | solution.py:678
  454.8 1.8 slice.116
  456.6 3.0 slice.120
  460.9 1.2 slice_bitcast_fusion.4
  462.3 2.0 copy.36
  (53 shorter events, 14.1 us)
Async XLA Ops:
  7.2 447.6 %all-reduce.4.cloned.1.call-start = ((), (), s32[]{:S(2)}) async-start(), calls=%async_computation | async-start | bytes 7077888 | tf_op jit(solution)/shard_map/psum | solution.py:678
  169.2 6.1 %collective-permute-start.3 = (bf16[1728,768]{1,0:T(8,128)(2,1)S(1)}, bf16[1728,768]{1,0:T(8,128)(2,1)S(1)}, u32[]{:S(2)}, u32[]{:S(2)}) collective-permute-start(bf16[1728,768]{1,0:T(8,128)(2,1)S(1)} %get-tuple-element.100), channel_id=1, source_target_pairs={{0,1},{1,0},{2,3},{3,2},{4,5},{5,4},{6,7},{7,6},{8,9},{9,8},{10,11... | collective-permute-start | bytes 7962632 | tf_op jit(solution)/shard_map/ppermute | solution.py:664
  170.7 136.4 %collective-permute-start.2 = (bf16[1728,768]{1,0:T(8,128)(2,1)}, bf16[1728,768]{1,0:T(8,128)(2,1)}, u32[]{:S(2)}, u32[]{:S(2)}) collective-permute-start(bf16[1728,768]{1,0:T(8,128)(2,1)} %get-tuple-element.99), channel_id=1, source_target_pairs={{0,1},{1,0},{2,3},{3,2},{4,5},{5,4},{6,7},{7,6},{8,9},{9,8},{10,11... | collective-permute-start | bytes 7962632 | tf_op jit(solution)/shard_map/ppermute | solution.py:664
  179.4 127.8 %collective-permute-start.4 = (bf16[1728,768]{1,0:T(8,128)(2,1)}, bf16[1728,768]{1,0:T(8,128)(2,1)}, u32[]{:S(2)}, u32[]{:S(2)}) collective-permute-start(bf16[1728,768]{1,0:T(8,128)(2,1)} %fusion), channel_id=1, source_target_pairs={{0,2},{2,0},{1,3},{3,1},{4,6},{6,4},{5,7},{7,5},{8,10},{10,8},{9,1... | collective-permute-start | bytes 7962632 | tf_op jit(solution)/shard_map/ppermute | solution.py:667
  284.8 20.0 %collective-permute-start = (bf16[576,768]{1,0:T(8,128)(2,1)S(1)}, bf16[576,768]{1,0:T(8,128)(2,1)S(1)}, u32[]{:S(2)}, u32[]{:S(2)}) collective-permute-start(bf16[576,768]{1,0:T(8,128)(2,1)S(1)} %slice_bitcast_fusion.3), channel_id=1, source_target_pairs={{0,2},{2,0},{1,3},{3,1},{4,6},{6,4},{5,7},{7,5},{8,10},{10,8},{9,1... | collective-permute-start | bytes 2654216 | tf_op jit(solution)/shard_map/ppermute | solution.py:667
  313.0 1.1 copy-start.4
  313.0 3.1 copy-start.5
  314.3 47.8 %collective-permute-start.1 = (f32[576]{0:T(1024)S(1)}, f32[576]{0:T(1024)S(1)}, u32[]{:S(2)}, u32[]{:S(2)}) collective-permute-start(f32[576]{0:T(1024)S(1)} %get-tuple-element.83), channel_id=1, source_target_pairs={{0,2},{2,0},{1,3},{3,1},{4,6},{6,4},{5,7},{7,5},{8,10},{10,8},{9,1... | collective-permute-start | bytes 6920 | tf_op jit(solution)/shard_map/ppermute | solution.py:667
  316.1 46.0 %collective-permute-start.5 = (f32[768]{0:T(1024)S(1)}, f32[768]{0:T(1024)S(1)}, u32[]{:S(2)}, u32[]{:S(2)}) collective-permute-start(f32[768]{0:T(1024)S(1)} %get-tuple-element.85), channel_id=1, source_target_pairs={{0,1},{1,0},{2,3},{3,2},{4,5},{5,4},{6,7},{7,6},{8,9},{9,8},{10,11... | collective-permute-start | bytes 9224 | tf_op jit(solution)/shard_map/ppermute | solution.py:664
  316.2 45.2 %collective-permute-start.6 = (f32[768]{0:T(1024)S(1)}, f32[768]{0:T(1024)S(1)}, u32[]{:S(2)}, u32[]{:S(2)}) collective-permute-start(f32[768]{0:T(1024)S(1)} %get-tuple-element.86), channel_id=1, source_target_pairs={{0,1},{1,0},{2,3},{3,2},{4,5},{5,4},{6,7},{7,6},{8,9},{9,8},{10,11... | collective-permute-start | bytes 9224 | tf_op jit(solution)/shard_map/ppermute | solution.py:664
  361.4 3.7 collective-permute-start.7
  456.6 3.0 copy-start
  459.6 1.2 copy-start.3
  462.3 2.0 copy-start.1
  464.3 1.7 copy-start.2
Sparse Core Ops, SparseCore 0:
  313.1 141.6 all-reduce.3

commit v2 on v1

v2 whole, which is shorter than its diff:
```python
import math
from functools import partial

import jax
import jax.numpy as jnp
from jax import lax
from jax.experimental import pallas as pl
from jax.experimental.pallas import tpu as pltpu
from jax.sharding import PartitionSpec as P

F32 = jnp.float32
BF = jnp.bfloat16
MESH = pl.DeviceIdType.MESH
HEAD_DIM = 64
EPSILON = 1e-05
BIG = 1e30
LOG2E = 1.0 / math.log(2.0)
QSCALE = HEAD_DIM ** (-0.5) * LOG2E
BLK = 256
IN_EARLY = 1
Y_EARLY = 1
UNIT_STEPS = {
    2: (("after_x", 0),),
    3: (("after_y", 2),),
    4: (("after_x", 1), ("after_end", 0)),
    6: (("after_y", 3), ("after_x", 2), ("after_end", 1), ("after_mate", 0)),
    8: (("after_y", 4), ("after_x", 3), ("after_end", 2), ("after_mate", 1)),
}
TAIL_INPUT = 7
TAIL_STEPS = (
    ("after_y", "p5"), ("after_x", "p4"), ("after_end", "p3"), ("after_mate", "p2"),
    ("after_y", "w0"), ("after_x", "p5"), ("after_end", "p4"), ("after_mate", "p3"),
    ("after_y", "w1"), ("after_x", "w0"), ("after_end", "p5"), ("after_mate", "p4"),
    ("after_y", "w2"), ("after_x", "w1"), ("after_end", "w0"), ("after_mate", "p5"),
    ("after_y", "w3"), ("after_y", "t"), ("after_x", "w2"), ("after_end", "w1"), ("after_mate", "w0"),
    ("after_x", "w3"), ("after_x", "t"), ("after_end", "w2"), ("after_mate", "w1"),
    ("after_end", "w3"), ("after_end", "t"), ("after_mate", "w2"),
    ("after_mate", "w3"), ("after_mate", "t"),
)


def dg(a, b, ca, cb):
    return lax.dot_general(a, b, (((ca,), (cb,)), ((), ())), preferred_element_type=F32)


def where_am_i():
    t = lax.axis_index("tensor")
    d = lax.axis_index("dp")
    core = t + 1 - 2 * (t % 2)
    across = (t + 2) % 4
    diag = 3 - t
    side = d + 1 - 2 * (d % 2)
    return t, d, core, across, diag, side


def block_of(t, i):
    b = 3 * t + i
    middle = (b // 4) % 2
    return middle, b % 4


def greet(devices):
    barrier = pltpu.get_barrier_semaphore()
    for dev in devices:
        pl.semaphore_signal(barrier, inc=1, device_id=dev, device_id_type=MESH)
    pl.semaphore_wait(barrier, len(devices))


def half_rows(half, total, pieces, i):
    n = total // 2 // pieces
    return pl.ds(pl.multiple_of(half * (total // 2) + i * n, n), n)


class Copies:
    def __init__(self, send, recv):
        self.send, self.recv, self.used = send, recv, 0

    def new(self, src, dst, **device):
        k = self.used
        self.used += 1
        return pltpu.make_async_remote_copy(
            src_ref=src,
            dst_ref=dst,
            send_sem=self.send.at[k],
            recv_sem=self.recv.at[k],
            device_id=device,
            device_id_type=MESH,
        )


def start_all(copies):
    for copy in copies:
        copy.start()


def k1(
    x_ref, wt_ref, bias_ref, seg_ref, wout_ref, win_ref,
    qkv_out, o_out, lse_ref, xab_out, wpar_out, woutg_ref, wing_ref, biasg_ref,
    qkv, o_v, xab, w_v, bcol, qa, ka, va, send, recv, local,
):
    length = 1024
    t, d, core, across, diag, side = where_am_i()
    y, c = t // 2, t % 2
    half = d % 2
    greet([{"tensor": core}, {"tensor": across}, {"tensor": diag}, {"dp": side}])
    cp = Copies(send, recv)
    rows_out, rows_local = [], []
    for i in range(3):
        middle, blk = block_of(t, i)
        src = x_ref.at[pl.ds(i * BLK, BLK)]
        dst = xab.at[middle, pl.ds(pl.multiple_of(blk * BLK, BLK), BLK)]
        rows_local.append(pltpu.make_async_copy(src, dst, local.at[i]))
        rows_out.append(cp.new(src, dst, tensor=core))
    w_local = pltpu.make_async_copy(wt_ref, w_v.at[0], local.at[3])
    cross_in = 2 * (1 - y) + c
    cross_slot = pl.ds(pl.multiple_of(cross_in * BLK, BLK), BLK)
    mixed = (t == 1) | (t == 2)
    first_middle = jnp.where(t == 1, 1, 0)
    cross_out = []
    base = cp.used
    for k in range(2):
        src = x_ref.at[pl.ds(pl.multiple_of((first_middle + k) * BLK, BLK), BLK)]
        dst = xab.at[1, pl.ds(pl.multiple_of((2 * y + k) * BLK, BLK), BLK)]
        cross_out.append(
            pltpu.make_async_remote_copy(
                src_ref=src, dst_ref=dst, send_sem=send.at[base + k], recv_sem=recv.at[base],
                device_id={"tensor": 2 * (1 - y) + k}, device_id_type=MESH,
            )
        )
    cp.used += 2
    cross_arrived = pltpu.make_async_remote_copy(
        src_ref=x_ref.at[pl.ds(0, BLK)], dst_ref=xab.at[1, cross_slot], send_sem=send.at[base],
        recv_sem=recv.at[base], device_id={"tensor": core}, device_id_type=MESH,
    )
    cross_forward = cp.new(xab.at[1, cross_slot], xab.at[1, cross_slot], tensor=core)
    wp_first, wp_second = [], []
    for i in range(3):
        part = half_rows(half, 576, 3, i)
        wp_first.append(cp.new(wt_ref.at[part], w_v.at[1, part], tensor=across))
        wp_second.append(cp.new(w_v.at[1, part], w_v.at[1, part], dp=side))
    bias_out = [
        cp.new(bias_ref, biasg_ref.at[0], tensor=core),
        cp.new(bias_ref, biasg_ref.at[1], tensor=across),
        cp.new(bias_ref, biasg_ref.at[2], tensor=diag),
    ]
    part = half_rows(half, 192, 1, 0)
    wo_first = cp.new(wout_ref.at[part], woutg_ref.at[1, part], tensor=across)
    wo_second = cp.new(woutg_ref.at[1, part], woutg_ref.at[1, part], dp=side)
    wo_core = cp.new(wout_ref, woutg_ref.at[0], tensor=core)
    wo_diag = cp.new(woutg_ref.at[1], woutg_ref.at[2], tensor=core)
    wi_first, wi_second, wi_diag = [], [], []
    for i in range(IN_EARLY):
        part = half_rows(half, 768, 3, i)
        wi_first.append(cp.new(win_ref.at[part], wing_ref.at[0, part], tensor=across))
        wi_second.append(cp.new(wing_ref.at[0, part], wing_ref.at[0, part], dp=side))
        for h in range(2):
            both = half_rows(h, 768, 3, i)
            wi_diag.append(cp.new(wing_ref.at[0, both], wing_ref.at[1, both], tensor=core))

    start_all(rows_local + [w_local] + rows_out)
    start_all(bias_out)

    @pl.when(mixed)
    def _():
        start_all(cross_out)

    start_all(wp_first)
    start_all([wo_core, wo_first] + wi_first)

    row64 = lax.broadcasted_iota(jnp.int32, (64, length), 0)
    va[64:80, :] = jnp.ones((16, length), BF)
    factor = jnp.where(lax.broadcasted_iota(jnp.int32, (576, 1), 0) % 192 < 64, QSCALE, 1.0)

    def outgoing(g):
        return [
            pltpu.make_async_copy(qkv.at[g], qkv_out.at[g], local.at[4 + 2 * (g % 3)]),
            pltpu.make_async_copy(o_v.at[g], o_out.at[g], local.at[5 + 2 * (g % 3)]),
        ]

    def at(u, k, copies_recv, copies_start=()):
        @pl.when(u == k)
        def _():
            for copy in copies_recv:
                copy.wait_recv()
            start_all(copies_start)

    def unit(u, _):
        g = (2 * (u // 3)) % 3
        h = u % 3
        par = jnp.where(g == 1, 1, 0)
        middle = jnp.where(g == 2, 1, 0)

        @pl.when(u == 3)
        def _():
            cross_arrived.wait_recv()
            cross_forward.start()
            cross_forward.wait_recv()

        at(u, 4, [wp_first[0]], [wp_second[0]])
        at(u, 5, [wp_first[1]], [wp_second[1]])
        at(u, 6, [wp_first[2]], [wp_second[2]])
        at(u, 6, wp_second + [bias_out[1]])
        at(u, 8, [wo_first], [wo_second])

        @pl.when(h == 0)
        def _():
            @pl.when(u > 0)
            def _():
                start_all(outgoing(jnp.where(g == 2, 0, 2)))

            @pl.when(par == 0)
            def _():
                bcol[...] = jnp.transpose(bias_ref[...])[0:576, 1:2]

            @pl.when(par == 1)
            def _():
                bcol[...] = jnp.transpose(biasg_ref[1])[0:576, 1:2]

            col = bcol[...]

            def body(n, _):
                cs = pl.ds(pl.multiple_of(n * BLK, BLK), BLK)
                r = (dg(w_v[par], xab[middle, cs, :], 1, 1) + col) * factor
                for k in range(3):
                    qkv[g, k, :, cs] = r[192 * k : 192 * (k + 1)].astype(BF)
                return 0

            lax.fori_loop(0, length // BLK, body, 0)
            same = (row64 == seg_ref[jnp.where(g == 2, 1, 2 * y)]).astype(F32)
            qa[64:128, :] = same.astype(BF)
            ka[64:128, :] = ((same - 1.0) * BIG).astype(BF)

        qa[0:64, :] = qkv[g, h, 0:64, :]
        ka[0:64, :] = qkv[g, h, 64:128, :]
        va[0:64, :] = qkv[g, h, 128:192, :]
        s = jnp.dot(ka[...].T, qa[...], preferred_element_type=F32)
        m = jnp.max(s, axis=0, keepdims=True)
        p = jnp.exp2(s - m).astype(BF)
        o = jnp.dot(va[...], p, preferred_element_type=F32)
        total = o[64:65, :]
        res = (o[0:64] * (1.0 / total)).astype(BF)
        hs = pl.ds(pl.multiple_of(h * 64, 64), 64)
        for b in range(4):
            o_v[g, b, hs, :] = res[:, b * BLK : (b + 1) * BLK]
        lse_ref[g * 3 + h] = m + jnp.log2(total)
        return 0

    for copy in rows_local + [w_local]:
        copy.wait()
    for copy in rows_out:
        copy.wait_recv()
    lax.fori_loop(0, 9, unit, 0)
    tail = outgoing(1)
    tail.append(pltpu.make_async_copy(xab, xab_out, local.at[0]))
    tail.append(pltpu.make_async_copy(w_v.at[1], wpar_out, local.at[1]))
    start_all(tail)
    for i in range(IN_EARLY):
        wi_first[i].wait_recv()
        wi_second[i].start()
    wo_second.wait_recv()
    wo_diag.start()
    for i in range(IN_EARLY):
        wi_second[i].wait_recv()
        start_all(wi_diag[2 * i : 2 * i + 2])
    for copy in [bias_out[0], bias_out[2], wo_core, wo_diag] + wi_diag:
        copy.wait_recv()
    for copy in outgoing(0) + outgoing(2) + tail:
        copy.wait()
    sent = rows_out + [cross_forward] + wp_first + wp_second + bias_out + [wo_first, wo_second, wo_core, wo_diag]
    for copy in sent + wi_first + wi_second + wi_diag:
        copy.wait_send()

    @pl.when(mixed)
    def _():
        for copy in cross_out:
            copy.wait_send()

def layer_stats(z):
    mean = jnp.mean(z, axis=-1, keepdims=True)
    cen = z - mean
    var = jnp.mean(cen * cen, axis=-1, keepdims=True)
    inv = lax.rsqrt(var + EPSILON)
    return cen * inv, inv


def k2(
    x_ref, cot_ref, vec_ref, bias_ref, biasg_ref, o_ref, wout_ref, woutg_ref, win_ref, wing_ref, wback_ref,
    out_ref, dz1_ref, do_ref, gf_ref, go_ref, small_ref,
    ot, wo, wi, wb, h1b, h1t, xh1, inv1, gg, gp, z2, dz2b, dz2t, gsend, rc, ry, send, recv, local,
):
    t, d, core, across, diag, side = where_am_i()
    half = d % 2
    greet([{"tensor": core}, {"tensor": across}, {"tensor": diag}, {"dp": side}])

    peers = (t, core, across, diag)
    pending = []
    for j, dev in enumerate(peers):
        for i in range(3):
            middle, blk = block_of(dev, i)
            for second in (False, True) if j < 2 else (False,):
                slot = j + 2 if second else j
                src = o_ref.at[1 if second else 2 * middle, blk]
                dst = ot.at[i, pl.ds(slot * 192, 192)]
                sem = recv.at[i * 4 + slot]
                if j == 0:
                    copy = pltpu.make_async_copy(src, dst, sem)
                else:
                    k = 3 * (j - 1) + i if not second else 9 + i
                    copy = pltpu.make_async_remote_copy(
                        src_ref=src, dst_ref=dst, send_sem=send.at[k], recv_sem=sem,
                        device_id={"tensor": dev}, device_id_type=MESH,
                    )
                if second:
                    cond = middle == 0
                else:
                    cond = None if j < 2 else middle == 1
                if cond is None:
                    copy.start()
                else:
                    pl.when(cond)(copy.start)
                if j:
                    pending.append((cond, copy))
    cp = Copies(send, recv)
    cp.used = 12

    def lanes(j):
        return pl.ds(768 * j, 768)

    in_core = cp.new(win_ref, wi.at[:, lanes(1)], tensor=core)
    in_first, in_second, in_diag, loads_in = [], [], [], [pltpu.make_async_copy(win_ref, wi.at[:, lanes(0)], local.at[4])]
    for i in range(IN_EARLY, 3):
        part = half_rows(half, 768, 3, i)
        in_first.append(cp.new(win_ref.at[part], wi.at[part, lanes(2)], tensor=across))
        in_second.append(cp.new(wi.at[part, lanes(2)], wi.at[part, lanes(2)], dp=side))
        for h in range(2):
            both = half_rows(h, 768, 3, i)
            in_diag.append(cp.new(wi.at[both, lanes(2)], wi.at[both, lanes(3)], tensor=core))
    for i in range(IN_EARLY):
        for h in range(2):
            part = half_rows(h, 768, 3, i)
            for k in range(2):
                loads_in.append(pltpu.make_async_copy(wing_ref.at[k, part], wi.at[part, lanes(2 + k)], local.at[4 + len(loads_in)]))
    back_core = cp.new(wback_ref, wb.at[lanes(1)], tensor=core)
    back_first, back_second, back_diag = [], [], []
    for i in range(3):
        part = half_rows(half, 768, 3, i)
        place = half_rows(half, 768, 3, i)
        place = pl.ds(place.start + 2 * 768, place.size)
        back_first.append(cp.new(wback_ref.at[part], wb.at[place], tensor=across))
        back_second.append(cp.new(wb.at[place], wb.at[place], dp=side))
        for h in range(2):
            n = h * 384 + i * 128
            back_diag.append(cp.new(wb.at[pl.ds(2 * 768 + n, 128)], wb.at[pl.ds(3 * 768 + n, 128)], tensor=core))
    load_b0 = pltpu.make_async_copy(wback_ref, wb.at[lanes(0)], local.at[4 + len(loads_in)])
    start_all(in_first + [in_core, back_core] + back_first)
    loads = [pltpu.make_async_copy(wout_ref, wo.at[pl.ds(0, 192)], local.at[0])]
    loads += [pltpu.make_async_copy(woutg_ref.at[j], wo.at[pl.ds(192 * (j + 1), 192)], local.at[j + 1]) for j in range(3)]
    start_all(loads + loads_in + [load_b0])

    b_out, gain1, shift1, b_back, gain2, shift2 = [vec_ref[k : k + 1, :] for k in range(6)]
    for copy in loads:
        copy.wait()
    for i in range(3):
        for slot in range(4):
            pltpu.make_async_copy(o_ref.at[0, 0], ot.at[i, pl.ds(slot * 192, 192)], recv.at[i * 4 + slot]).wait()

    def first(i, _):
        rs = pl.ds(pl.multiple_of(i * BLK, BLK), BLK)
        z = x_ref[rs, :].astype(F32) + dg(ot[i], wo[...], 0, 0) + b_out
        xh, inv = layer_stats(z)
        xh1[rs, :] = xh
        inv1[rs, :] = inv
        h1b[rs, :] = (xh * gain1 + shift1).astype(BF)
        return 0

    lax.fori_loop(0, 3, first, 0)
    h1t[...] = h1b[...].T
    for copy in loads_in:
        copy.wait()

    def at(n, k, copies_recv, copies_start=()):
        @pl.when(n == k)
        def _():
            for copy in copies_recv:
                copy.wait_recv()
            start_all(copies_start)

    late = len(in_first)

    def up(n, _):
        at(n, 2, in_first[:1], in_second[:1])
        at(n, 3, [in_core])
        if late > 1:
            at(n, 4, in_first[1:], in_second[1:])
        at(n, 6, in_second, in_diag)
        at(n, 7, [back_first[0]], [back_second[0]])
        at(n, 9, in_diag)
        at(n, 9, [back_first[1]], [back_second[1]])
        at(n, 11, [back_first[2]], [back_second[2]])
        cs = pl.ds(pl.multiple_of(n * BLK, BLK), BLK)
        j = n // 3
        low = pl.ds(pl.multiple_of((n % 3) * BLK, BLK), BLK)
        bias = jnp.where(j == 0, bias_ref[0:1, low], biasg_ref[jnp.maximum(j - 1, 0), 0:1, low])
        u = jnp.dot(h1b[...], wi[:, cs], preferred_element_type=F32) + bias
        cdf = 0.5 * (1.0 + lax.erf(u * (2.0 ** -0.5)))
        pdf = jnp.exp(-0.5 * u * u) * (1.0 / math.sqrt(2.0 * math.pi))
        gg[:, cs] = (u * cdf).astype(BF)
        gp[:, cs] = (cdf + u * pdf).astype(BF)
        return 0

    lax.fori_loop(0, 12, up, 0)
    for i in range(3):
        back_second[i].wait_recv()
        start_all(back_diag[2 * i : 2 * i + 2])
    back_core.wait_recv()
    load_b0.wait()
    for copy in back_diag:
        copy.wait_recv()

    def down(n, _):
        cs = pl.ds(pl.multiple_of(n * BLK, BLK), BLK)
        z2[:, cs] = jnp.dot(gg[...], wb[:, cs], preferred_element_type=F32)
        return 0

    lax.fori_loop(0, 3, down, 0)

    def second_norm(i, sums):
        rs = pl.ds(pl.multiple_of(i * BLK, BLK), BLK)
        h1 = xh1[rs, :] * gain1 + shift1
        xh, inv = layer_stats(h1 + z2[rs, :] + b_back)
        out_ref[rs, :] = (xh * gain2 + shift2).astype(BF)
        cot = cot_ref[rs, :].astype(F32)
        dxh = cot * gain2
        dz = inv * (dxh - jnp.mean(dxh, axis=-1, keepdims=True) - xh * jnp.mean(dxh * xh, axis=-1, keepdims=True))
        z2[rs, :] = dz
        dz2b[rs, :] = dz.astype(BF)
        return (
            sums[0] + jnp.sum(dz, axis=0, keepdims=True),
            sums[1] + jnp.sum(cot * xh, axis=0, keepdims=True),
            sums[2] + jnp.sum(cot, axis=0, keepdims=True),
        )

    zero = jnp.zeros((1, 768), F32)
    s3, s4, s5 = lax.fori_loop(0, 3, second_norm, (zero, zero, zero))
    small_ref[3:4, :] = s3
    small_ref[4:5, :] = s4
    small_ref[5:6, :] = s5
    dz2t[...] = dz2b[...].T

    base = cp.used

    def to_core(stage, ch):
        k = base + stage * 3 + ch
        return pltpu.make_async_remote_copy(
            src_ref=gsend.at[stage, ch], dst_ref=rc.at[stage, ch], send_sem=send.at[k], recv_sem=recv.at[k],
            device_id={"tensor": core}, device_id_type=MESH,
        )

    def to_across(ch):
        k = base + 6 + ch
        return pltpu.make_async_remote_copy(
            src_ref=gf_ref.at[1, ch], dst_ref=ry.at[ch], send_sem=send.at[k], recv_sem=recv.at[k],
            device_id={"tensor": across}, device_id_type=MESH,
        )

    def back(m, _):
        stage = m // 6
        ch = (m % 6) // 2
        slot = 3 - 2 * stage - m % 2
        n = slot * 3 + ch
        cs = pl.ds(pl.multiple_of(n * BLK, BLK), BLK)
        low = pl.ds(pl.multiple_of(ch * BLK, BLK), BLK)
        g_back = jnp.dot(dz2t[...], gg[:, cs], preferred_element_type=F32)
        du = (dg(dz2b[...], wb[cs, :], 1, 1) * gp[:, cs].astype(F32)).astype(BF)
        gg[:, cs] = du
        small_ref[pl.ds(8 + slot, 1), low] = jnp.sum(du.astype(F32), axis=0, keepdims=True)
        g_in = jnp.dot(h1t[...], du, preferred_element_type=F32)

        @pl.when(m % 2 == 0)
        def _():
            gsend[stage, ch, 0] = g_in.astype(BF)
            gsend[stage, ch, 1] = g_back.astype(BF)
            to_core(stage, ch).start()

        @pl.when(m % 2 == 1)
        def _():
            to_core(stage, ch).wait_recv()
            gf_ref[1 - stage, ch, 0] = (g_in + rc[stage, ch, 0].astype(F32)).astype(BF)
            gf_ref[1 - stage, ch, 1] = (g_back + rc[stage, ch, 1].astype(F32)).astype(BF)
            pl.when((stage == 0) & (ch < Y_EARLY))(to_across(ch).start)

        return 0

    lax.fori_loop(0, 12, back, 0)

    def into_h(n, _):
        cs = pl.ds(pl.multiple_of(n * BLK, BLK), BLK)
        z2[:, cs] += dg(gg[...], wi[cs, :], 1, 1)
        return 0

    lax.fori_loop(0, 3, into_h, 0)

    def first_norm(i, sums):
        rs = pl.ds(pl.multiple_of(i * BLK, BLK), BLK)
        dh = z2[rs, :]
        xh = xh1[rs, :]
        dxh = dh * gain1
        dz = inv1[rs, :] * (dxh - jnp.mean(dxh, axis=-1, keepdims=True) - xh * jnp.mean(dxh * xh, axis=-1, keepdims=True))
        dz1_ref[rs, :] = dz
        dzb = dz.astype(BF)
        dz2b[rs, :] = dzb
        do_ref[i] = dg(wo[...], dzb, 1, 1).astype(BF)
        return (
            sums[0] + jnp.sum(dz, axis=0, keepdims=True),
            sums[1] + jnp.sum(dh * xh, axis=0, keepdims=True),
            sums[2] + jnp.sum(dh, axis=0, keepdims=True),
        )

    s0, s1, s2 = lax.fori_loop(0, 3, first_norm, (zero, zero, zero))
    small_ref[0:1, :] = s0
    small_ref[1:2, :] = s1
    small_ref[2:3, :] = s2
    for j in range(4):
        rows = pl.ds(192 * j, 192)
        acc = jnp.dot(ot[0, rows, :], dz2b[0:BLK, :], preferred_element_type=F32)
        acc += jnp.dot(ot[1, rows, :], dz2b[BLK : 2 * BLK, :], preferred_element_type=F32)
        acc += jnp.dot(ot[2, rows, :], dz2b[2 * BLK : 3 * BLK, :], preferred_element_type=F32)
        go_ref[j] = acc.astype(BF)
    small_ref[6:8, :] = jnp.zeros((2, 768), F32)
    small_ref[12:16, :] = jnp.zeros((4, 768), F32)

    for cond, copy in pending:
        if cond is None:
            copy.wait_send()
        else:
            pl.when(cond)(copy.wait_send)
    sent = [in_core, back_core] + in_first + in_second + in_diag + back_first + back_second + back_diag
    for copy in sent + [to_core(s, ch) for s in range(2) for ch in range(3)]:
        copy.wait_send()
    for ch in range(Y_EARLY):
        to_across(ch).wait_recv()
        for k in range(2):
            gf_ref[0, ch, k] = (gf_ref[0, ch, k].astype(F32) + ry[ch, k].astype(F32)).astype(BF)
        to_across(ch).wait_send()

def split3(v):
    a = v.astype(BF).astype(F32)
    b = (v - a).astype(BF).astype(F32)
    return a, b, v - a - b


class Piece:
    def __init__(self, value, other, from_y, from_x, from_end, from_mate, final, send, recv, where, fold=None):
        self.value, self.other, self.final = value, other, final
        self.from_y, self.from_x, self.from_end, self.from_mate = from_y, from_x, from_end, from_mate
        self.send, self.recv, self.where, self.fold = send, recv, where, fold

    def copy(self, stage, src, dst, **device):
        return pltpu.make_async_remote_copy(
            src_ref=src, dst_ref=dst, send_sem=self.send.at[stage], recv_sem=self.recv.at[stage],
            device_id=device, device_id_type=MESH,
        )

    def to_y(self):
        return self.copy(0, self.other, self.from_y, tensor=self.where["across"])

    def to_x(self):
        return self.copy(1, self.value, self.from_x, dp=self.where["side"])

    def to_inner(self):
        return self.copy(2, self.value, self.from_end, dp=self.where["pair"])

    def to_mate(self):
        return self.copy(3, self.value, self.from_mate, dp=self.where["mate"])

    def to_end(self):
        return self.copy(4, self.final, self.final, dp=self.where["pair"])

    def add(self, arrived, into):
        into[...] = (self.value[...].astype(F32) + arrived[...].astype(F32)).astype(into.dtype)

    def after_y(self):
        self.to_y().wait_recv()
        if self.fold is None:
            self.add(self.from_y, self.value)
        else:
            self.fold(self)
        self.begin_x()

    def begin_x(self):
        if self.where["line"]:
            self.to_x().start()
        else:
            self.final[...] = self.value[...]

    def after_x(self):
        if not self.where["line"]:
            return
        self.to_x().wait()
        self.add(self.from_x, self.value)
        pl.when(self.where["end"])(lambda: self.to_inner().start())

    def after_end(self):
        if not self.where["line"]:
            return

        @pl.when(self.where["inner"])
        def _():
            self.to_inner().wait_recv()
            self.add(self.from_end, self.value)
            self.to_mate().start()

    def after_mate(self):
        if not self.where["line"]:
            return

        @pl.when(self.where["inner"])
        def _():
            self.to_mate().wait_recv()
            self.add(self.from_mate, self.final)
            self.to_end().start()

    def finish(self, had_y=True):
        if had_y:
            self.to_y().wait_send()
        if not self.where["line"]:
            return

        @pl.when(self.where["end"])
        def _():
            self.to_end().wait_recv()
            self.to_inner().wait_send()

        @pl.when(self.where["inner"])
        def _():
            self.to_mate().wait_send()
            self.to_end().wait_send()


def k3(
    line,
    qkv_ref, seg_ref, o_ref, lse_ref, xab_ref, wt_ref, wpar_ref, do_in, dz1_in, gf_ref, go_ref, small_ref,
    din_ref, ff_ref, fs_ref, sm_ref,
    dz1_ref, do_ref, dq_s, qa, ka, va, da, dk, dv, sbuf, rcore, rmid, rhalf, hsum,
    fv, fy, fx, fe, fm, sv, so, sy, sx, se, sm, rgo, tv, to, tc, ty, tx, te, tm,
    psend, precv, send, recv, landed, local,
):
    length = 1024
    t, d, core, across, diag, side = where_am_i()
    y, c = t // 2, t % 2
    where = {"across": across, "side": side, "line": line}
    known = [{"tensor": core}, {"tensor": across}, {"tensor": diag}]
    if line:
        z = d // 2
        where["pair"] = d + 2 - 4 * (z % 2)
        where["mate"] = d + 2 - 4 * ((z + 1) % 2)
        where["end"] = (z == 0) | (z == 3)
        where["inner"] = (z == 1) | (z == 2)
        known += [{"dp": side}, {"dp": where["pair"]}]
    barrier = pltpu.get_barrier_semaphore()
    for dev in known:
        pl.semaphore_signal(barrier, inc=1, device_id=dev, device_id_type=MESH)
    if line:
        @pl.when(where["inner"])
        def _():
            pl.semaphore_signal(barrier, inc=1, device_id={"dp": where["mate"]}, device_id_type=MESH)
            pl.semaphore_wait(barrier, len(known) + 1)

        @pl.when(where["end"])
        def _():
            pl.semaphore_wait(barrier, len(known))
    else:
        pl.semaphore_wait(barrier, len(known))

    pending = []
    peers = (t, core, across, diag)
    for i in range(3):
        middle, blk = block_of(t, i)
        for j, dev in enumerate(peers):
            src = do_in.at[i, pl.ds(192 * j, 192)]
            group = jnp.where(middle == 1, 2, j // 2)
            dst = do_ref.at[group, blk]
            sem = landed.at[group * 4 + blk]
            if j == 0:
                pltpu.make_async_copy(src, dst, sem).start()
                continue
            if j == 2:
                pl.when(middle == 0)(pltpu.make_async_copy(src, dst, sem).start)
                dev_to, cond = across, middle == 1
            elif j == 1:
                dev_to, cond = core, None
            else:
                dev_to, cond = jnp.where(middle == 1, diag, core), None
            copy = pltpu.make_async_remote_copy(
                src_ref=src, dst_ref=dst, send_sem=send.at[i * 3 + j - 1], recv_sem=sem,
                device_id={"tensor": dev_to}, device_id_type=MESH,
            )
            if cond is None:
                copy.start()
            else:
                pl.when(cond)(copy.start)
            pending.append((cond, copy))

    loads = [pltpu.make_async_copy(gf_ref.at[0, p // 2, p % 2], fv.at[p], local.at[p]) for p in range(6)]
    loads.append(pltpu.make_async_copy(dz1_in, dz1_ref, local.at[6]))
    start_all(loads)
    go_core = [
        pltpu.make_async_remote_copy(
            src_ref=go_ref.at[2 * k + 1], dst_ref=rgo.at[k], send_sem=send.at[9 + k], recv_sem=recv.at[6 + k],
            device_id={"tensor": core}, device_id_type=MESH,
        )
        for k in range(2)
    ]
    small_core = pltpu.make_async_remote_copy(
        src_ref=small_ref, dst_ref=tc, send_sem=send.at[11], recv_sem=recv.at[8],
        device_id={"tensor": core}, device_id_type=MESH,
    )
    start_all(go_core + [small_core])
    big = [
        Piece(fv.at[p], gf_ref.at[1, p // 2, p % 2], fy.at[p], fx.at[p], fe.at[p], fm.at[p], ff_ref.at[p],
              psend.at[p], precv.at[p], where)
        for p in range(6)
    ]
    thin = [
        Piece(sv.at[p], so.at[p], sy.at[p], sx.at[p], se.at[p], sm.at[p], fs_ref.at[p],
              psend.at[6 + p], precv.at[6 + p], where)
        for p in range(4)
    ]

    def fold_small(piece):
        got = ty[...]
        add = jnp.concatenate([got[0:8], got[10:11], jnp.zeros((3, 768), F32), got[13:14], jnp.zeros((3, 768), F32)])
        tv[...] = tv[...] + add

    tiny = Piece(tv, to, ty, tx, te, tm, sm_ref, psend.at[10], precv.at[10], where, fold_small)
    early = 2 * Y_EARLY
    for p in range(early, 6):
        big[p].to_y().start()
    for copy in loads:
        copy.wait()
    for p in range(early):
        big[p].begin_x()

    row64 = lax.broadcasted_iota(jnp.int32, (64, length), 0)

    def rows_of(blk):
        return pl.ds(pl.multiple_of(blk * BLK, BLK), BLK)

    own_seq = 2 * y

    def keep_or_send(middle, blk, r):
        seq = 1 if middle else own_seq
        i = 4 * seq + blk - 3 * t
        mine = (i >= 0) & (i < 3)

        @pl.when(mine)
        def _():
            rs = rows_of(i)
            dz1_ref[rs, :] += r

        @pl.when(jnp.logical_not(mine))
        def _():
            sbuf[1 if middle else 0, rows_of(blk), :] = r.astype(BF)

    def into_middle(n, _):
        keep_or_send(True, n, dg(dq2[:, rows_of(n)], wt_ref[...], 0, 0))
        return 0

    dq0, dq1, dq2 = [dq_s.at[g] for g in range(3)]

    def into_own(n, _):
        r = dg(dq0[:, rows_of(n)], wt_ref[...], 0, 0) + dg(dq1[:, rows_of(n)], wpar_ref[...], 0, 0)
        keep_or_send(False, n, r)
        return 0

    far = 2 * (1 - y)
    half_copy = pltpu.make_async_remote_copy(
        src_ref=sbuf.at[1, rows_of(far + 1 - c)], dst_ref=rhalf, send_sem=send.at[12],
        recv_sem=recv.at[3], device_id={"tensor": core}, device_id_type=MESH,
    )
    far_copy = pltpu.make_async_remote_copy(
        src_ref=hsum, dst_ref=rmid.at[c], send_sem=send.at[13], recv_sem=recv.at[4 + c],
        device_id={"tensor": 2 * (1 - y) + y}, device_id_type=MESH,
    )
    core_copies = []
    for i in range(3):
        middle, blk = block_of(core, i)
        core_copies.append((
            middle,
            pltpu.make_async_remote_copy(
                src_ref=sbuf.at[middle, rows_of(blk)], dst_ref=rcore.at[i], send_sem=send.at[14 + i],
                recv_sem=recv.at[i], device_id={"tensor": core}, device_id_type=MESH,
            ),
        ))

    def unit(u, _):
        g = (u // 3 + 1) % 3
        h = u % 3

        @pl.when(u == 1)
        def _():
            for copy in go_core:
                copy.wait_recv()
            small_core.wait_recv()
            sv[0] = (go_ref[0].astype(F32) + rgo[0].astype(F32)).astype(BF)
            so[0] = (go_ref[2].astype(F32) + rgo[1].astype(F32)).astype(BF)
            thin[0].to_y().start()
            a, b = small_ref[...], tc[...]
            swapped = jnp.concatenate([b[0:8], b[9:10], b[8:9], b[11:12], b[10:11], b[12:16]])
            tv[...] = a + swapped

        @pl.when(u == 3)
        def _():
            for k in range(3):
                so[1 + k] = jnp.dot(dq_s[1, pl.ds(192 * k, 192), :], xab_ref[0], preferred_element_type=F32).astype(BF)
                thin[1 + k].to_y().start()

        @pl.when(u == 6)
        def _():
            lax.fori_loop(0, 4, into_middle, 0)
            half_copy.start()

        for k, steps in UNIT_STEPS.items():
            @pl.when(u == k)
            def _(steps=steps):
                for stage, p in steps:
                    getattr(big[p], stage)()

        @pl.when(u == 7)
        def _():
            half_copy.wait_recv()
            hsum[...] = (sbuf[1, rows_of(far + c), :].astype(F32) + rhalf[...].astype(F32)).astype(BF)
            far_copy.start()

        @pl.when(h == 0)
        def _():
            for blk in range(4):
                pltpu.make_async_copy(do_in.at[0, pl.ds(0, 192)], do_ref.at[g, blk], landed.at[g * 4 + blk]).wait()

        same = (row64 == seg_ref[jnp.where(g == 2, 1, own_seq)]).astype(F32)
        ro = pl.multiple_of(h * 192, 64)
        qh, kh, vh = pl.ds(ro, 64), pl.ds(ro + 64, 64), pl.ds(ro + 128, 64)
        l1, l2, l3 = split3(-lse_ref[g * 3 + h])
        qa[0:64, :] = qkv_ref[g, h, 0:64, :]
        qa[64:128, :] = jnp.where(row64 == 8, l1, jnp.where(row64 == 9, l2, jnp.where(row64 == 10, l3, same))).astype(BF)
        key_mark = jnp.where(row64 >= 8, 1.0, (same - 1.0) * BIG).astype(BF)
        ka[...] = jnp.concatenate([qkv_ref[g, h, 64:128, :], key_mark], axis=0).T
        va[...] = jnp.concatenate([qkv_ref[g, h, 128:192, :], jnp.ones((64, length), BF)], axis=0).T
        hs = pl.ds(pl.multiple_of(h * 64, 64), 64)
        for b in range(4):
            bs = slice(b * BLK, (b + 1) * BLK)
            do = do_ref[g, b, hs, :]
            e1, e2, e3 = split3(-jnp.sum(do.astype(F32) * o_ref[g, b, hs, :].astype(F32), axis=0, keepdims=True))
            da[0:64, bs] = do
            rb = row64[:, bs]
            da[64:128, bs] = jnp.where(rb == 8, e1, jnp.where(rb == 9, e2, jnp.where(rb == 10, e3, 0.0))).astype(BF)
        dk[...] = jnp.zeros_like(dk)
        dv[...] = jnp.zeros_like(dv)

        def chunk(n, _):
            cs = pl.ds(pl.multiple_of(n * 512, 512), 512)
            s = jnp.dot(ka[...], qa[:, cs], preferred_element_type=F32)
            p = jnp.exp2(s)
            dp = jnp.dot(va[...], da[:, cs], preferred_element_type=F32)
            pb = p.astype(BF)
            ds = (p * dp).astype(BF)
            dv[...] += dg(da[0:64, cs], pb, 1, 1)
            dk[...] += dg(qa[0:64, cs], ds, 1, 1)
            dq = jnp.dot(qkv_ref[g, h, 64:128, :], ds, preferred_element_type=F32)
            dq_s[g, qh, cs] = (dq * (HEAD_DIM ** (-0.5))).astype(BF)
            return 0

        lax.fori_loop(0, length // 512, chunk, 0)
        dq_s[g, kh, :] = (dk[...] * math.log(2.0)).astype(BF)
        dq_s[g, vh, :] = dv[...].astype(BF)

        @pl.when(u >= 6)
        def _():
            rows = pl.ds(ro, 192)
            r = jnp.dot(dq_s[0, rows, :], xab_ref[0], preferred_element_type=F32)
            sv[1 + h] = (r + jnp.dot(dq_s[2, rows, :], xab_ref[1], preferred_element_type=F32)).astype(BF)

        return 0

    lax.fori_loop(0, 9, unit, 0)
    ones = jnp.ones((8, length), BF)
    tv[12:13, 0:576] = (dg(ones, dq_s[0], 1, 1) + dg(ones, dq_s[2], 1, 1))[0:1]
    tv[13:14, 0:576] = dg(ones, dq_s[1], 1, 1)[0:1]
    to[...] = tv[...]
    tiny.to_y().start()
    lax.fori_loop(0, 4, into_own, 0)
    for middle, copy in core_copies:
        copy.start()

    named = {"p%d" % p: piece for p, piece in enumerate(big)}
    named.update({"w%d" % p: piece for p, piece in enumerate(thin)})
    named["t"] = tiny
    for k, (stage, name) in enumerate(TAIL_STEPS):
        getattr(named[name], stage)()
        if k == TAIL_INPUT:
            for i in range(3):
                core_copies[i][1].wait_recv()
                middle, blk = block_of(t, i)
                rs = pl.ds(i * BLK, BLK)

                @pl.when(middle == 0)
                def _():
                    din_ref[rs, :] = (dz1_ref[rs, :] + rcore[i].astype(F32)).astype(BF)

                @pl.when(middle == 1)
                def _():
                    k = blk % 2
                    pltpu.make_async_copy(hsum, rmid.at[k], recv.at[4 + k]).wait()
                    din_ref[rs, :] = (dz1_ref[rs, :] + rcore[i].astype(F32) + rmid[k].astype(F32)).astype(BF)

    for p, piece in enumerate(big):
        piece.finish(p >= early)
    for piece in thin + [tiny]:
        piece.finish()
    for copy in [c for _, c in core_copies] + [half_copy, far_copy] + go_core + [small_core]:
        copy.wait_send()
    for cond, copy in pending:
        if cond is None:
            copy.wait_send()
        else:
            pl.when(cond)(copy.wait_send)

def vm(*shape, dtype=BF):
    return pltpu.VMEM(shape, dtype)


def sds(*shape, dtype=BF):
    return jax.ShapeDtypeStruct(shape, dtype)


VM = pl.BlockSpec(memory_space=pltpu.VMEM)
ANY = pl.BlockSpec(memory_space=pl.ANY)


def params(cid):
    return pltpu.CompilerParams(collective_id=cid, has_side_effects=True, vmem_limit_bytes=62 * 2**20)


def local_step(
    line,
    layer_input, segment_ids, w_query, b_query, w_key, w_value, b_value, w_out, b_out, first_gain, first_shift,
    w_in, b_in, w_back, b_back, second_gain, second_shift, cotangent,
):
    seg = segment_ids.reshape(3, 1, 1024)
    wt = jnp.stack([w_query, w_key, w_value]).reshape(3, 768, 3, 64).transpose(2, 0, 3, 1).reshape(576, 768)
    zeros = jnp.zeros((192,), F32)
    heads = jnp.stack([b_query.astype(F32), zeros, b_value.astype(F32)]).reshape(3, 3, 64).transpose(1, 0, 2).reshape(576)
    bias = jnp.stack([b_in.astype(F32), jnp.concatenate([heads, zeros])])
    bias = jnp.concatenate([bias, jnp.zeros((6, 768), F32)])
    vec = jnp.stack([b_out, first_gain, first_shift, b_back, second_gain, second_shift])
    vec = jnp.concatenate([vec, jnp.zeros((2, 768), F32)])
    dma = pltpu.SemaphoreType.DMA

    qkv, o, lse, xab, wpar, woutg, wing, biasg = pl.pallas_call(
        k1,
        out_shape=(
            sds(3, 3, 192, 1024), sds(3, 4, 192, BLK), sds(9, 1, 1024, dtype=F32), sds(2, 1024, 768), sds(576, 768),
            sds(3, 192, 768), sds(2, 768, 768), sds(3, 8, 768, dtype=F32),
        ),
        in_specs=[ANY, ANY, VM, VM, ANY, ANY],
        out_specs=(ANY, ANY, VM, ANY, ANY, ANY, ANY, VM),
        scratch_shapes=[
            vm(3, 3, 192, 1024), vm(3, 4, 192, BLK), vm(2, 1024, 768), vm(2, 576, 768), vm(576, 1, dtype=F32),
            vm(128, 1024), vm(128, 1024), vm(80, 1024), dma((32,)), dma((32,)), dma((10,)),
        ],
        compiler_params=params(0),
        name="attention_forward",
    )(layer_input, wt, bias, seg, w_out, w_in)

    out, dz1, do, gf, go, small = pl.pallas_call(
        k2,
        out_shape=(
            sds(768, 768), sds(768, 768, dtype=F32), sds(3, 768, BLK), sds(2, 3, 2, 768, BLK), sds(4, 192, 768),
            sds(16, 768, dtype=F32),
        ),
        in_specs=[VM, VM, VM, VM, VM, ANY, ANY, ANY, ANY, ANY, ANY],
        out_specs=(VM, VM, VM, VM, VM, VM),
        scratch_shapes=[
            vm(3, 768, BLK), vm(768, 768), vm(768, 3072), vm(3072, 768),
            vm(768, 768), vm(768, 768), vm(768, 768, dtype=F32), vm(768, 1, dtype=F32), vm(768, 3072), vm(768, 3072),
            vm(768, 768, dtype=F32), vm(768, 768), vm(768, 768),
            vm(2, 3, 2, 768, BLK), vm(2, 3, 2, 768, BLK), vm(max(Y_EARLY, 1), 2, 768, BLK),
            dma((48,)), dma((48,)), dma((20,)),
        ],
        compiler_params=params(1),
        name="feed_forward",
    )(layer_input, cotangent, vec, bias, biasg, o, w_out, woutg, w_in, wing, w_back)

    piece, slab, tiny = vm(6, 768, BLK), vm(4, 192, 768), vm(16, 768, dtype=F32)
    din, ff, fs, sm = pl.pallas_call(
        partial(k3, line),
        out_shape=(sds(768, 768), sds(6, 768, BLK), sds(4, 192, 768), sds(16, 768, dtype=F32)),
        in_specs=[VM, VM, VM, VM, VM, VM, VM, ANY, ANY, ANY, VM, VM],
        out_specs=(VM, VM, VM, VM),
        scratch_shapes=[
            vm(768, 768, dtype=F32),
            vm(3, 4, 192, BLK), vm(3, 576, 1024), vm(128, 1024), vm(1024, 128), vm(1024, 128), vm(128, 1024),
            vm(64, 1024, dtype=F32), vm(64, 1024, dtype=F32), vm(2, 1024, 768),
            vm(3, BLK, 768), vm(2, BLK, 768), vm(BLK, 768), vm(BLK, 768),
            piece, piece, piece, piece, piece, slab, slab, slab, slab, slab, slab, vm(2, 192, 768),
            tiny, tiny, tiny, tiny, tiny, tiny, tiny,
            dma((11, 5)), dma((11, 5)), dma((17,)), dma((9,)), dma((12,)), dma((7,)),
        ],
        compiler_params=params(2),
        name="attention_backward",
    )(qkv, seg, o, lse, xab, wt, wpar, do, dz1, gf, go, small)
    if not line:
        ff, fs = lax.psum((ff, fs), "dp")
        sm = lax.psum(sm, "dp")
    ff = ff.astype(F32).reshape(3, 2, 768, BLK)
    g_in = jnp.concatenate([ff[0, 0], ff[1, 0], ff[2, 0]], axis=1)
    g_back = jnp.concatenate([ff[0, 1].T, ff[1, 1].T, ff[2, 1].T], axis=0)
    heads = fs[1:4].astype(F32).reshape(3, 3, 64, 768).transpose(1, 3, 0, 2).reshape(3, 768, 192)
    bq = sm[12, 0:576].reshape(3, 3, 64).transpose(1, 0, 2).reshape(3, 192)
    return (
        out, din, heads[0], bq[0], heads[1], heads[2], bq[2], fs[0].astype(F32),
        sm[0], sm[1], sm[2], g_in, sm[8], g_back, sm[3], sm[4], sm[5],
    )

def solution(mesh):
    rows = P(("dp", "tensor"), None)
    in_specs = (
        rows, P("dp", None), P(None, "tensor"), P("tensor"), P(None, "tensor"), P(None, "tensor"), P("tensor"),
        P("tensor", None), P(), P(), P(), P(None, "tensor"), P("tensor"), P("tensor", None), P(), P(), P(), rows,
    )
    out_specs = (
        rows, rows, P(None, "tensor"), P("tensor"), P(None, "tensor"), P(None, "tensor"), P("tensor"),
        P("tensor", None), P(), P(), P(), P(None, "tensor"), P("tensor"), P("tensor", None), P(), P(), P(),
    )
    line = mesh.shape["dp"] == 8
    return jax.shard_map(partial(local_step, line), mesh=mesh, in_specs=in_specs, out_specs=out_specs, check_vma=False)
```

time: 476 us -> 300 us (0.63)
  waiting for transfers between devices: 96.2 us -> 0 us
  blocking collectives: 65.2 us -> 0 us
  between operations: 14.2 us -> 0.74 us
  Pallas kernels: 249 us -> 261 us
  other arithmetic: 16.9 us -> 9.3 us
  starting transfers between devices: 5.59 us -> 0 us
    psum x1 -> x0, waiting for transfers between devices: 68.7 us -> none  [local_step(): big = lax.psum((p0.astype(BF), pq.astype(BF)), 'dp')]
    psum x2 -> x0, blocking collectives: 65.2 us -> none  [the longest x1 44.7 us: local_step(): shared = lax.psum(small[0:6], ('dp', 'tensor'))]
    ppermute x8 -> x0, waiting for transfers between devices: 27.5 us -> none  [the longest x4 22.9 us: across_swap(): return lax.ppermute(v, 'tensor', [(0, 2), (2, 0), (1, 3), (3, 1)])]
    convert_element_type x7 -> x1, other arithmetic: 14 us -> 1.81 us  [local_step(): fs[0].astype(F32)]
    pallas_call x3, Pallas kernels: 249 us -> 261 us  [the longest x1 126 us: local_step(): pl.pallas_call(partial(k3, line), out_shape=(sds(768, 768), sds(6, 768, B...]
    ppermute x8 -> x0, starting transfers between devices: 5.56 us -> none  [the longest x4 3.44 us: across_swap(): return lax.ppermute(v, 'tensor', [(0, 2), (2, 0), (1, 3), (3, 1)])]
  transfers between devices with their start and end apart: 9 -> 0, of which waited for: 4 -> 0; matrix products, arithmetic and copies ran while one was open for 2% -> 0% of each run, Pallas kernels for 22% -> 0%
where the time goes in v2:
time: 300 us; the launch traced here: 297 us
  Pallas kernels  261 us (87%)
  local copies, waits for them, and re-layouts  26.5 us (9%)
  other arithmetic  9.3 us (3%)
    pallas_call x1, Pallas kernels, local_step(): pl.pallas_call(partial(k3, line), out_shape=(sds(768, 768), sds(6, 768, B...  126 us
    pallas_call x1, Pallas kernels, local_step(): pl.pallas_call(k2, out_shape=(sds(768, 768), sds(768, 768, dtype=F32), sd...  82.1 us
    pallas_call x1, Pallas kernels, local_step(): pl.pallas_call(k1, out_shape=(sds(3, 3, 192, 1024), sds(3, 4, 192, BLK),...  52.4 us
    unnamed x15, local copies, waits for them, and re-layouts  8.82 us

profile of v2, /device:TPU:4, one launch (start us, length us, event | category | flops | bytes accessed | tf_op | source)
XLA Modules:
  0.0 297.5 jit_solution(4587779947325805384)
XLA Ops:
  0.7 0.7 stack.52
  1.3 0.7 stack.53
  2.0 0.7 stack.54
  2.7 0.7 stack.55
  5.4 0.7 reshape.90
  6.2 0.7 reshape.89
  8.6 2.1 pad_maximum_fusion.2
  10.8 1.3 reshape.84.seg_ref
  12.1 52.4 %attention_forward.1 = (bf16[3,3,192,1024]{3,2,1,0:T(8,128)(2,1)}, bf16[3,4,192,256]{3,2,1,0:T(8,128)(2,1)}, f32[9,1,1024]{2,1,0:T(1,128)}, bf16[2,1024,768]{2,1...) custom-call(bf16[768,768]{1,0:T(8,128)(2,1)} %x_ref.3, ...), custom_call_target="tpu_custom_call" | custom-call | tf_op jit(solution)/shard_map/attention_forward/pallas_call | solution.py:959
  64.5 82.1 %feed_forward.1 = (bf16[768,768]{1,0:T(8,128)(2,1)}, f32[768,768]{1,0:T(8,128)}, bf16[3,768,256]{2,1,0:T(8,128)(2,1)}, bf16[2,3,2,768,256]{4,3,2,1,0:T(8,128)(2,...) custom-call(bf16[768,768]{1,0:T(8,128)(2,1)} %x_ref.3, bf16[768,768]{1,0:T(8,128)(2,1)} %cot_ref.1, ...), custom_call_target="tpu_custom_call" | custom-call | tf_op jit(solution)/shard_map/feed_forward/pallas_call | solution.py:975
  146.6 126.4 %attention_backward.1 = (bf16[768,768]{1,0:T(8,128)(2,1)}, bf16[6,768,256]{2,1,0:T(8,128)(2,1)}, bf16[4,192,768]{2,1,0:T(8,128)(2,1)}, f32[16,768]{1,0:T(8,128)}) custom-call(bf16[3,3,192,1024]{3,2,1,0:T(8,128)(2,1)} %get-tuple-element.40.qkv_ref, s32[3,1,1024]{2,1,0:T(1,128)} %reshape.84.seg_ref, bf16[3,4,192,256]{3,2,1,0:T(8,128)(2,1)} %get-tuple-element.36.o_ref, ...), custom_call_target="tpu_custom_call" | custom-call | tf_op jit(solution)/shard_map/attention_backward/pallas_call | solution.py:995
  273.0 1.2 slice.68
  274.4 1.2 fusion.1
  275.7 0.8 slice_reduce_fusion.7
  277.9 1.8 bitcast_convert_fusion
  279.7 1.8 slice_reduce_fusion
  281.9 1.3 slice_bitcast_fusion.2
  283.2 1.5 fusion
  284.6 1.5 copy.50
  286.1 2.3 copy.49
  288.4 2.3 copy.48
  290.7 4.0 %pad_maximum_fusion = (f32[768,768]{1,0:T(8,128)}, f32[768,768]{1,0:T(8,128)}) fusion(f32[768,256]{1,0:T(8,128)S(1)} %copy-done.1, f32[768,256]{1,0:T(8,128)S(1)} %copy-done.2, f32[768,256]{1,0:T(8,128)S(1)} %get-tuple-element.62, f32[256,768]{1,0:T(8,128)S(1)} %bitcast.48, f32[256,768]{1,0:T(8,128)} %bitcast.49, f32[256,768]{1,0:T(8,128)} %bitcast.50), kind=kLoop, calls=%fused_computation | loop fusion | flops 2359296 | bytes 9437184 | tf_op jit(solution)/shard_map/concatenate | solution.py:1016
  294.7 1.0 copy.53
  296.4 1.0 copy.54
  (30 shorter events, 6.4 us)
Async XLA Ops:
  274.4 7.0 %copy-start = (bf16[6,768,256]{2,1,0:T(8,128)(2,1)S(1)}, bf16[6,768,256]{2,1,0:T(8,128)(2,1)}, u32[]{:S(2)}) copy-start(bf16[6,768,256]{2,1,0:T(8,128)(2,1)} %get-tuple-element.52) | copy-start | bytes 7077892
  284.6 6.1 %copy-start.1 = (f32[768,256]{1,0:T(8,128)S(1)}, f32[768,256]{1,0:T(8,128)}, u32[]{:S(2)}) copy-start(f32[768,256]{1,0:T(8,128)} %get-tuple-element.63) | copy-start | bytes 2359300
  284.6 6.1 %copy-start.2 = (f32[768,256]{1,0:T(8,128)S(1)}, f32[768,256]{1,0:T(8,128)}, u32[]{:S(2)}) copy-start(f32[768,256]{1,0:T(8,128)} %get-tuple-element.64) | copy-start | bytes 2359300
  290.7 4.0 %copy-start.3 = (bf16[768,768]{1,0:T(8,128)(2,1)S(1)}, bf16[768,768]{1,0:T(8,128)(2,1)}, u32[]{:S(2)}) copy-start(bf16[768,768]{1,0:T(8,128)(2,1)} %get-tuple-element.90) | copy-start | bytes 3538948
  294.7 1.7 copy-start.4

commit v3 on v2

--- a/solution.py
+++ b/solution.py
@@ -17,22 +17,21 @@
 LOG2E = 1.0 / math.log(2.0)
 QSCALE = HEAD_DIM ** (-0.5) * LOG2E
 BLK = 256
-IN_EARLY = 1
-Y_EARLY = 1
+Y_EARLY = 2
+X_EARLY = 1
 UNIT_STEPS = {
-    2: (("after_x", 0),),
-    3: (("after_y", 2),),
-    4: (("after_x", 1), ("after_end", 0)),
-    6: (("after_y", 3), ("after_x", 2), ("after_end", 1), ("after_mate", 0)),
-    8: (("after_y", 4), ("after_x", 3), ("after_end", 2), ("after_mate", 1)),
+    2: (("after_end", 0), ("after_x", 2), ("after_y", 4)),
+    4: (("after_end", 1), ("after_mate", 0), ("after_x", 3), ("after_y", 5)),
+    5: (("after_end", 2),),
+    6: (("after_mate", 1), ("after_x", 4)),
+    7: (("after_end", 3),),
+    8: (("after_mate", 2), ("after_x", 5), ("after_end", 4)),
 }
-TAIL_INPUT = 7
+TAIL_INPUT = 4
 TAIL_STEPS = (
-    ("after_y", "p5"), ("after_x", "p4"), ("after_end", "p3"), ("after_mate", "p2"),
-    ("after_y", "w0"), ("after_x", "p5"), ("after_end", "p4"), ("after_mate", "p3"),
-    ("after_y", "w1"), ("after_x", "w0"), ("after_end", "p5"), ("after_mate", "p4"),
-    ("after_y", "w2"), ("after_x", "w1"), ("after_end", "w0"), ("after_mate", "p5"),
-    ("after_y", "w3"), ("after_y", "t"), ("after_x", "w2"), ("after_end", "w1"), ("after_mate", "w0"),
+    ("after_y", "w0"), ("after_y", "w1"), ("after_mate", "p3"), ("after_end", "p5"), ("after_y", "w2"),
+    ("after_x", "w0"), ("after_mate", "p4"), ("after_x", "w1"), ("after_y", "w3"), ("after_y", "t"),
+    ("after_end", "w0"), ("after_mate", "p5"), ("after_x", "w2"), ("after_end", "w1"), ("after_mate", "w0"),
     ("after_x", "w3"), ("after_x", "t"), ("after_end", "w2"), ("after_mate", "w1"),
     ("after_end", "w3"), ("after_end", "t"), ("after_mate", "w2"),
     ("after_mate", "w3"), ("after_mate", "t"),
@@ -93,50 +92,74 @@
         copy.start()
 
 
-def k1(
-    x_ref, wt_ref, bias_ref, seg_ref, wout_ref, win_ref,
-    qkv_out, o_out, lse_ref, xab_out, wpar_out, woutg_ref, wing_ref, biasg_ref,
-    qkv, o_v, xab, w_v, bcol, qa, ka, va, send, recv, local,
+def layer_stats(z):
+    mean = jnp.mean(z, axis=-1, keepdims=True)
+    cen = z - mean
+    var = jnp.mean(cen * cen, axis=-1, keepdims=True)
+    inv = lax.rsqrt(var + EPSILON)
+    return cen * inv, inv
+
+
+def forward(
+    line,
+    x_ref, cot_in, wq_ref, wk_ref, wv_ref, bq_ref, bv_ref, bin_ref, v0, v1, v2, v3, v4, v5, seg_ref,
+    wout_ref, win_ref, wback_ref,
+    qkv_out, o_out, lse_ref, xab_out, wts_out, out_ref, dz1_out, do_ref, gf_ref, go_ref, small_ref,
+    qkv, o_v, xab, w_v, bias_ref, biasg_ref, bcol, qa, ka, va,
+    cot_ref, ot, wo, wi, wb, h1b, h1t, xh1, inv1, gg, gp, z2, dz2b, dz2t, gsend, rc, ry, rx, send, recv, local,
 ):
     length = 1024
     t, d, core, across, diag, side = where_am_i()
     y, c = t // 2, t % 2
     half = d % 2
-    greet([{"tensor": core}, {"tensor": across}, {"tensor": diag}, {"dp": side}])
+    x_early = X_EARLY if line else 0
+
+    rows_out, rows_local = [], []
     cp = Copies(send, recv)
-    rows_out, rows_local = [], []
+    cp.used = 12
     for i in range(3):
         middle, blk = block_of(t, i)
         src = x_ref.at[pl.ds(i * BLK, BLK)]
         dst = xab.at[middle, pl.ds(pl.multiple_of(blk * BLK, BLK), BLK)]
         rows_local.append(pltpu.make_async_copy(src, dst, local.at[i]))
         rows_out.append(cp.new(src, dst, tensor=core))
-    w_local = pltpu.make_async_copy(wt_ref, w_v.at[0], local.at[3])
-    cross_in = 2 * (1 - y) + c
-    cross_slot = pl.ds(pl.multiple_of(cross_in * BLK, BLK), BLK)
+    own = [
+        pltpu.make_async_copy(wout_ref, wo.at[pl.ds(0, 192)], local.at[12]),
+        pltpu.make_async_copy(win_ref, wi.at[:, pl.ds(0, 768)], local.at[13]),
+        pltpu.make_async_copy(wback_ref, wb.at[pl.ds(0, 768)], local.at[14]),
+        pltpu.make_async_copy(cot_in, cot_ref, local.at[15]),
+    ]
+    start_all(rows_local + own)
+
+    for k, ref in enumerate((wq_ref, wk_ref, wv_ref)):
+        for h in range(3):
+            n = 192 * h + 64 * k
+            w_v[0, n : n + 64, :] = ref[64 * h : 64 * h + 64, :]
+    bias_ref[...] = jnp.zeros((8, 768), F32)
+    bias_ref[0:1, :] = bin_ref[...].astype(F32).reshape(1, 768)
+    bq, bv = bq_ref[...].astype(F32).reshape(1, 192), bv_ref[...].astype(F32).reshape(1, 192)
+    parts = []
+    for h in range(3):
+        parts += [bq[:, 64 * h : 64 * h + 64], jnp.zeros((1, 64), F32), bv[:, 64 * h : 64 * h + 64]]
+    bias_ref[1:2, 0:576] = jnp.concatenate(parts, axis=1)
+
+    greet([{"tensor": core}, {"tensor": across}, {"tensor": diag}, {"dp": side}])
+
     mixed = (t == 1) | (t == 2)
-    first_middle = jnp.where(t == 1, 1, 0)
-    cross_out = []
-    base = cp.used
-    for k in range(2):
-        src = x_ref.at[pl.ds(pl.multiple_of((first_middle + k) * BLK, BLK), BLK)]
-        dst = xab.at[1, pl.ds(pl.multiple_of((2 * y + k) * BLK, BLK), BLK)]
-        cross_out.append(
-            pltpu.make_async_remote_copy(
-                src_ref=src, dst_ref=dst, send_sem=send.at[base + k], recv_sem=recv.at[base],
-                device_id={"tensor": 2 * (1 - y) + k}, device_id_type=MESH,
-            )
-        )
-    cp.used += 2
+    k_out = jnp.where(mixed, 0, 1)
+    block_out = pl.ds(pl.multiple_of((2 * y + k_out) * BLK, BLK), BLK)
+    block_in = pl.ds(pl.multiple_of((2 * (1 - y) + c) * BLK, BLK), BLK)
+    n = cp.used
+    cross_out = cp.new(xab.at[1, block_out], xab.at[1, block_out], tensor=2 * (1 - y) + k_out)
     cross_arrived = pltpu.make_async_remote_copy(
-        src_ref=x_ref.at[pl.ds(0, BLK)], dst_ref=xab.at[1, cross_slot], send_sem=send.at[base],
-        recv_sem=recv.at[base], device_id={"tensor": core}, device_id_type=MESH,
+        src_ref=xab.at[1, block_out], dst_ref=xab.at[1, block_in], send_sem=send.at[n], recv_sem=recv.at[n],
+        device_id={"tensor": core}, device_id_type=MESH,
     )
-    cross_forward = cp.new(xab.at[1, cross_slot], xab.at[1, cross_slot], tensor=core)
+    cross_forward = cp.new(xab.at[1, block_in], xab.at[1, block_in], tensor=core)
     wp_first, wp_second = [], []
     for i in range(3):
         part = half_rows(half, 576, 3, i)
-        wp_first.append(cp.new(wt_ref.at[part], w_v.at[1, part], tensor=across))
+        wp_first.append(cp.new(w_v.at[0, part], w_v.at[1, part], tensor=across))
         wp_second.append(cp.new(w_v.at[1, part], w_v.at[1, part], dp=side))
     bias_out = [
         cp.new(bias_ref, biasg_ref.at[0], tensor=core),
@@ -144,31 +167,61 @@
         cp.new(bias_ref, biasg_ref.at[2], tensor=diag),
     ]
     part = half_rows(half, 192, 1, 0)
-    wo_first = cp.new(wout_ref.at[part], woutg_ref.at[1, part], tensor=across)
-    wo_second = cp.new(woutg_ref.at[1, part], woutg_ref.at[1, part], dp=side)
-    wo_core = cp.new(wout_ref, woutg_ref.at[0], tensor=core)
-    wo_diag = cp.new(woutg_ref.at[1], woutg_ref.at[2], tensor=core)
-    wi_first, wi_second, wi_diag = [], [], []
-    for i in range(IN_EARLY):
+    place = pl.ds(part.start + 384, part.size)
+    wo_first = cp.new(wout_ref.at[part], wo.at[place], tensor=across)
+    wo_second = cp.new(wo.at[place], wo.at[place], dp=side)
+    wo_core = cp.new(wout_ref, wo.at[pl.ds(192, 192)], tensor=core)
+    wo_diag = cp.new(wo.at[pl.ds(384, 192)], wo.at[pl.ds(576, 192)], tensor=core)
+
+    def lanes(j):
+        return pl.ds(768 * j, 768)
+
+    in_core = cp.new(win_ref, wi.at[:, lanes(1)], tensor=core)
+    back_core = cp.new(wback_ref, wb.at[lanes(1)], tensor=core)
+    in_first, in_second, in_diag, back_first, back_second, back_diag = [], [], [], [], [], []
+    for i in range(3):
         part = half_rows(half, 768, 3, i)
-        wi_first.append(cp.new(win_ref.at[part], wing_ref.at[0, part], tensor=across))
-        wi_second.append(cp.new(wing_ref.at[0, part], wing_ref.at[0, part], dp=side))
+        in_first.append(cp.new(win_ref.at[part], wi.at[part, lanes(2)], tensor=across))
+        in_second.append(cp.new(wi.at[part, lanes(2)], wi.at[part, lanes(2)], dp=side))
+        place = pl.ds(part.start + 2 * 768, part.size)
+        back_first.append(cp.new(wback_ref.at[part], wb.at[place], tensor=across))
+        back_second.append(cp.new(wb.at[place], wb.at[place], dp=side))
         for h in range(2):
             both = half_rows(h, 768, 3, i)
-            wi_diag.append(cp.new(wing_ref.at[0, both], wing_ref.at[1, both], tensor=core))
-
-    start_all(rows_local + [w_local] + rows_out)
-    start_all(bias_out)
-
-    @pl.when(mixed)
-    def _():
-        start_all(cross_out)
-
-    start_all(wp_first)
-    start_all([wo_core, wo_first] + wi_first)
-
+            in_diag.append(cp.new(wi.at[both, lanes(2)], wi.at[both, lanes(3)], tensor=core))
+            m = h * 384 + i * 128
+            back_diag.append(cp.new(wb.at[pl.ds(2 * 768 + m, 128)], wb.at[pl.ds(3 * 768 + m, 128)], tensor=core))
+
+    peers = (t, core, across, diag)
+
+    def heads_to_rows(group):
+        found = []
+        for j, dev in enumerate(peers):
+            if group != 2 and j >= 2:
+                continue
+            for i in range(3):
+                middle, blk = block_of(dev, i)
+                slot = j + 2 if group == 1 else j
+                src, dst = o_v.at[group, blk], ot.at[i, pl.ds(slot * 192, 192)]
+                sem = recv.at[i * 4 + slot]
+                if j == 0:
+                    copy = pltpu.make_async_copy(src, dst, sem)
+                else:
+                    copy = pltpu.make_async_remote_copy(
+                        src_ref=src, dst_ref=dst, send_sem=send.at[9 + i if group == 1 else 3 * (j - 1) + i],
+                        recv_sem=sem, device_id={"tensor": dev}, device_id_type=MESH,
+                    )
+                found.append((j, (middle == 1) if group == 2 else (middle == 0), copy))
+        return found
+
+    def start_heads(group):
+        for _, cond, copy in heads_to_rows(group):
+            pl.when(cond)(copy.start)
+
+    start_all(rows_out + bias_out + wp_first[:1])
+    start_all([wo_core, in_core, back_core])
+    va[64:80, :] = jnp.ones((16, length), BF)
     row64 = lax.broadcasted_iota(jnp.int32, (64, length), 0)
-    va[64:80, :] = jnp.ones((16, length), BF)
     factor = jnp.where(lax.broadcasted_iota(jnp.int32, (576, 1), 0) % 192 < 64, QSCALE, 1.0)
 
     def outgoing(g):
@@ -177,8 +230,8 @@
             pltpu.make_async_copy(o_v.at[g], o_out.at[g], local.at[5 + 2 * (g % 3)]),
         ]
 
-    def at(u, k, copies_recv, copies_start=()):
-        @pl.when(u == k)
+    def at(n, k, copies_recv, copies_start=()):
+        @pl.when(n == k)
         def _():
             for copy in copies_recv:
                 copy.wait_recv()
@@ -190,17 +243,28 @@
         par = jnp.where(g == 1, 1, 0)
         middle = jnp.where(g == 2, 1, 0)
 
+        at(u, 1, wp_first[:1], wp_second[:1])
+
         @pl.when(u == 3)
         def _():
             cross_arrived.wait_recv()
             cross_forward.start()
+            start_heads(0)
             cross_forward.wait_recv()
 
-        at(u, 4, [wp_first[0]], [wp_second[0]])
-        at(u, 5, [wp_first[1]], [wp_second[1]])
-        at(u, 6, [wp_first[2]], [wp_second[2]])
+        at(u, 4, wp_first[1:2], wp_second[1:2])
+        at(u, 5, wp_first[2:3], wp_second[2:3])
+
+        @pl.when(u == 6)
+        def _():
+            start_heads(2)
+            start_all(in_first[2:] + back_first)
+
+        at(u, 6, [wo_first], [wo_second])
         at(u, 6, wp_second + [bias_out[1]])
-        at(u, 8, [wo_first], [wo_second])
+        at(u, 7, in_first[:1], in_second[:1])
+        at(u, 8, in_first[1:2], in_second[1:2])
+        at(u, 8, [wo_second], [wo_diag])
 
         @pl.when(h == 0)
         def _():
@@ -226,7 +290,7 @@
                 return 0
 
             lax.fori_loop(0, length // BLK, body, 0)
-            same = (row64 == seg_ref[jnp.where(g == 2, 1, 2 * y)]).astype(F32)
+            same = (row64 == seg_ref[pl.ds(jnp.where(g == 2, 1, 2 * y), 1), :]).astype(F32)
             qa[64:128, :] = same.astype(BF)
             ka[64:128, :] = ((same - 1.0) * BIG).astype(BF)
 
@@ -245,124 +309,28 @@
         lse_ref[g * 3 + h] = m + jnp.log2(total)
         return 0
 
-    for copy in rows_local + [w_local]:
+    for copy in rows_local:
         copy.wait()
     for copy in rows_out:
         copy.wait_recv()
+    start_all([cross_out] + wp_first[1:] + [wo_first] + in_first[:2])
     lax.fori_loop(0, 9, unit, 0)
+    start_heads(1)
     tail = outgoing(1)
-    tail.append(pltpu.make_async_copy(xab, xab_out, local.at[0]))
-    tail.append(pltpu.make_async_copy(w_v.at[1], wpar_out, local.at[1]))
+    tail.append(pltpu.make_async_copy(xab, xab_out, local.at[10]))
+    tail.append(pltpu.make_async_copy(w_v, wts_out, local.at[11]))
     start_all(tail)
-    for i in range(IN_EARLY):
-        wi_first[i].wait_recv()
-        wi_second[i].start()
-    wo_second.wait_recv()
-    wo_diag.start()
-    for i in range(IN_EARLY):
-        wi_second[i].wait_recv()
-        start_all(wi_diag[2 * i : 2 * i + 2])
-    for copy in [bias_out[0], bias_out[2], wo_core, wo_diag] + wi_diag:
+
+    b_out, gain1, shift1, b_back, gain2, shift2 = [v[...].reshape(1, 768) for v in (v0, v1, v2, v3, v4, v5)]
+    own[0].wait()
+    for copy in [wo_core, wo_diag, bias_out[0], bias_out[2]]:
         copy.wait_recv()
-    for copy in outgoing(0) + outgoing(2) + tail:
-        copy.wait()
-    sent = rows_out + [cross_forward] + wp_first + wp_second + bias_out + [wo_first, wo_second, wo_core, wo_diag]
-    for copy in sent + wi_first + wi_second + wi_diag:
-        copy.wait_send()
-
-    @pl.when(mixed)
-    def _():
-        for copy in cross_out:
-            copy.wait_send()
-
-def layer_stats(z):
-    mean = jnp.mean(z, axis=-1, keepdims=True)
-    cen = z - mean
-    var = jnp.mean(cen * cen, axis=-1, keepdims=True)
-    inv = lax.rsqrt(var + EPSILON)
-    return cen * inv, inv
-
-
-def k2(
-    x_ref, cot_ref, vec_ref, bias_ref, biasg_ref, o_ref, wout_ref, woutg_ref, win_ref, wing_ref, wback_ref,
-    out_ref, dz1_ref, do_ref, gf_ref, go_ref, small_ref,
-    ot, wo, wi, wb, h1b, h1t, xh1, inv1, gg, gp, z2, dz2b, dz2t, gsend, rc, ry, send, recv, local,
-):
-    t, d, core, across, diag, side = where_am_i()
-    half = d % 2
-    greet([{"tensor": core}, {"tensor": across}, {"tensor": diag}, {"dp": side}])
-
-    peers = (t, core, across, diag)
-    pending = []
-    for j, dev in enumerate(peers):
-        for i in range(3):
-            middle, blk = block_of(dev, i)
-            for second in (False, True) if j < 2 else (False,):
-                slot = j + 2 if second else j
-                src = o_ref.at[1 if second else 2 * middle, blk]
-                dst = ot.at[i, pl.ds(slot * 192, 192)]
-                sem = recv.at[i * 4 + slot]
-                if j == 0:
-                    copy = pltpu.make_async_copy(src, dst, sem)
-                else:
-                    k = 3 * (j - 1) + i if not second else 9 + i
-                    copy = pltpu.make_async_remote_copy(
-                        src_ref=src, dst_ref=dst, send_sem=send.at[k], recv_sem=sem,
-                        device_id={"tensor": dev}, device_id_type=MESH,
-                    )
-                if second:
-                    cond = middle == 0
-                else:
-                    cond = None if j < 2 else middle == 1
-                if cond is None:
-                    copy.start()
-                else:
-                    pl.when(cond)(copy.start)
-                if j:
-                    pending.append((cond, copy))
-    cp = Copies(send, recv)
-    cp.used = 12
-
-    def lanes(j):
-        return pl.ds(768 * j, 768)
-
-    in_core = cp.new(win_ref, wi.at[:, lanes(1)], tensor=core)
-    in_first, in_second, in_diag, loads_in = [], [], [], [pltpu.make_async_copy(win_ref, wi.at[:, lanes(0)], local.at[4])]
-    for i in range(IN_EARLY, 3):
-        part = half_rows(half, 768, 3, i)
-        in_first.append(cp.new(win_ref.at[part], wi.at[part, lanes(2)], tensor=across))
-        in_second.append(cp.new(wi.at[part, lanes(2)], wi.at[part, lanes(2)], dp=side))
-        for h in range(2):
-            both = half_rows(h, 768, 3, i)
-            in_diag.append(cp.new(wi.at[both, lanes(2)], wi.at[both, lanes(3)], tensor=core))
-    for i in range(IN_EARLY):
-        for h in range(2):
-            part = half_rows(h, 768, 3, i)
-            for k in range(2):
-                loads_in.append(pltpu.make_async_copy(wing_ref.at[k, part], wi.at[part, lanes(2 + k)], local.at[4 + len(loads_in)]))
-    back_core = cp.new(wback_ref, wb.at[lanes(1)], tensor=core)
-    back_first, back_second, back_diag = [], [], []
-    for i in range(3):
-        part = half_rows(half, 768, 3, i)
-        place = half_rows(half, 768, 3, i)
-        place = pl.ds(place.start + 2 * 768, place.size)
-        back_first.append(cp.new(wback_ref.at[part], wb.at[place], tensor=across))
-        back_second.append(cp.new(wb.at[place], wb.at[place], dp=side))
-        for h in range(2):
-            n = h * 384 + i * 128
-            back_diag.append(cp.new(wb.at[pl.ds(2 * 768 + n, 128)], wb.at[pl.ds(3 * 768 + n, 128)], tensor=core))
-    load_b0 = pltpu.make_async_copy(wback_ref, wb.at[lanes(0)], local.at[4 + len(loads_in)])
-    start_all(in_first + [in_core, back_core] + back_first)
-    loads = [pltpu.make_async_copy(wout_ref, wo.at[pl.ds(0, 192)], local.at[0])]
-    loads += [pltpu.make_async_copy(woutg_ref.at[j], wo.at[pl.ds(192 * (j + 1), 192)], local.at[j + 1]) for j in range(3)]
-    start_all(loads + loads_in + [load_b0])
-
-    b_out, gain1, shift1, b_back, gain2, shift2 = [vec_ref[k : k + 1, :] for k in range(6)]
-    for copy in loads:
-        copy.wait()
+    for i in range(2):
+        in_second[i].wait_recv()
+        start_all(in_diag[2 * i : 2 * i + 2])
     for i in range(3):
         for slot in range(4):
-            pltpu.make_async_copy(o_ref.at[0, 0], ot.at[i, pl.ds(slot * 192, 192)], recv.at[i * 4 + slot]).wait()
+            pltpu.make_async_copy(o_v.at[0, 0], ot.at[i, pl.ds(slot * 192, 192)], recv.at[i * 4 + slot]).wait()
 
     def first(i, _):
         rs = pl.ds(pl.multiple_of(i * BLK, BLK), BLK)
@@ -375,28 +343,18 @@
 
     lax.fori_loop(0, 3, first, 0)
     h1t[...] = h1b[...].T
-    for copy in loads_in:
-        copy.wait()
-
-    def at(n, k, copies_recv, copies_start=()):
-        @pl.when(n == k)
-        def _():
-            for copy in copies_recv:
-                copy.wait_recv()
-            start_all(copies_start)
-
-    late = len(in_first)
+    own[1].wait()
 
     def up(n, _):
-        at(n, 2, in_first[:1], in_second[:1])
+        at(n, 1, in_first[2:], in_second[2:])
         at(n, 3, [in_core])
-        if late > 1:
-            at(n, 4, in_first[1:], in_second[1:])
-        at(n, 6, in_second, in_diag)
-        at(n, 7, [back_first[0]], [back_second[0]])
+        at(n, 4, back_first[:1], back_second[:1])
+        at(n, 6, in_second[2:], in_diag[4:])
+        at(n, 7, back_first[1:2], back_second[1:2])
         at(n, 9, in_diag)
-        at(n, 9, [back_first[1]], [back_second[1]])
-        at(n, 11, [back_first[2]], [back_second[2]])
+        at(n, 9, back_second[:1], back_diag[:2])
+        at(n, 10, back_first[2:], back_second[2:])
+        at(n, 11, back_second[1:2], back_diag[2:4])
         cs = pl.ds(pl.multiple_of(n * BLK, BLK), BLK)
         j = n // 3
         low = pl.ds(pl.multiple_of((n % 3) * BLK, BLK), BLK)
@@ -409,20 +367,26 @@
         return 0
 
     lax.fori_loop(0, 12, up, 0)
-    for i in range(3):
-        back_second[i].wait_recv()
-        start_all(back_diag[2 * i : 2 * i + 2])
+    own[2].wait()
     back_core.wait_recv()
-    load_b0.wait()
+
+    def down_near(n, _):
+        cs = pl.ds(pl.multiple_of(n * BLK, BLK), BLK)
+        z2[:, cs] = jnp.dot(gg[:, 0:1536], wb[0:1536, cs], preferred_element_type=F32)
+        return 0
+
+    def down_far(n, _):
+        cs = pl.ds(pl.multiple_of(n * BLK, BLK), BLK)
+        z2[:, cs] += jnp.dot(gg[:, 1536:3072], wb[1536:3072, cs], preferred_element_type=F32)
+        return 0
+
+    lax.fori_loop(0, 3, down_near, 0)
+    back_second[2].wait_recv()
+    start_all(back_diag[4:])
+    own[3].wait()
     for copy in back_diag:
         copy.wait_recv()
-
-    def down(n, _):
-        cs = pl.ds(pl.multiple_of(n * BLK, BLK), BLK)
-        z2[:, cs] = jnp.dot(gg[...], wb[:, cs], preferred_element_type=F32)
-        return 0
-
-    lax.fori_loop(0, 3, down, 0)
+    lax.fori_loop(0, 3, down_far, 0)
 
     def second_norm(i, sums):
         rs = pl.ds(pl.multiple_of(i * BLK, BLK), BLK)
@@ -452,7 +416,7 @@
     def to_core(stage, ch):
         k = base + stage * 3 + ch
         return pltpu.make_async_remote_copy(
-            src_ref=gsend.at[stage, ch], dst_ref=rc.at[stage, ch], send_sem=send.at[k], recv_sem=recv.at[k],
+            src_ref=gsend.at[ch], dst_ref=rc.at[ch], send_sem=send.at[k], recv_sem=recv.at[k],
             device_id={"tensor": core}, device_id_type=MESH,
         )
 
@@ -461,6 +425,13 @@
         return pltpu.make_async_remote_copy(
             src_ref=gf_ref.at[1, ch], dst_ref=ry.at[ch], send_sem=send.at[k], recv_sem=recv.at[k],
             device_id={"tensor": across}, device_id_type=MESH,
+        )
+
+    def to_side(ch):
+        k = base + 9 + ch
+        return pltpu.make_async_remote_copy(
+            src_ref=gf_ref.at[0, ch], dst_ref=rx.at[ch], send_sem=send.at[k], recv_sem=recv.at[k],
+            device_id={"dp": side}, device_id_type=MESH,
         )
 
     def back(m, _):
@@ -478,20 +449,30 @@
 
         @pl.when(m % 2 == 0)
         def _():
-            gsend[stage, ch, 0] = g_in.astype(BF)
-            gsend[stage, ch, 1] = g_back.astype(BF)
+            pl.when(stage == 1)(to_core(0, ch).wait_send)
+            gsend[ch, 0] = g_in.astype(BF)
+            gsend[ch, 1] = g_back.astype(BF)
             to_core(stage, ch).start()
 
         @pl.when(m % 2 == 1)
         def _():
             to_core(stage, ch).wait_recv()
-            gf_ref[1 - stage, ch, 0] = (g_in + rc[stage, ch, 0].astype(F32)).astype(BF)
-            gf_ref[1 - stage, ch, 1] = (g_back + rc[stage, ch, 1].astype(F32)).astype(BF)
+            gf_ref[1 - stage, ch, 0] = (g_in + rc[ch, 0].astype(F32)).astype(BF)
+            gf_ref[1 - stage, ch, 1] = (g_back + rc[ch, 1].astype(F32)).astype(BF)
             pl.when((stage == 0) & (ch < Y_EARLY))(to_across(ch).start)
 
         return 0
 
     lax.fori_loop(0, 12, back, 0)
+
+    def take_y(ch):
+        to_across(ch).wait_recv()
+        for k in range(2):
+            gf_ref[0, ch, k] = (gf_ref[0, ch, k].astype(F32) + ry[ch, k].astype(F32)).astype(BF)
+
+    for ch in range(x_early):
+        take_y(ch)
+        to_side(ch).start()
 
     def into_h(n, _):
         cs = pl.ds(pl.multiple_of(n * BLK, BLK), BLK)
@@ -506,7 +487,7 @@
         xh = xh1[rs, :]
         dxh = dh * gain1
         dz = inv1[rs, :] * (dxh - jnp.mean(dxh, axis=-1, keepdims=True) - xh * jnp.mean(dxh * xh, axis=-1, keepdims=True))
-        dz1_ref[rs, :] = dz
+        z2[rs, :] = dz
         dzb = dz.astype(BF)
         dz2b[rs, :] = dzb
         do_ref[i] = dg(wo[...], dzb, 1, 1).astype(BF)
@@ -517,6 +498,8 @@
         )
 
     s0, s1, s2 = lax.fori_loop(0, 3, first_norm, (zero, zero, zero))
+    dz1_copy = pltpu.make_async_copy(z2, dz1_out, local.at[0])
+    dz1_copy.start()
     small_ref[0:1, :] = s0
     small_ref[1:2, :] = s1
     small_ref[2:3, :] = s2
@@ -529,19 +512,26 @@
     small_ref[6:8, :] = jnp.zeros((2, 768), F32)
     small_ref[12:16, :] = jnp.zeros((4, 768), F32)
 
-    for cond, copy in pending:
-        if cond is None:
-            copy.wait_send()
-        else:
-            pl.when(cond)(copy.wait_send)
-    sent = [in_core, back_core] + in_first + in_second + in_diag + back_first + back_second + back_diag
-    for copy in sent + [to_core(s, ch) for s in range(2) for ch in range(3)]:
+    for group in range(3):
+        for j, cond, copy in heads_to_rows(group):
+            if j:
+                pl.when(cond)(copy.wait_send)
+    sent = rows_out + [cross_out, cross_forward] + wp_first + wp_second + bias_out
+    sent += [wo_first, wo_second, wo_core, wo_diag, in_core, back_core]
+    sent += in_first + in_second + in_diag + back_first + back_second + back_diag
+    for copy in sent + [to_core(1, ch) for ch in range(3)]:
         copy.wait_send()
+    for copy in outgoing(0) + outgoing(2) + tail + [dz1_copy]:
+        copy.wait()
     for ch in range(Y_EARLY):
-        to_across(ch).wait_recv()
+        if ch >= x_early:
+            take_y(ch)
+        to_across(ch).wait_send()
+    for ch in range(x_early):
+        to_side(ch).wait()
         for k in range(2):
-            gf_ref[0, ch, k] = (gf_ref[0, ch, k].astype(F32) + ry[ch, k].astype(F32)).astype(BF)
-        to_across(ch).wait_send()
+            gf_ref[0, ch, k] = (gf_ref[0, ch, k].astype(F32) + rx[ch, k].astype(F32)).astype(BF)
+
 
 def split3(v):
     a = v.astype(BF).astype(F32)
@@ -598,6 +588,9 @@
             return
         self.to_x().wait()
         self.add(self.from_x, self.value)
+        self.begin_z()
+
+    def begin_z(self):
         pl.when(self.where["end"])(lambda: self.to_inner().start())
 
     def after_end(self):
@@ -639,7 +632,7 @@
 
 def k3(
     line,
-    qkv_ref, seg_ref, o_ref, lse_ref, xab_ref, wt_ref, wpar_ref, do_in, dz1_in, gf_ref, go_ref, small_ref,
+    qkv_ref, seg_ref, o_ref, lse_ref, xab_ref, wts_ref, do_in, dz1_in, gf_ref, go_ref, small_ref,
     din_ref, ff_ref, fs_ref, sm_ref,
     dz1_ref, do_ref, dq_s, qa, ka, va, da, dk, dv, sbuf, rcore, rmid, rhalf, hsum,
     fv, fy, fx, fe, fm, sv, so, sy, sx, se, sm, rgo, tv, to, tc, ty, tx, te, tm,
@@ -734,12 +727,16 @@
 
     tiny = Piece(tv, to, ty, tx, te, tm, sm_ref, psend.at[10], precv.at[10], where, fold_small)
     early = 2 * Y_EARLY
+    summed = 2 * X_EARLY if line else 0
     for p in range(early, 6):
         big[p].to_y().start()
     for copy in loads:
         copy.wait()
     for p in range(early):
-        big[p].begin_x()
+        if p < summed:
+            big[p].begin_z()
+        else:
+            big[p].begin_x()
 
     row64 = lax.broadcasted_iota(jnp.int32, (64, length), 0)
 
@@ -763,13 +760,13 @@
             sbuf[1 if middle else 0, rows_of(blk), :] = r.astype(BF)
 
     def into_middle(n, _):
-        keep_or_send(True, n, dg(dq2[:, rows_of(n)], wt_ref[...], 0, 0))
+        keep_or_send(True, n, dg(dq2[:, rows_of(n)], wts_ref[0], 0, 0))
         return 0
 
     dq0, dq1, dq2 = [dq_s.at[g] for g in range(3)]
 
     def into_own(n, _):
-        r = dg(dq0[:, rows_of(n)], wt_ref[...], 0, 0) + dg(dq1[:, rows_of(n)], wpar_ref[...], 0, 0)
+        r = dg(dq0[:, rows_of(n)], wts_ref[0], 0, 0) + dg(dq1[:, rows_of(n)], wts_ref[1], 0, 0)
         keep_or_send(False, n, r)
         return 0
 
@@ -837,7 +834,7 @@
             for blk in range(4):
                 pltpu.make_async_copy(do_in.at[0, pl.ds(0, 192)], do_ref.at[g, blk], landed.at[g * 4 + blk]).wait()
 
-        same = (row64 == seg_ref[jnp.where(g == 2, 1, own_seq)]).astype(F32)
+        same = (row64 == seg_ref[pl.ds(jnp.where(g == 2, 1, own_seq), 1), :]).astype(F32)
         ro = pl.multiple_of(h * 192, 64)
         qh, kh, vh = pl.ds(ro, 64), pl.ds(ro + 64, 64), pl.ds(ro + 128, 64)
         l1, l2, l3 = split3(-lse_ref[g * 3 + h])
@@ -925,6 +922,52 @@
         else:
             pl.when(cond)(copy.wait_send)
 
+def finish(
+    out_in, din_in, ff_in, fs_in, sm,
+    out_o, din_o, gwq, gbq, gwk, gwv, gbv, gwo, gbo, gg1, gs1, gwin, gbin, gwback, gbback, gg2, gs2,
+    out_v, din_v, ff, fs, win_v, wback_v, q_v, wo_v, local,
+):
+    loads = [
+        pltpu.make_async_copy(ff_in, ff, local.at[0]),
+        pltpu.make_async_copy(fs_in, fs, local.at[1]),
+        pltpu.make_async_copy(out_in, out_v, local.at[2]),
+        pltpu.make_async_copy(din_in, din_v, local.at[3]),
+    ]
+    start_all(loads)
+    stores = []
+
+    def store(src, dst):
+        copy = pltpu.make_async_copy(src, dst, local.at[4 + len(stores)])
+        copy.start()
+        stores.append(copy)
+
+    for k, ref in ((0, gbo), (1, gg1), (2, gs1), (8, gbin), (3, gbback), (4, gg2), (5, gs2)):
+        ref[...] = sm[k : k + 1, :].reshape(768)
+    heads = sm[12:13, 0:576]
+    for k, ref in ((0, gbq), (2, gbv)):
+        ref[...] = jnp.concatenate([heads[:, 192 * h + 64 * k : 192 * h + 64 * k + 64] for h in range(3)], axis=1).reshape(192)
+    loads[0].wait()
+    for ch in range(3):
+        cs = slice(ch * BLK, (ch + 1) * BLK)
+        wback_v[cs, :] = ff[2 * ch + 1].T.astype(F32)
+        win_v[:, cs] = ff[2 * ch].astype(F32)
+    store(wback_v, gwback)
+    store(win_v, gwin)
+    loads[2].wait()
+    store(out_v, out_o)
+    loads[3].wait()
+    store(din_v, din_o)
+    loads[1].wait()
+    wo_v[...] = fs[0].astype(F32)
+    store(wo_v, gwo)
+    for k, ref in enumerate((gwq, gwk, gwv)):
+        for h in range(3):
+            q_v[k, 64 * h : 64 * h + 64, :] = fs[1 + h, 64 * k : 64 * k + 64, :].astype(F32)
+        store(q_v.at[k], ref)
+    for copy in stores:
+        copy.wait()
+
+
 def vm(*shape, dtype=BF):
     return pltpu.VMEM(shape, dtype)
 
@@ -946,56 +989,38 @@
     layer_input, segment_ids, w_query, b_query, w_key, w_value, b_value, w_out, b_out, first_gain, first_shift,
     w_in, b_in, w_back, b_back, second_gain, second_shift, cotangent,
 ):
-    seg = segment_ids.reshape(3, 1, 1024)
-    wt = jnp.stack([w_query, w_key, w_value]).reshape(3, 768, 3, 64).transpose(2, 0, 3, 1).reshape(576, 768)
-    zeros = jnp.zeros((192,), F32)
-    heads = jnp.stack([b_query.astype(F32), zeros, b_value.astype(F32)]).reshape(3, 3, 64).transpose(1, 0, 2).reshape(576)
-    bias = jnp.stack([b_in.astype(F32), jnp.concatenate([heads, zeros])])
-    bias = jnp.concatenate([bias, jnp.zeros((6, 768), F32)])
-    vec = jnp.stack([b_out, first_gain, first_shift, b_back, second_gain, second_shift])
-    vec = jnp.concatenate([vec, jnp.zeros((2, 768), F32)])
     dma = pltpu.SemaphoreType.DMA
-
-    qkv, o, lse, xab, wpar, woutg, wing, biasg = pl.pallas_call(
-        k1,
+    qkv, o, lse, xab, wts, out, dz1, do, gf, go, small = pl.pallas_call(
+        partial(forward, line),
         out_shape=(
-            sds(3, 3, 192, 1024), sds(3, 4, 192, BLK), sds(9, 1, 1024, dtype=F32), sds(2, 1024, 768), sds(576, 768),
-            sds(3, 192, 768), sds(2, 768, 768), sds(3, 8, 768, dtype=F32),
-        ),
-        in_specs=[ANY, ANY, VM, VM, ANY, ANY],
-        out_specs=(ANY, ANY, VM, ANY, ANY, ANY, ANY, VM),
-        scratch_shapes=[
-            vm(3, 3, 192, 1024), vm(3, 4, 192, BLK), vm(2, 1024, 768), vm(2, 576, 768), vm(576, 1, dtype=F32),
-            vm(128, 1024), vm(128, 1024), vm(80, 1024), dma((32,)), dma((32,)), dma((10,)),
-        ],
-        compiler_params=params(0),
-        name="attention_forward",
-    )(layer_input, wt, bias, seg, w_out, w_in)
-
-    out, dz1, do, gf, go, small = pl.pallas_call(
-        k2,
-        out_shape=(
+            sds(3, 3, 192, 1024), sds(3, 4, 192, BLK), sds(9, 1, 1024, dtype=F32), sds(2, 1024, 768), sds(2, 576, 768),
             sds(768, 768), sds(768, 768, dtype=F32), sds(3, 768, BLK), sds(2, 3, 2, 768, BLK), sds(4, 192, 768),
             sds(16, 768, dtype=F32),
         ),
-        in_specs=[VM, VM, VM, VM, VM, ANY, ANY, ANY, ANY, ANY, ANY],
-        out_specs=(VM, VM, VM, VM, VM, VM),
+        in_specs=[VM, ANY] + [VM] * 13 + [ANY] * 3,
+        out_specs=(ANY, ANY, VM, ANY, ANY, VM, ANY, VM, VM, VM, VM),
         scratch_shapes=[
-            vm(3, 768, BLK), vm(768, 768), vm(768, 3072), vm(3072, 768),
+            vm(3, 3, 192, 1024), vm(3, 4, 192, BLK), vm(2, 1024, 768), vm(2, 576, 768),
+            vm(8, 768, dtype=F32), vm(3, 8, 768, dtype=F32), vm(576, 1, dtype=F32),
+            vm(128, 1024), vm(128, 1024), vm(80, 1024),
+            vm(768, 768), vm(3, 768, BLK), vm(768, 768), vm(768, 3072), vm(3072, 768),
             vm(768, 768), vm(768, 768), vm(768, 768, dtype=F32), vm(768, 1, dtype=F32), vm(768, 3072), vm(768, 3072),
             vm(768, 768, dtype=F32), vm(768, 768), vm(768, 768),
-            vm(2, 3, 2, 768, BLK), vm(2, 3, 2, 768, BLK), vm(max(Y_EARLY, 1), 2, 768, BLK),
-            dma((48,)), dma((48,)), dma((20,)),
+            vm(3, 2, 768, BLK), vm(3, 2, 768, BLK), vm(max(Y_EARLY, 1), 2, 768, BLK), vm(max(X_EARLY, 1), 2, 768, BLK),
+            dma((72,)), dma((72,)), dma((16,)),
         ],
-        compiler_params=params(1),
-        name="feed_forward",
-    )(layer_input, cotangent, vec, bias, biasg, o, w_out, woutg, w_in, wing, w_back)
+        compiler_params=params(0),
+        name="forward_and_feed_forward",
+    )(
+        layer_input, cotangent, w_query.T, w_key.T, w_value.T, b_query, b_value, b_in,
+        b_out, first_gain, first_shift, b_back, second_gain, second_shift, segment_ids, w_out, w_in, w_back,
+    )
 
     piece, slab, tiny = vm(6, 768, BLK), vm(4, 192, 768), vm(16, 768, dtype=F32)
     din, ff, fs, sm = pl.pallas_call(
         partial(k3, line),
         out_shape=(sds(768, 768), sds(6, 768, BLK), sds(4, 192, 768), sds(16, 768, dtype=F32)),
-        in_specs=[VM, VM, VM, VM, VM, VM, VM, ANY, ANY, ANY, VM, VM],
+        in_specs=[VM, VM, VM, VM, VM, VM, ANY, ANY, ANY, VM, VM],
         out_specs=(VM, VM, VM, VM),
         scratch_shapes=[
             vm(768, 768, dtype=F32),
@@ -1006,21 +1031,32 @@
             tiny, tiny, tiny, tiny, tiny, tiny, tiny,
             dma((11, 5)), dma((11, 5)), dma((17,)), dma((9,)), dma((12,)), dma((7,)),
         ],
-        compiler_params=params(2),
+        compiler_params=params(1),
         name="attention_backward",
-    )(qkv, seg, o, lse, xab, wt, wpar, do, dz1, gf, go, small)
+    )(qkv, segment_ids, o, lse, xab, wts, do, dz1, gf, go, small)
     if not line:
         ff, fs = lax.psum((ff, fs), "dp")
         sm = lax.psum(sm, "dp")
-    ff = ff.astype(F32).reshape(3, 2, 768, BLK)
-    g_in = jnp.concatenate([ff[0, 0], ff[1, 0], ff[2, 0]], axis=1)
-    g_back = jnp.concatenate([ff[0, 1].T, ff[1, 1].T, ff[2, 1].T], axis=0)
-    heads = fs[1:4].astype(F32).reshape(3, 3, 64, 768).transpose(1, 3, 0, 2).reshape(3, 768, 192)
-    bq = sm[12, 0:576].reshape(3, 3, 64).transpose(1, 0, 2).reshape(3, 192)
-    return (
-        out, din, heads[0], bq[0], heads[1], heads[2], bq[2], fs[0].astype(F32),
-        sm[0], sm[1], sm[2], g_in, sm[8], g_back, sm[3], sm[4], sm[5],
-    )
+    row = sds(768, dtype=F32)
+    cols, thin = sds(192, 768, dtype=F32), sds(192, dtype=F32)
+    square = sds(768, 768, dtype=F32)
+    outs = pl.pallas_call(
+        finish,
+        out_shape=(
+            sds(768, 768), sds(768, 768), cols, thin, cols, cols, thin, sds(192, 768, dtype=F32),
+            row, row, row, square, row, square, row, row, row,
+        ),
+        in_specs=[ANY, ANY, ANY, ANY, VM],
+        out_specs=(ANY, ANY, ANY, VM, ANY, ANY, VM, ANY, VM, VM, VM, ANY, VM, ANY, VM, VM, VM),
+        scratch_shapes=[
+            vm(768, 768), vm(768, 768), vm(6, 768, BLK), vm(4, 192, 768), vm(768, 768, dtype=F32), vm(768, 768, dtype=F32),
+            vm(3, 192, 768, dtype=F32), vm(192, 768, dtype=F32), dma((16,)),
+        ],
+        compiler_params=pltpu.CompilerParams(vmem_limit_bytes=62 * 2**20),
+        name="results",
+    )(out, din, ff, fs, sm)
+    return (*outs[:2], outs[2].T, outs[3], outs[4].T, outs[5].T, *outs[6:])
+
 
 def solution(mesh):
     rows = P(("dp", "tensor"), None)

time: 300 us -> 248 us (0.83)
  local copies, waits for them, and re-layouts: 26.5 us -> 0 us
  Pallas kernels: 261 us -> 246 us
  other arithmetic: 9.3 us -> 0 us
    unnamed x15 -> x0, local copies, waits for them, and re-layouts: 8.82 us -> none
    pallas_call x1, Pallas kernels: 126 us -> 119 us  [local_step(): pl.pallas_call(partial(k3, line), out_shape=(sds(768, 768), sds(6, 768, B...]
    pallas_call x2, Pallas kernels: 134 us -> 127 us  [the longest x1 120 us: local_step(): pl.pallas_call(partial(forward, line), out_shape=(sds(3, 3, 192, 1024), s...]
    slice x6 -> x0, local copies, waits for them, and re-layouts: 6.53 us -> none  [the longest x1 1.75 us: local_step(): sm[5]]
    another operation x12 -> x0, local copies, waits for them, and re-layouts: 6.45 us -> none  [the longest x6 4.14 us: local_step(): jnp.stack([b_out, first_gain, first_shift, b_back, second_gain, second_sh...]
    concatenate x2 -> x0, other arithmetic: 4.68 us -> none  [the longest x1 4 us: local_step(): g_in = jnp.concatenate([ff[0, 0], ff[1, 0], ff[2, 0]], axis=1)]
where the time goes in v3:
time: 248 us; the launch traced here: 247 us
  Pallas kernels  246 us (99%)
    pallas_call x1, Pallas kernels, local_step(): pl.pallas_call(partial(forward, line), out_shape=(sds(3, 3, 192, 1024), s...  120 us
    pallas_call x1, Pallas kernels, local_step(): pl.pallas_call(partial(k3, line), out_shape=(sds(768, 768), sds(6, 768, B...  119 us
    pallas_call x1, Pallas kernels, local_step(): pl.pallas_call(finish, out_shape=(sds(768, 768), sds(768, 768), cols, thi...  7.26 us

profile of v3, /device:TPU:4, one launch (start us, length us, event | category | flops | bytes accessed | tf_op | source)
XLA Modules:
  0.0 247.2 jit_solution(12453541667602533277)
XLA Ops:
  0.7 120.0 %forward_and_feed_forward.1 = (bf16[3,3,192,1024]{3,2,1,0:T(8,128)(2,1)}, bf16[3,4,192,256]{3,2,1,0:T(8,128)(2,1)}, f32[9,1,1024]{2,1,0:T(1,128)}, bf16[2,1024,7...) custom-call(bf16[768,768]{1,0:T(8,128)(2,1)} %x_ref.1, ...), custom_call_target="tpu_custom_call" | custom-call | tf_op jit(solution)/shard_map/forward_and_feed_forward/pallas_call | solution.py:993
  120.7 119.1 %attention_backward.1 = (bf16[768,768]{1,0:T(8,128)(2,1)}, bf16[6,768,256]{2,1,0:T(8,128)(2,1)}, bf16[4,192,768]{2,1,0:T(8,128)(2,1)}, f32[16,768]{1,0:T(8,128)}) custom-call(bf16[3,3,192,1024]{3,2,1,0:T(8,128)(2,1)} %get-tuple-element.50.qkv_ref, s32[3,1024]{1,0:T(4,128)} %seg_ref.3, bf16[3,4,192,256]{3,2,1,0:T(8,128)(2,1)} %get-tuple-element.51.o_ref, ...), custom_call_target="tpu_custom_call" | custom-call | tf_op jit(solution)/shard_map/attention_backward/pallas_call | solution.py:1020
  239.8 7.3 %results.1 = (bf16[768,768]{1,0:T(8,128)(2,1)}, bf16[768,768]{1,0:T(8,128)(2,1)}, f32[192,768]{1,0:T(8,128)}, f32[192]{0:T(256)}, f32[192,768]{1,0:T(8,128)}, /*...) custom-call(bf16[768,768]{1,0:T(8,128)(2,1)} %get-tuple-element.49.o, ...), custom_call_target="tpu_custom_call" | custom-call | tf_op jit(solution)/shard_map/results/pallas_call | solution.py:1043

commit v4 on v3

--- a/solution.py
+++ b/solution.py
@@ -17,24 +17,55 @@
 LOG2E = 1.0 / math.log(2.0)
 QSCALE = HEAD_DIM ** (-0.5) * LOG2E
 BLK = 256
-Y_EARLY = 2
+Y_EARLY = 3
 X_EARLY = 1
-UNIT_STEPS = {
-    2: (("after_end", 0), ("after_x", 2), ("after_y", 4)),
-    4: (("after_end", 1), ("after_mate", 0), ("after_x", 3), ("after_y", 5)),
-    5: (("after_end", 2),),
-    6: (("after_mate", 1), ("after_x", 4)),
-    7: (("after_end", 3),),
-    8: (("after_mate", 2), ("after_x", 5), ("after_end", 4)),
+SPLIT = (2, 3, 4, 5)
+STEPS = {
+    3: (("after_end", "p0"), ("after_x", "p1"),),
+    4: (("after_x", "p2"), ("after_y", "w0"),),
+    6: (("after_y", "p3"),),
+    7: (("after_mate", "p0"), ("after_end", "p1"), ("after_x", "w0"),),
+    8: (("after_end", "p2"), ("after_y", "w1"),),
+    9: (("after_x", "p3"),),
+    10: (("after_end", "w0"),),
+    11: (("after_mate", "p1"), ("after_x", "w1"), ("after_y", "p4"),),
+    12: (("after_mate", "p2"), ("after_end", "p3"),),
+    13: (("after_y", "w2"),),
+    14: (("after_mate", "w0"), ("after_end", "w1"), ("after_x", "p4"),),
+    16: (("after_mate", "p3"), ("after_x", "w2"), ("after_y", "p5"),),
+    17: (("after_end", "p4"),),
 }
-TAIL_INPUT = 4
+FIRST_TAIL = (
+    ("after_mate", "w1"),
+    ("after_x", "p5"),
+    ("after_y", "w3"),
+)
+TAIL_INPUT = 14
 TAIL_STEPS = (
-    ("after_y", "w0"), ("after_y", "w1"), ("after_mate", "p3"), ("after_end", "p5"), ("after_y", "w2"),
-    ("after_x", "w0"), ("after_mate", "p4"), ("after_x", "w1"), ("after_y", "w3"), ("after_y", "t"),
-    ("after_end", "w0"), ("after_mate", "p5"), ("after_x", "w2"), ("after_end", "w1"), ("after_mate", "w0"),
-    ("after_x", "w3"), ("after_x", "t"), ("after_end", "w2"), ("after_mate", "w1"),
-    ("after_end", "w3"), ("after_end", "t"), ("after_mate", "w2"),
-    ("after_mate", "w3"), ("after_mate", "t"),
+    ("after_y", "w4"),
+    ("after_y", "w5"),
+    ("after_final", "p2"),
+    ("after_end", "w2"),
+    ("after_mate", "p4"),
+    ("after_final", "p3"),
+    ("after_y", "t"),
+    ("after_x", "w3"),
+    ("after_end", "p5"),
+    ("after_x", "w4"),
+    ("after_end", "w3"),
+    ("after_x", "w5"),
+    ("after_mate", "w2"),
+    ("after_end", "w4"),
+    ("after_end", "w5"),
+    ("after_final", "p4"),
+    ("after_mate", "p5"),
+    ("after_mate", "w3"),
+    ("after_x", "t"),
+    ("after_mate", "w4"),
+    ("after_mate", "w5"),
+    ("after_end", "t"),
+    ("after_final", "p5"),
+    ("after_mate", "t"),
 )
 
 
@@ -104,8 +135,8 @@
     line,
     x_ref, cot_in, wq_ref, wk_ref, wv_ref, bq_ref, bv_ref, bin_ref, v0, v1, v2, v3, v4, v5, seg_ref,
     wout_ref, win_ref, wback_ref,
-    qkv_out, o_out, lse_ref, xab_out, wts_out, out_ref, dz1_out, do_ref, gf_ref, go_ref, small_ref,
-    qkv, o_v, xab, w_v, bias_ref, biasg_ref, bcol, qa, ka, va,
+    qkv_out, o_out, lse_ref, xab_out, wts_out, out_out, dz1_out, do_out, gf_out, go_out, small_ref,
+    out_ref, do_ref, gf_ref, go_ref, qkv, o_v, xab, w_v, bias_ref, biasg_ref, bcol, qa, ka, va,
     cot_ref, ot, wo, wi, wb, h1b, h1t, xh1, inv1, gg, gp, z2, dz2b, dz2t, gsend, rc, ry, rx, send, recv, local,
 ):
     length = 1024
@@ -409,6 +440,8 @@
     small_ref[3:4, :] = s3
     small_ref[4:5, :] = s4
     small_ref[5:6, :] = s5
+    out_copy = pltpu.make_async_copy(out_ref, out_out, local.at[16])
+    out_copy.start()
     dz2t[...] = dz2b[...].T
 
     base = cp.used
@@ -420,17 +453,17 @@
             device_id={"tensor": core}, device_id_type=MESH,
         )
 
-    def to_across(ch):
-        k = base + 6 + ch
+    def to_across(p):
+        k = base + 6 + p
         return pltpu.make_async_remote_copy(
-            src_ref=gf_ref.at[1, ch], dst_ref=ry.at[ch], send_sem=send.at[k], recv_sem=recv.at[k],
+            src_ref=gf_ref.at[1, p // 2, p % 2], dst_ref=ry.at[p], send_sem=send.at[k], recv_sem=recv.at[k],
             device_id={"tensor": across}, device_id_type=MESH,
         )
 
-    def to_side(ch):
-        k = base + 9 + ch
+    def to_side(p):
+        k = base + 12 + p
         return pltpu.make_async_remote_copy(
-            src_ref=gf_ref.at[0, ch], dst_ref=rx.at[ch], send_sem=send.at[k], recv_sem=recv.at[k],
+            src_ref=gf_ref.at[0, p // 2, p % 2], dst_ref=rx.at[p], send_sem=send.at[k], recv_sem=recv.at[k],
             device_id={"dp": side}, device_id_type=MESH,
         )
 
@@ -459,20 +492,28 @@
             to_core(stage, ch).wait_recv()
             gf_ref[1 - stage, ch, 0] = (g_in + rc[ch, 0].astype(F32)).astype(BF)
             gf_ref[1 - stage, ch, 1] = (g_back + rc[ch, 1].astype(F32)).astype(BF)
-            pl.when((stage == 0) & (ch < Y_EARLY))(to_across(ch).start)
+            for p in range(Y_EARLY):
+                pl.when((stage == 0) & (ch == p // 2))(to_across(p).start)
 
         return 0
 
     lax.fori_loop(0, 12, back, 0)
 
-    def take_y(ch):
-        to_across(ch).wait_recv()
-        for k in range(2):
-            gf_ref[0, ch, k] = (gf_ref[0, ch, k].astype(F32) + ry[ch, k].astype(F32)).astype(BF)
-
-    for ch in range(x_early):
-        take_y(ch)
-        to_side(ch).start()
+    def gf_copy(p):
+        k = (0, p // 2, p % 2)
+        return pltpu.make_async_copy(gf_ref.at[k], gf_out.at[k], local.at[18 + p])
+
+    gf_other = pltpu.make_async_copy(gf_ref.at[1], gf_out.at[1], local.at[17])
+    start_all([gf_other] + [gf_copy(p) for p in range(Y_EARLY, 6)])
+
+    def take(p, arrived):
+        k = (0, p // 2, p % 2)
+        gf_ref[k] = (gf_ref[k].astype(F32) + arrived[p].astype(F32)).astype(BF)
+
+    for p in range(x_early):
+        to_across(p).wait_recv()
+        take(p, ry)
+        to_side(p).start()
 
     def into_h(n, _):
         cs = pl.ds(pl.multiple_of(n * BLK, BLK), BLK)
@@ -499,7 +540,8 @@
 
     s0, s1, s2 = lax.fori_loop(0, 3, first_norm, (zero, zero, zero))
     dz1_copy = pltpu.make_async_copy(z2, dz1_out, local.at[0])
-    dz1_copy.start()
+    do_copy = pltpu.make_async_copy(do_ref, do_out, local.at[1])
+    start_all([dz1_copy, do_copy])
     small_ref[0:1, :] = s0
     small_ref[1:2, :] = s1
     small_ref[2:3, :] = s2
@@ -509,6 +551,8 @@
         acc += jnp.dot(ot[1, rows, :], dz2b[BLK : 2 * BLK, :], preferred_element_type=F32)
         acc += jnp.dot(ot[2, rows, :], dz2b[2 * BLK : 3 * BLK, :], preferred_element_type=F32)
         go_ref[j] = acc.astype(BF)
+    go_copy = pltpu.make_async_copy(go_ref, go_out, local.at[2])
+    go_copy.start()
     small_ref[6:8, :] = jnp.zeros((2, 768), F32)
     small_ref[12:16, :] = jnp.zeros((4, 768), F32)
 
@@ -521,16 +565,21 @@
     sent += in_first + in_second + in_diag + back_first + back_second + back_diag
     for copy in sent + [to_core(1, ch) for ch in range(3)]:
         copy.wait_send()
-    for copy in outgoing(0) + outgoing(2) + tail + [dz1_copy]:
+    for copy in outgoing(0) + outgoing(2) + tail + [dz1_copy, do_copy, out_copy, gf_other] + [gf_copy(p) for p in range(Y_EARLY, 6)]:
         copy.wait()
-    for ch in range(Y_EARLY):
-        if ch >= x_early:
-            take_y(ch)
-        to_across(ch).wait_send()
-    for ch in range(x_early):
-        to_side(ch).wait()
-        for k in range(2):
-            gf_ref[0, ch, k] = (gf_ref[0, ch, k].astype(F32) + rx[ch, k].astype(F32)).astype(BF)
+    for p in range(Y_EARLY):
+        if p >= x_early:
+            to_across(p).wait_recv()
+            take(p, ry)
+            gf_copy(p).start()
+        to_across(p).wait_send()
+    for p in range(x_early):
+        to_side(p).wait()
+        take(p, rx)
+        gf_copy(p).start()
+    for p in range(Y_EARLY):
+        gf_copy(p).wait()
+    go_copy.wait()
 
 
 def split3(v):
@@ -540,10 +589,20 @@
 
 
 class Piece:
-    def __init__(self, value, other, from_y, from_x, from_end, from_mate, final, send, recv, where, fold=None):
+    def __init__(self, value, other, from_y, from_x, from_end, from_mate, final, send, recv, where, fold=None, split=False):
         self.value, self.other, self.final = value, other, final
         self.from_y, self.from_x, self.from_end, self.from_mate = from_y, from_x, from_end, from_mate
         self.send, self.recv, self.where, self.fold = send, recv, where, fold
+        self.split = split
+
+    def part(self, ref, which):
+        if not self.split:
+            return ref
+        n = 768 // 2
+        return ref.at[pl.ds(pl.multiple_of(which * n, n), n)]
+
+    def mine(self, ref):
+        return self.part(ref, self.where["half"])
 
     def copy(self, stage, src, dst, **device):
         return pltpu.make_async_remote_copy(
@@ -555,19 +614,27 @@
         return self.copy(0, self.other, self.from_y, tensor=self.where["across"])
 
     def to_x(self):
-        return self.copy(1, self.value, self.from_x, dp=self.where["side"])
+        away = 1 - self.where["half"]
+        return self.copy(1, self.part(self.value, away), self.part(self.from_x, away), dp=self.where["side"])
 
     def to_inner(self):
-        return self.copy(2, self.value, self.from_end, dp=self.where["pair"])
+        return self.copy(2, self.mine(self.value), self.mine(self.from_end), dp=self.where["pair"])
 
     def to_mate(self):
-        return self.copy(3, self.value, self.from_mate, dp=self.where["mate"])
+        return self.copy(3, self.mine(self.value), self.mine(self.from_mate), dp=self.where["mate"])
 
     def to_end(self):
-        return self.copy(4, self.final, self.final, dp=self.where["pair"])
+        return self.copy(4, self.mine(self.final), self.mine(self.final), dp=self.where["pair"])
+
+    def to_side(self):
+        return self.copy(5, self.mine(self.final), self.mine(self.final), dp=self.where["side"])
 
     def add(self, arrived, into):
         into[...] = (self.value[...].astype(F32) + arrived[...].astype(F32)).astype(into.dtype)
+
+    def add_mine(self, arrived, into):
+        total = self.mine(self.value)[...].astype(F32) + self.mine(arrived)[...].astype(F32)
+        self.mine(into)[...] = total.astype(into.dtype)
 
     def after_y(self):
         self.to_y().wait_recv()
@@ -587,7 +654,7 @@
         if not self.where["line"]:
             return
         self.to_x().wait()
-        self.add(self.from_x, self.value)
+        self.add_mine(self.from_x, self.value)
         self.begin_z()
 
     def begin_z(self):
@@ -600,7 +667,7 @@
         @pl.when(self.where["inner"])
         def _():
             self.to_inner().wait_recv()
-            self.add(self.from_end, self.value)
+            self.add_mine(self.from_end, self.value)
             self.to_mate().start()
 
     def after_mate(self):
@@ -610,8 +677,19 @@
         @pl.when(self.where["inner"])
         def _():
             self.to_mate().wait_recv()
-            self.add(self.from_mate, self.final)
+            self.add_mine(self.from_mate, self.final)
             self.to_end().start()
+            if self.split:
+                self.to_side().start()
+
+    def after_final(self):
+        if not self.where["line"]:
+            return
+
+        @pl.when(self.where["end"])
+        def _():
+            self.to_end().wait_recv()
+            self.to_side().start()
 
     def finish(self, had_y=True):
         if had_y:
@@ -621,7 +699,8 @@
 
         @pl.when(self.where["end"])
         def _():
-            self.to_end().wait_recv()
+            if not self.split:
+                self.to_end().wait_recv()
             self.to_inner().wait_send()
 
         @pl.when(self.where["inner"])
@@ -629,19 +708,22 @@
             self.to_mate().wait_send()
             self.to_end().wait_send()
 
+        if self.split:
+            self.to_side().wait()
+
 
 def k3(
     line,
-    qkv_ref, seg_ref, o_ref, lse_ref, xab_ref, wts_ref, do_in, dz1_in, gf_ref, go_ref, small_ref,
+    qkv_in, seg_ref, o_in, lse_ref, xab_in, wts_in, do_in, dz1_in, gf_ref, go_in, small_ref,
     din_ref, ff_ref, fs_ref, sm_ref,
-    dz1_ref, do_ref, dq_s, qa, ka, va, da, dk, dv, sbuf, rcore, rmid, rhalf, hsum,
+    qkv_ref, o_ref, xab_ref, wts_ref, go_ref, dz1_ref, do_ref, dq_s, qa, ka, va, da, dk, dv, sbuf, rcore, rmid, rhalf, hsum,
     fv, fy, fx, fe, fm, sv, so, sy, sx, se, sm, rgo, tv, to, tc, ty, tx, te, tm,
     psend, precv, send, recv, landed, local,
 ):
     length = 1024
     t, d, core, across, diag, side = where_am_i()
     y, c = t // 2, t % 2
-    where = {"across": across, "side": side, "line": line}
+    where = {"across": across, "side": side, "line": line, "half": d % 2}
     known = [{"tensor": core}, {"tensor": across}, {"tensor": diag}]
     if line:
         z = d // 2
@@ -650,6 +732,14 @@
         where["end"] = (z == 0) | (z == 3)
         where["inner"] = (z == 1) | (z == 2)
         known += [{"dp": side}, {"dp": where["pair"]}]
+    load_go, load_qkv, load_o, load_xab, load_wts, load_dz1 = [
+        pltpu.make_async_copy(src, dst, local.at[6 + k])
+        for k, (src, dst) in enumerate((
+            (go_in, go_ref), (qkv_in, qkv_ref), (o_in, o_ref), (xab_in, xab_ref), (wts_in, wts_ref), (dz1_in, dz1_ref),
+        ))
+    ]
+    loads = [pltpu.make_async_copy(gf_ref.at[0, p // 2, p % 2], fv.at[p], local.at[p]) for p in range(6)]
+    start_all([load_go] + loads[:Y_EARLY] + [load_qkv, load_o] + loads[Y_EARLY:] + [load_xab, load_wts, load_dz1])
     barrier = pltpu.get_barrier_semaphore()
     for dev in known:
         pl.semaphore_signal(barrier, inc=1, device_id=dev, device_id_type=MESH)
@@ -694,12 +784,9 @@
                 pl.when(cond)(copy.start)
             pending.append((cond, copy))
 
-    loads = [pltpu.make_async_copy(gf_ref.at[0, p // 2, p % 2], fv.at[p], local.at[p]) for p in range(6)]
-    loads.append(pltpu.make_async_copy(dz1_in, dz1_ref, local.at[6]))
-    start_all(loads)
     go_core = [
         pltpu.make_async_remote_copy(
-            src_ref=go_ref.at[2 * k + 1], dst_ref=rgo.at[k], send_sem=send.at[9 + k], recv_sem=recv.at[6 + k],
+            src_ref=go_in.at[2 * k + 1], dst_ref=rgo.at[k], send_sem=send.at[9 + k], recv_sem=recv.at[6 + k],
             device_id={"tensor": core}, device_id_type=MESH,
         )
         for k in range(2)
@@ -711,13 +798,13 @@
     start_all(go_core + [small_core])
     big = [
         Piece(fv.at[p], gf_ref.at[1, p // 2, p % 2], fy.at[p], fx.at[p], fe.at[p], fm.at[p], ff_ref.at[p],
-              psend.at[p], precv.at[p], where)
+              psend.at[p], precv.at[p], where, split=line and p in SPLIT)
         for p in range(6)
     ]
+    places = [(p, slice(0, 192)) for p in range(3)] + [(3, slice(64 * k, 64 * k + 64)) for k in range(3)]
     thin = [
-        Piece(sv.at[p], so.at[p], sy.at[p], sx.at[p], se.at[p], sm.at[p], fs_ref.at[p],
-              psend.at[6 + p], precv.at[6 + p], where)
-        for p in range(4)
+        Piece(*[ref.at[p, rows] for ref in (sv, so, sy, sx, se, sm, fs_ref)], psend.at[6 + i], precv.at[6 + i], where)
+        for i, (p, rows) in enumerate(places)
     ]
 
     def fold_small(piece):
@@ -725,11 +812,16 @@
         add = jnp.concatenate([got[0:8], got[10:11], jnp.zeros((3, 768), F32), got[13:14], jnp.zeros((3, 768), F32)])
         tv[...] = tv[...] + add
 
-    tiny = Piece(tv, to, ty, tx, te, tm, sm_ref, psend.at[10], precv.at[10], where, fold_small)
-    early = 2 * Y_EARLY
-    summed = 2 * X_EARLY if line else 0
-    for p in range(early, 6):
-        big[p].to_y().start()
+    tiny = Piece(tv, to, ty, tx, te, tm, sm_ref, psend.at[12], precv.at[12], where, fold_small)
+    early = Y_EARLY
+    summed = X_EARLY if line else 0
+    load_go.wait()
+    for copy in go_core:
+        copy.wait_recv()
+    sv[0] = (go_ref[0].astype(F32) + rgo[0].astype(F32)).astype(BF)
+    so[0] = (go_ref[2].astype(F32) + rgo[1].astype(F32)).astype(BF)
+    thin[0].to_y().start()
+    big[3].to_y().start()
     for copy in loads:
         copy.wait()
     for p in range(early):
@@ -738,6 +830,9 @@
         else:
             big[p].begin_x()
 
+    named = {"p%d" % p: piece for p, piece in enumerate(big)}
+    named.update({"w%d" % p: piece for p, piece in enumerate(thin)})
+    named["t"] = tiny
     row64 = lax.broadcasted_iota(jnp.int32, (64, length), 0)
 
     def rows_of(blk):
@@ -791,43 +886,30 @@
         ))
 
     def unit(u, _):
-        g = (u // 3 + 1) % 3
-        h = u % 3
+        g = (u % 3 + 1) % 3
+        h = u // 3
 
         @pl.when(u == 1)
         def _():
-            for copy in go_core:
-                copy.wait_recv()
             small_core.wait_recv()
-            sv[0] = (go_ref[0].astype(F32) + rgo[0].astype(F32)).astype(BF)
-            so[0] = (go_ref[2].astype(F32) + rgo[1].astype(F32)).astype(BF)
-            thin[0].to_y().start()
             a, b = small_ref[...], tc[...]
             swapped = jnp.concatenate([b[0:8], b[9:10], b[8:9], b[11:12], b[10:11], b[12:16]])
             tv[...] = a + swapped
 
-        @pl.when(u == 3)
-        def _():
-            for k in range(3):
-                so[1 + k] = jnp.dot(dq_s[1, pl.ds(192 * k, 192), :], xab_ref[0], preferred_element_type=F32).astype(BF)
-                thin[1 + k].to_y().start()
-
-        @pl.when(u == 6)
-        def _():
+        @pl.when(u == 2)
+        def _():
+            big[4].to_y().start()
+
+        @pl.when(u == 4)
+        def _():
+            big[5].to_y().start()
+
+        @pl.when(u == 8)
+        def _():
+            load_wts.wait()
+            load_dz1.wait()
             lax.fori_loop(0, 4, into_middle, 0)
             half_copy.start()
-
-        for k, steps in UNIT_STEPS.items():
-            @pl.when(u == k)
-            def _(steps=steps):
-                for stage, p in steps:
-                    getattr(big[p], stage)()
-
-        @pl.when(u == 7)
-        def _():
-            half_copy.wait_recv()
-            hsum[...] = (sbuf[1, rows_of(far + c), :].astype(F32) + rhalf[...].astype(F32)).astype(BF)
-            far_copy.start()
 
         @pl.when(h == 0)
         def _():
@@ -855,6 +937,12 @@
         dv[...] = jnp.zeros_like(dv)
 
         def chunk(n, _):
+            for k, steps in STEPS.items():
+                @pl.when(2 * u + n == k)
+                def _(steps=steps):
+                    for stage, name in steps:
+                        getattr(named[name], stage)()
+
             cs = pl.ds(pl.multiple_of(n * 512, 512), 512)
             s = jnp.dot(ka[...], qa[:, cs], preferred_element_type=F32)
             p = jnp.exp2(s)
@@ -871,7 +959,18 @@
         dq_s[g, kh, :] = (dk[...] * math.log(2.0)).astype(BF)
         dq_s[g, vh, :] = dv[...].astype(BF)
 
-        @pl.when(u >= 6)
+        @pl.when(g == 1)
+        def _():
+            pl.when(h == 0)(load_xab.wait)
+            so[1 + h] = jnp.dot(dq_s[1, pl.ds(ro, 192), :], xab_ref[0], preferred_element_type=F32).astype(BF)
+
+        for k, pieces in ((0, thin[1:2]), (3, thin[2:3]), (6, thin[3:])):
+            @pl.when(u == k)
+            def _(pieces=pieces):
+                for piece in pieces:
+                    piece.to_y().start()
+
+        @pl.when(g == 0)
         def _():
             rows = pl.ds(ro, 192)
             r = jnp.dot(dq_s[0, rows, :], xab_ref[0], preferred_element_type=F32)
@@ -879,7 +978,14 @@
 
         return 0
 
+    load_qkv.wait()
+    load_o.wait()
     lax.fori_loop(0, 9, unit, 0)
+    for stage, name in FIRST_TAIL:
+        getattr(named[name], stage)()
+    half_copy.wait_recv()
+    hsum[...] = (sbuf[1, rows_of(far + c), :].astype(F32) + rhalf[...].astype(F32)).astype(BF)
+    far_copy.start()
     ones = jnp.ones((8, length), BF)
     tv[12:13, 0:576] = (dg(ones, dq_s[0], 1, 1) + dg(ones, dq_s[2], 1, 1))[0:1]
     tv[13:14, 0:576] = dg(ones, dq_s[1], 1, 1)[0:1]
@@ -889,9 +995,6 @@
     for middle, copy in core_copies:
         copy.start()
 
-    named = {"p%d" % p: piece for p, piece in enumerate(big)}
-    named.update({"w%d" % p: piece for p, piece in enumerate(thin)})
-    named["t"] = tiny
     for k, (stage, name) in enumerate(TAIL_STEPS):
         getattr(named[name], stage)()
         if k == TAIL_INPUT:
@@ -998,16 +1101,17 @@
             sds(16, 768, dtype=F32),
         ),
         in_specs=[VM, ANY] + [VM] * 13 + [ANY] * 3,
-        out_specs=(ANY, ANY, VM, ANY, ANY, VM, ANY, VM, VM, VM, VM),
+        out_specs=(ANY, ANY, VM, ANY, ANY, ANY, ANY, ANY, ANY, ANY, VM),
         scratch_shapes=[
+            vm(768, 768), vm(3, 768, BLK), vm(2, 3, 2, 768, BLK), vm(4, 192, 768),
             vm(3, 3, 192, 1024), vm(3, 4, 192, BLK), vm(2, 1024, 768), vm(2, 576, 768),
             vm(8, 768, dtype=F32), vm(3, 8, 768, dtype=F32), vm(576, 1, dtype=F32),
             vm(128, 1024), vm(128, 1024), vm(80, 1024),
             vm(768, 768), vm(3, 768, BLK), vm(768, 768), vm(768, 3072), vm(3072, 768),
             vm(768, 768), vm(768, 768), vm(768, 768, dtype=F32), vm(768, 1, dtype=F32), vm(768, 3072), vm(768, 3072),
             vm(768, 768, dtype=F32), vm(768, 768), vm(768, 768),
-            vm(3, 2, 768, BLK), vm(3, 2, 768, BLK), vm(max(Y_EARLY, 1), 2, 768, BLK), vm(max(X_EARLY, 1), 2, 768, BLK),
-            dma((72,)), dma((72,)), dma((16,)),
+            vm(3, 2, 768, BLK), vm(3, 2, 768, BLK), vm(max(Y_EARLY, 1), 768, BLK), vm(max(X_EARLY, 1), 768, BLK),
+            dma((80,)), dma((80,)), dma((24,)),
         ],
         compiler_params=params(0),
         name="forward_and_feed_forward",
@@ -1020,16 +1124,17 @@
     din, ff, fs, sm = pl.pallas_call(
         partial(k3, line),
         out_shape=(sds(768, 768), sds(6, 768, BLK), sds(4, 192, 768), sds(16, 768, dtype=F32)),
-        in_specs=[VM, VM, VM, VM, VM, VM, ANY, ANY, ANY, VM, VM],
+        in_specs=[ANY, VM, ANY, VM, ANY, ANY, ANY, ANY, ANY, ANY, VM],
         out_specs=(VM, VM, VM, VM),
         scratch_shapes=[
+            vm(3, 3, 192, 1024), vm(3, 4, 192, BLK), vm(2, 1024, 768), vm(2, 576, 768), vm(4, 192, 768),
             vm(768, 768, dtype=F32),
             vm(3, 4, 192, BLK), vm(3, 576, 1024), vm(128, 1024), vm(1024, 128), vm(1024, 128), vm(128, 1024),
             vm(64, 1024, dtype=F32), vm(64, 1024, dtype=F32), vm(2, 1024, 768),
             vm(3, BLK, 768), vm(2, BLK, 768), vm(BLK, 768), vm(BLK, 768),
             piece, piece, piece, piece, piece, slab, slab, slab, slab, slab, slab, vm(2, 192, 768),
             tiny, tiny, tiny, tiny, tiny, tiny, tiny,
-            dma((11, 5)), dma((11, 5)), dma((17,)), dma((9,)), dma((12,)), dma((7,)),
+            dma((13, 6)), dma((13, 6)), dma((17,)), dma((9,)), dma((12,)), dma((12,)),
         ],
         compiler_params=params(1),
         name="attention_backward",

time: 248 us -> 222 us (0.90)
  Pallas kernels: 246 us -> 221 us
    pallas_call x1, Pallas kernels: 119 us -> 104 us  [local_step(): pl.pallas_call(partial(k3, line), out_shape=(sds(768, 768), sds(6, 768, B...]
    pallas_call x1, Pallas kernels: 120 us -> 109 us  [local_step(): pl.pallas_call(partial(forward, line), out_shape=(sds(3, 3, 192, 1024), s...]
where the time goes in v4:
time: 222 us; the launch traced here: 221 us
  Pallas kernels  221 us (100%)
    pallas_call x1, Pallas kernels, local_step(): pl.pallas_call(partial(forward, line), out_shape=(sds(3, 3, 192, 1024), s...  109 us
    pallas_call x1, Pallas kernels, local_step(): pl.pallas_call(partial(k3, line), out_shape=(sds(768, 768), sds(6, 768, B...  104 us
    pallas_call x1, Pallas kernels, local_step(): pl.pallas_call(finish, out_shape=(sds(768, 768), sds(768, 768), cols, thi...  7.26 us

profile of v4, /device:TPU:4, one launch (start us, length us, event | category | flops | bytes accessed | tf_op | source)
XLA Modules:
  0.0 221.4 jit_solution(11971722704896236793)
XLA Ops:
  0.7 109.2 %forward_and_feed_forward.1 = (bf16[3,3,192,1024]{3,2,1,0:T(8,128)(2,1)}, bf16[3,4,192,256]{3,2,1,0:T(8,128)(2,1)}, f32[9,1,1024]{2,1,0:T(1,128)}, bf16[2,1024,7...) custom-call(bf16[768,768]{1,0:T(8,128)(2,1)} %x_ref.1, ...), custom_call_target="tpu_custom_call" | custom-call | tf_op jit(solution)/shard_map/forward_and_feed_forward/pallas_call | solution.py:1096
  109.8 104.2 %attention_backward.1 = (bf16[768,768]{1,0:T(8,128)(2,1)}, bf16[6,768,256]{2,1,0:T(8,128)(2,1)}, bf16[4,192,768]{2,1,0:T(8,128)(2,1)}, f32[16,768]{1,0:T(8,128)}) custom-call(bf16[3,3,192,1024]{3,2,1,0:T(8,128)(2,1)} %get-tuple-element.50.qkv_in, s32[3,1024]{1,0:T(4,128)} %seg_ref.3, bf16[3,4,192,256]{3,2,1,0:T(8,128)(2,1)} %get-tuple-element.51.o_in, ...), custom_call_target="tpu_custom_call" | custom-call | tf_op jit(solution)/shard_map/attention_backward/pallas_call | solution.py:1124
  214.0 7.3 %results.1 = (bf16[768,768]{1,0:T(8,128)(2,1)}, bf16[768,768]{1,0:T(8,128)(2,1)}, f32[192,768]{1,0:T(8,128)}, f32[192]{0:T(256)}, f32[192,768]{1,0:T(8,128)}, /*...) custom-call(bf16[768,768]{1,0:T(8,128)(2,1)} %get-tuple-element.49.o, ...), custom_call_target="tpu_custom_call" | custom-call | tf_op jit(solution)/shard_map/results/pallas_call | solution.py:1148

commit v5 on v4

--- a/solution.py
+++ b/solution.py
@@ -20,52 +20,66 @@
 Y_EARLY = 3
 X_EARLY = 1
 SPLIT = (2, 3, 4, 5)
+AY, AX, AE, AM, AF = "after_y", "after_x", "after_end", "after_mate", "after_final"
 STEPS = {
-    3: (("after_end", "p0"), ("after_x", "p1"),),
-    4: (("after_x", "p2"), ("after_y", "w0"),),
-    6: (("after_y", "p3"),),
-    7: (("after_mate", "p0"), ("after_end", "p1"), ("after_x", "w0"),),
-    8: (("after_end", "p2"), ("after_y", "w1"),),
-    9: (("after_x", "p3"),),
-    10: (("after_end", "w0"),),
-    11: (("after_mate", "p1"), ("after_x", "w1"), ("after_y", "p4"),),
-    12: (("after_mate", "p2"), ("after_end", "p3"),),
-    13: (("after_y", "w2"),),
-    14: (("after_mate", "w0"), ("after_end", "w1"), ("after_x", "p4"),),
-    16: (("after_mate", "p3"), ("after_x", "w2"), ("after_y", "p5"),),
-    17: (("after_end", "p4"),),
+    3: ((AE, 0), (AX, 1),),
+    4: ((AY, 6),),
+    5: ((AX, 2),),
+    7: ((AM, 0), (AE, 1), (AX, 6), (AY, 3),),
+    9: ((AE, 2), (AY, 7),),
+    10: ((AX, 3),),
+    11: ((AM, 1), (AE, 6),),
+    12: ((AX, 7), (AY, 4),),
+    13: ((AM, 2), (AE, 3),),
+    14: ((AY, 8),),
+    15: ((AM, 6), (AE, 7), (AX, 4),),
+    16: ((AM, 3),),
+    17: ((AX, 8), (AY, 5),),
 }
 FIRST_TAIL = (
-    ("after_mate", "w1"),
-    ("after_x", "p5"),
-    ("after_y", "w3"),
+    (AE, 4),
+    (AM, 7),
+    (AY, 9),
 )
-TAIL_INPUT = 14
+TAIL_INPUT = 20
 TAIL_STEPS = (
-    ("after_y", "w4"),
-    ("after_y", "w5"),
-    ("after_final", "p2"),
-    ("after_end", "w2"),
-    ("after_mate", "p4"),
-    ("after_final", "p3"),
-    ("after_y", "t"),
-    ("after_x", "w3"),
-    ("after_end", "p5"),
-    ("after_x", "w4"),
-    ("after_end", "w3"),
-    ("after_x", "w5"),
-    ("after_mate", "w2"),
-    ("after_end", "w4"),
-    ("after_end", "w5"),
-    ("after_final", "p4"),
-    ("after_mate", "p5"),
-    ("after_mate", "w3"),
-    ("after_x", "t"),
-    ("after_mate", "w4"),
-    ("after_mate", "w5"),
-    ("after_end", "t"),
-    ("after_final", "p5"),
-    ("after_mate", "t"),
+    (AY, 10),
+    (AY, 11),
+    (AY, 12),
+    (AY, 13),
+    (AY, 14),
+    (AF, 2),
+    (AX, 5),
+    (AY, -1),
+    (AX, 9),
+    (AF, 3),
+    (AE, 8),
+    (AX, 10),
+    (AM, 4),
+    (AX, 11),
+    (AX, 12),
+    (AX, 13),
+    (AE, 5),
+    (AX, 14),
+    (AE, 9),
+    (AE, 10),
+    (AE, 11),
+    (AM, 8),
+    (AE, 12),
+    (AE, 13),
+    (AX, -1),
+    (AF, 4),
+    (AE, 14),
+    (AM, 5),
+    (AE, -1),
+    (AM, 9),
+    (AM, 10),
+    (AM, 11),
+    (AM, 12),
+    (AM, 13),
+    (AM, 14),
+    (AM, -1),
+    (AF, 5),
 )
 
 
@@ -143,6 +157,8 @@
     t, d, core, across, diag, side = where_am_i()
     y, c = t // 2, t % 2
     half = d % 2
+    zbit = (d // 2) % 2
+    pair = d + 2 - 4 * zbit
     x_early = X_EARLY if line else 0
 
     rows_out, rows_local = [], []
@@ -174,7 +190,7 @@
         parts += [bq[:, 64 * h : 64 * h + 64], jnp.zeros((1, 64), F32), bv[:, 64 * h : 64 * h + 64]]
     bias_ref[1:2, 0:576] = jnp.concatenate(parts, axis=1)
 
-    greet([{"tensor": core}, {"tensor": across}, {"tensor": diag}, {"dp": side}])
+    greet([{"tensor": core}, {"tensor": across}, {"tensor": diag}, {"dp": side}, {"dp": pair}])
 
     mixed = (t == 1) | (t == 2)
     k_out = jnp.where(mixed, 0, 1)
@@ -209,11 +225,16 @@
 
     in_core = cp.new(win_ref, wi.at[:, lanes(1)], tensor=core)
     back_core = cp.new(wback_ref, wb.at[lanes(1)], tensor=core)
-    in_first, in_second, in_diag, back_first, back_second, back_diag = [], [], [], [], [], []
+    in_first, in_second, in_third, in_diag, back_first, back_second, back_diag = [], [], [], [], [], [], []
     for i in range(3):
         part = half_rows(half, 768, 3, i)
-        in_first.append(cp.new(win_ref.at[part], wi.at[part, lanes(2)], tensor=across))
-        in_second.append(cp.new(wi.at[part, lanes(2)], wi.at[part, lanes(2)], dp=side))
+        first_part = part
+        if i < 2:
+            z_part = half_rows(zbit, 768, 3, i)
+            first_part = pl.ds(pl.multiple_of(z_part.start + 64 * half, 64), 64)
+            in_third.append(cp.new(wi.at[z_part, lanes(2)], wi.at[z_part, lanes(2)], dp=pair))
+        in_first.append(cp.new(win_ref.at[first_part], wi.at[first_part, lanes(2)], tensor=across))
+        in_second.append(cp.new(wi.at[first_part, lanes(2)], wi.at[first_part, lanes(2)], dp=side))
         place = pl.ds(part.start + 2 * 768, part.size)
         back_first.append(cp.new(wback_ref.at[part], wb.at[place], tensor=across))
         back_second.append(cp.new(wb.at[place], wb.at[place], dp=side))
@@ -293,8 +314,8 @@
 
         at(u, 6, [wo_first], [wo_second])
         at(u, 6, wp_second + [bias_out[1]])
-        at(u, 7, in_first[:1], in_second[:1])
-        at(u, 8, in_first[1:2], in_second[1:2])
+        at(u, 7, in_first[:2], in_second[:2])
+        at(u, 8, in_second[:1], in_third[:1])
         at(u, 8, [wo_second], [wo_diag])
 
         @pl.when(h == 0)
@@ -356,9 +377,8 @@
     own[0].wait()
     for copy in [wo_core, wo_diag, bias_out[0], bias_out[2]]:
         copy.wait_recv()
-    for i in range(2):
-        in_second[i].wait_recv()
-        start_all(in_diag[2 * i : 2 * i + 2])
+    in_second[1].wait_recv()
+    in_third[1].start()
     for i in range(3):
         for slot in range(4):
             pltpu.make_async_copy(o_v.at[0, 0], ot.at[i, pl.ds(slot * 192, 192)], recv.at[i * 4 + slot]).wait()
@@ -377,10 +397,10 @@
     own[1].wait()
 
     def up(n, _):
-        at(n, 1, in_first[2:], in_second[2:])
+        at(n, 0, in_first[2:], in_second[2:])
         at(n, 3, [in_core])
-        at(n, 4, back_first[:1], back_second[:1])
-        at(n, 6, in_second[2:], in_diag[4:])
+        at(n, 5, back_first[:1], back_second[:1])
+        at(n, 6, in_third + in_second[2:], in_diag)
         at(n, 7, back_first[1:2], back_second[1:2])
         at(n, 9, in_diag)
         at(n, 9, back_second[:1], back_diag[:2])
@@ -562,7 +582,7 @@
                 pl.when(cond)(copy.wait_send)
     sent = rows_out + [cross_out, cross_forward] + wp_first + wp_second + bias_out
     sent += [wo_first, wo_second, wo_core, wo_diag, in_core, back_core]
-    sent += in_first + in_second + in_diag + back_first + back_second + back_diag
+    sent += in_first + in_second + in_third + in_diag + back_first + back_second + back_diag
     for copy in sent + [to_core(1, ch) for ch in range(3)]:
         copy.wait_send()
     for copy in outgoing(0) + outgoing(2) + tail + [dz1_copy, do_copy, out_copy, gf_other] + [gf_copy(p) for p in range(Y_EARLY, 6)]:
@@ -801,7 +821,7 @@
               psend.at[p], precv.at[p], where, split=line and p in SPLIT)
         for p in range(6)
     ]
-    places = [(p, slice(0, 192)) for p in range(3)] + [(3, slice(64 * k, 64 * k + 64)) for k in range(3)]
+    places = [(p, slice(0, 192)) for p in range(3)] + [(3, slice(32 * k, 32 * k + 32)) for k in range(6)]
     thin = [
         Piece(*[ref.at[p, rows] for ref in (sv, so, sy, sx, se, sm, fs_ref)], psend.at[6 + i], precv.at[6 + i], where)
         for i, (p, rows) in enumerate(places)
@@ -812,7 +832,7 @@
         add = jnp.concatenate([got[0:8], got[10:11], jnp.zeros((3, 768), F32), got[13:14], jnp.zeros((3, 768), F32)])
         tv[...] = tv[...] + add
 
-    tiny = Piece(tv, to, ty, tx, te, tm, sm_ref, psend.at[12], precv.at[12], where, fold_small)
+    tiny = Piece(tv, to, ty, tx, te, tm, sm_ref, psend.at[15], precv.at[15], where, fold_small)
     early = Y_EARLY
     summed = X_EARLY if line else 0
     load_go.wait()
@@ -830,9 +850,7 @@
         else:
             big[p].begin_x()
 
-    named = {"p%d" % p: piece for p, piece in enumerate(big)}
-    named.update({"w%d" % p: piece for p, piece in enumerate(thin)})
-    named["t"] = tiny
+    every = big + thin + [tiny]
     row64 = lax.broadcasted_iota(jnp.int32, (64, length), 0)
 
     def rows_of(blk):
@@ -900,7 +918,7 @@
         def _():
             big[4].to_y().start()
 
-        @pl.when(u == 4)
+        @pl.when(u == 5)
         def _():
             big[5].to_y().start()
 
@@ -941,7 +959,7 @@
                 @pl.when(2 * u + n == k)
                 def _(steps=steps):
                     for stage, name in steps:
-                        getattr(named[name], stage)()
+                        getattr(every[name], stage)()
 
             cs = pl.ds(pl.multiple_of(n * 512, 512), 512)
             s = jnp.dot(ka[...], qa[:, cs], preferred_element_type=F32)
@@ -982,7 +1000,7 @@
     load_o.wait()
     lax.fori_loop(0, 9, unit, 0)
     for stage, name in FIRST_TAIL:
-        getattr(named[name], stage)()
+        getattr(every[name], stage)()
     half_copy.wait_recv()
     hsum[...] = (sbuf[1, rows_of(far + c), :].astype(F32) + rhalf[...].astype(F32)).astype(BF)
     far_copy.start()
@@ -996,7 +1014,7 @@
         copy.start()
 
     for k, (stage, name) in enumerate(TAIL_STEPS):
-        getattr(named[name], stage)()
+        getattr(every[name], stage)()
         if k == TAIL_INPUT:
             for i in range(3):
                 core_copies[i][1].wait_recv()
@@ -1134,7 +1152,7 @@
             vm(3, BLK, 768), vm(2, BLK, 768), vm(BLK, 768), vm(BLK, 768),
             piece, piece, piece, piece, piece, slab, slab, slab, slab, slab, slab, vm(2, 192, 768),
             tiny, tiny, tiny, tiny, tiny, tiny, tiny,
-            dma((13, 6)), dma((13, 6)), dma((17,)), dma((9,)), dma((12,)), dma((12,)),
+            dma((16, 6)), dma((16, 6)), dma((17,)), dma((9,)), dma((12,)), dma((12,)),
         ],
         compiler_params=params(1),
         name="attention_backward",

time: 222 us -> 217 us (0.977); the launches traced: 221 us -> 214 us
  Pallas kernels: 221 us -> 213 us
    pallas_call x1, Pallas kernels: 104 us -> 99.7 us  [local_step(): pl.pallas_call(partial(k3, line), out_shape=(sds(768, 768), sds(6, 768, B...]
    pallas_call x1, Pallas kernels: 109 us -> 106 us  [local_step(): pl.pallas_call(partial(forward, line), out_shape=(sds(3, 3, 192, 1024), s...]
where the time goes in v5:
time: 217 us; the launch traced here: 214 us
  Pallas kernels  213 us (98%)
    pallas_call x1, Pallas kernels, local_step(): pl.pallas_call(partial(forward, line), out_shape=(sds(3, 3, 192, 1024), s...  106 us
    pallas_call x1, Pallas kernels, local_step(): pl.pallas_call(partial(k3, line), out_shape=(sds(768, 768), sds(6, 768, B...  99.7 us
    pallas_call x1, Pallas kernels, local_step(): pl.pallas_call(finish, out_shape=(sds(768, 768), sds(768, 768), cols, thi...  7.26 us

profile of v5, /device:TPU:4, one launch (start us, length us, event | category | flops | bytes accessed | tf_op | source)
XLA Modules:
  0.0 214.2 jit_solution(11070246610952439588)
XLA Ops:
  0.7 106.4 %forward_and_feed_forward.1 = (bf16[3,3,192,1024]{3,2,1,0:T(8,128)(2,1)}, bf16[3,4,192,256]{3,2,1,0:T(8,128)(2,1)}, f32[9,1,1024]{2,1,0:T(1,128)}, bf16[2,1024,7...) custom-call(bf16[768,768]{1,0:T(8,128)(2,1)} %x_ref.1, ...), custom_call_target="tpu_custom_call" | custom-call | tf_op jit(solution)/shard_map/forward_and_feed_forward/pallas_call | solution.py:1114
  107.1 99.7 %attention_backward.1 = (bf16[768,768]{1,0:T(8,128)(2,1)}, bf16[6,768,256]{2,1,0:T(8,128)(2,1)}, bf16[4,192,768]{2,1,0:T(8,128)(2,1)}, f32[16,768]{1,0:T(8,128)}) custom-call(bf16[3,3,192,1024]{3,2,1,0:T(8,128)(2,1)} %get-tuple-element.50.qkv_in, s32[3,1024]{1,0:T(4,128)} %seg_ref.3, bf16[3,4,192,256]{3,2,1,0:T(8,128)(2,1)} %get-tuple-element.51.o_in, ...), custom_call_target="tpu_custom_call" | custom-call | tf_op jit(solution)/shard_map/attention_backward/pallas_call | solution.py:1142
  206.8 7.3 %results.1 = (bf16[768,768]{1,0:T(8,128)(2,1)}, bf16[768,768]{1,0:T(8,128)(2,1)}, f32[192,768]{1,0:T(8,128)}, f32[192]{0:T(256)}, f32[192,768]{1,0:T(8,128)}, /*...) custom-call(bf16[768,768]{1,0:T(8,128)(2,1)} %get-tuple-element.49.o, ...), custom_call_target="tpu_custom_call" | custom-call | tf_op jit(solution)/shard_map/results/pallas_call | solution.py:1166

commit v6 on v5

--- a/solution.py
+++ b/solution.py
@@ -1048,13 +1048,13 @@
     out_o, din_o, gwq, gbq, gwk, gwv, gbv, gwo, gbo, gg1, gs1, gwin, gbin, gwback, gbback, gg2, gs2,
     out_v, din_v, ff, fs, win_v, wback_v, q_v, wo_v, local,
 ):
+    pieces = [pltpu.make_async_copy(ff_in.at[p], ff.at[p], local.at[16 + p]) for p in range(6)]
     loads = [
-        pltpu.make_async_copy(ff_in, ff, local.at[0]),
-        pltpu.make_async_copy(fs_in, fs, local.at[1]),
         pltpu.make_async_copy(out_in, out_v, local.at[2]),
         pltpu.make_async_copy(din_in, din_v, local.at[3]),
+        pltpu.make_async_copy(fs_in, fs, local.at[1]),
     ]
-    start_all(loads)
+    start_all(loads[:1] + pieces + loads[1:])
     stores = []
 
     def store(src, dst):
@@ -1068,17 +1068,18 @@
     for k, ref in ((0, gbq), (2, gbv)):
         ref[...] = jnp.concatenate([heads[:, 192 * h + 64 * k : 192 * h + 64 * k + 64] for h in range(3)], axis=1).reshape(192)
     loads[0].wait()
+    store(out_v, out_o)
     for ch in range(3):
-        cs = slice(ch * BLK, (ch + 1) * BLK)
+        cs = pl.ds(ch * BLK, BLK)
+        pieces[2 * ch].wait()
+        win_v[:, ch * BLK : (ch + 1) * BLK] = ff[2 * ch].astype(F32)
+        pieces[2 * ch + 1].wait()
         wback_v[cs, :] = ff[2 * ch + 1].T.astype(F32)
-        win_v[:, cs] = ff[2 * ch].astype(F32)
-    store(wback_v, gwback)
+        store(wback_v.at[cs], gwback.at[cs])
     store(win_v, gwin)
+    loads[1].wait()
+    store(din_v, din_o)
     loads[2].wait()
-    store(out_v, out_o)
-    loads[3].wait()
-    store(din_v, din_o)
-    loads[1].wait()
     wo_v[...] = fs[0].astype(F32)
     store(wo_v, gwo)
     for k, ref in enumerate((gwq, gwk, gwv)):
@@ -1173,7 +1174,7 @@
         out_specs=(ANY, ANY, ANY, VM, ANY, ANY, VM, ANY, VM, VM, VM, ANY, VM, ANY, VM, VM, VM),
         scratch_shapes=[
             vm(768, 768), vm(768, 768), vm(6, 768, BLK), vm(4, 192, 768), vm(768, 768, dtype=F32), vm(768, 768, dtype=F32),
-            vm(3, 192, 768, dtype=F32), vm(192, 768, dtype=F32), dma((16,)),
+            vm(3, 192, 768, dtype=F32), vm(192, 768, dtype=F32), dma((22,)),
         ],
         compiler_params=pltpu.CompilerParams(vmem_limit_bytes=62 * 2**20),
         name="results",

time: 217 us -> 216 us (level)
  no operation moved by 1% of the time
where the time goes in v6:
time: 216 us; the launch traced here: 214 us
  Pallas kernels  213 us (99%)
    pallas_call x1, Pallas kernels, local_step(): pl.pallas_call(partial(forward, line), out_shape=(sds(3, 3, 192, 1024), s...  106 us
    pallas_call x1, Pallas kernels, local_step(): pl.pallas_call(partial(k3, line), out_shape=(sds(768, 768), sds(6, 768, B...  99.7 us
    pallas_call x1, Pallas kernels, local_step(): pl.pallas_call(finish, out_shape=(sds(768, 768), sds(768, 768), cols, thi...  6.88 us

profile of v6, /device:TPU:4, one launch (start us, length us, event | category | flops | bytes accessed | tf_op | source)
XLA Modules:
  0.0 213.8 jit_solution(5504270108352266253)
XLA Ops:
  0.7 106.4 %forward_and_feed_forward.1 = (bf16[3,3,192,1024]{3,2,1,0:T(8,128)(2,1)}, bf16[3,4,192,256]{3,2,1,0:T(8,128)(2,1)}, f32[9,1,1024]{2,1,0:T(1,128)}, bf16[2,1024,7...) custom-call(bf16[768,768]{1,0:T(8,128)(2,1)} %x_ref.1, ...), custom_call_target="tpu_custom_call" | custom-call | tf_op jit(solution)/shard_map/forward_and_feed_forward/pallas_call | solution.py:1115
  107.1 99.7 %attention_backward.1 = (bf16[768,768]{1,0:T(8,128)(2,1)}, bf16[6,768,256]{2,1,0:T(8,128)(2,1)}, bf16[4,192,768]{2,1,0:T(8,128)(2,1)}, f32[16,768]{1,0:T(8,128)}) custom-call(bf16[3,3,192,1024]{3,2,1,0:T(8,128)(2,1)} %get-tuple-element.50.qkv_in, s32[3,1024]{1,0:T(4,128)} %seg_ref.3, bf16[3,4,192,256]{3,2,1,0:T(8,128)(2,1)} %get-tuple-element.51.o_in, ...), custom_call_target="tpu_custom_call" | custom-call | tf_op jit(solution)/shard_map/attention_backward/pallas_call | solution.py:1143
  206.8 6.9 %results.1 = (bf16[768,768]{1,0:T(8,128)(2,1)}, bf16[768,768]{1,0:T(8,128)(2,1)}, f32[192,768]{1,0:T(8,128)}, f32[192]{0:T(256)}, f32[192,768]{1,0:T(8,128)}, /*...) custom-call(bf16[768,768]{1,0:T(8,128)(2,1)} %get-tuple-element.49.o, ...), custom_call_target="tpu_custom_call" | custom-call | tf_op jit(solution)/shard_map/results/pallas_call | solution.py:1167
